TPU v7x, 256 devices: a whole 4x4x8 slice. The times are simulated.
256 devices in a mesh: lat: 8 (over x_hi, y), lon: 32 (over z, x_lo, core).
Axes of the slice: x: 4 (x_hi: 2, x_lo: 2; x = x_hi * 2 + x_lo), y: 4, z: 8, core: 2. Of those that a mesh axis runs over, the one named last changes fastest.
Arguments:
- state_field: bfloat16 [16, 2880, 512], P('lat', 'lon'), may hold values from -32 to 32
- cotangent: bfloat16 [16, 2880, 512], P('lat', 'lon'), may hold values from -6 to 6
- key_bias: bfloat16 [16, 2880, 16], P('lat', 'lon'), may hold values from -3 to 250
- input_gain: float32 [512], replicated, may hold values from 0.1 to 1.9
- expand_weight: bfloat16 [512, 2048], replicated, may hold values from -0.25 to 0.25
- depth_weight: bfloat16 [3, 3, 2048], replicated, may hold values from -2 to 2
- shrink_weight: bfloat16 [2048, 512], replicated, may hold values from -0.125 to 0.125
- attention_gain: float32 [512], replicated, may hold values from 0.1 to 1.9
- attention_in: bfloat16 [512, 1536], replicated, may hold values from -0.25 to 0.25
- attention_out: bfloat16 [512, 512], replicated, may hold values from -0.25 to 0.25
Outputs:
- output_field: bfloat16 [16, 2880, 512], P('lat', 'lon')
- input_grad: bfloat16 [16, 2880, 512], P('lat', 'lon')
- expand_grad: float32 [512, 2048], P('lat', 'lon')
- shrink_grad: float32 [2048, 512], P('lat', 'lon')
- attention_in_grad: float32 [512, 1536], P('lat', 'lon')
- attention_out_grad: float32 [512, 512], P('lat', 'lon')
- depth_grad: float32 [3, 3, 2048], replicated
- input_gain_grad: float32 [512], replicated
- attention_gain_grad: float32 [512], replicated
All inputs are finite; a program needn't handle non-finite values.
Results may differ from a plain program's by a relative error of at most 0.035.
Values may be sent and summed in bfloat16 or wider, within the bound.
A program may use at most 128 MiB of HBM per device.

v0:
```python
import math

import jax
import jax.numpy as jnp
from jax import lax
from jax.sharding import PartitionSpec as P

EPSILON = 1e-06


def with_halo(block, sides, width, periodic):
    for axis, dim in sides:
        count = lax.axis_size(axis)
        forward = [(i, i + 1) for i in range(count - 1)]
        if periodic:
            forward.append((count - 1, 0))
        backward = [(target, source) for source, target in forward]
        low = lax.ppermute(
            lax.slice_in_dim(block, block.shape[dim] - width, None, axis=dim), axis, forward
        )
        high = lax.ppermute(lax.slice_in_dim(block, 0, width, axis=dim), axis, backward)
        block = jnp.concatenate([low, block, high], axis=dim)
    return block


def inverse_rms(values):
    return lax.rsqrt(jnp.mean(values * values, axis=-1, keepdims=True) + EPSILON)


def silu_slope(values):
    sigmoid = jax.nn.sigmoid(values)
    return sigmoid * (1.0 + values * (1.0 - sigmoid))


def depthwise_sum(padded, weights, row_count, lon_count):
    total = jnp.zeros((row_count, lon_count, padded.shape[2]), jnp.float32)
    for lat_step in range(3):
        for lon_step in range(3):
            total = total + weights[lat_step, lon_step].astype(jnp.float32) * padded[
                lat_step : lat_step + row_count, lon_step : lon_step + lon_count
            ].astype(jnp.float32)
    return total


def transposed_sum(padded, weights, row_count, lon_count):
    total = jnp.zeros((row_count, lon_count, padded.shape[2]), jnp.float32)
    for lat_step in range(3):
        for lon_step in range(3):
            total = total + weights[lat_step, lon_step].astype(jnp.float32) * padded[
                2 - lat_step : 2 - lat_step + row_count, 2 - lon_step : 2 - lon_step + lon_count
            ].astype(jnp.float32)
    return total


def cross_cells(left, right):
    return lax.dot_general(
        left.reshape(-1, left.shape[-1]),
        right.reshape(-1, right.shape[-1]),
        (((0,), (0,)), ((), ())),
        preferred_element_type=jnp.float32,
    )


def times_transpose(values, weights):
    return lax.dot_general(
        values, weights, (((values.ndim - 1,), (1,)), ((), ())), preferred_element_type=jnp.float32
    )


def norm_back(back_normed, state, inverse, gain):
    scaled = back_normed * gain
    return inverse * scaled - inverse * inverse * inverse * state * jnp.mean(
        scaled * state, axis=-1, keepdims=True
    )


def to_items(values, head_count):
    row_count, lon_count, channels = values.shape
    head_width = channels // head_count
    return (
        values.reshape(row_count, lon_count, head_count, head_width)
        .transpose(0, 2, 1, 3)
        .reshape(row_count * head_count, lon_count, head_width)
    )


def from_items(values, row_count):
    item_count, lon_count, head_width = values.shape
    head_count = item_count // row_count
    return (
        values.reshape(row_count, head_count, lon_count, head_width)
        .transpose(0, 2, 1, 3)
        .reshape(row_count, lon_count, head_count * head_width)
    )


def per_device(
    state_field,
    cotangent,
    key_bias,
    input_gain,
    expand_weight,
    depth_weight,
    shrink_weight,
    attention_gain,
    attention_in,
    attention_out,
):
    row_count, lon_count, channels = state_field.shape
    head_count = key_bias.shape[2]
    head_width = channels // head_count
    query_parts = 4
    norm_factor = 1.0 / math.sqrt(
        row_count * lon_count * lax.axis_size("lat") * lax.axis_size("lon")
    )
    score_scale = 1.0 / math.sqrt(head_width)
    state_float = state_field.astype(jnp.float32)
    inverse_first = inverse_rms(state_float)
    normed = (state_float * inverse_first * input_gain).astype(jnp.bfloat16)
    expanded = jnp.dot(normed, expand_weight, preferred_element_type=jnp.float32)
    activated = jax.nn.silu(expanded).astype(jnp.bfloat16)
    padded = with_halo(activated, (("lon", 1),), 1, True)
    padded = with_halo(padded, (("lat", 0),), 1, False)
    convolved = depthwise_sum(padded, depth_weight, row_count, lon_count)
    mixed = jax.nn.silu(convolved).astype(jnp.bfloat16)
    inner_state = (
        state_float + jnp.dot(mixed, shrink_weight, preferred_element_type=jnp.float32)
    ).astype(jnp.bfloat16)
    inner_float = inner_state.astype(jnp.float32)
    inverse_second = inverse_rms(inner_float)
    normed_second = (inner_float * inverse_second * attention_gain).astype(jnp.bfloat16)
    projected = jnp.dot(normed_second, attention_in, preferred_element_type=jnp.float32).astype(
        jnp.bfloat16
    )
    queries = to_items(projected[..., :channels], head_count)
    keys_local = to_items(projected[..., channels : 2 * channels], head_count)
    values_local = to_items(projected[..., 2 * channels :], head_count)
    bias_items = key_bias.transpose(0, 2, 1).reshape(row_count * head_count, lon_count)
    query_rows, key_rows, value_rows, bias_rows = (
        lax.all_to_all(queries, "lon", split_axis=0, concat_axis=1, tiled=True),
        lax.all_to_all(keys_local, "lon", split_axis=0, concat_axis=1, tiled=True),
        lax.all_to_all(values_local, "lon", split_axis=0, concat_axis=1, tiled=True),
        lax.all_to_all(bias_items, "lon", split_axis=0, concat_axis=1, tiled=True),
    )

    def score_block(query_block, key_row, bias_row):
        return (
            jnp.einsum("qd,kd->qk", query_block, key_row, preferred_element_type=jnp.float32)
            * score_scale
            + bias_row.astype(jnp.float32)[None, :]
        )

    def attend(operands):
        query_row, key_row, value_row, bias_row = operands
        full_length = query_row.shape[0]
        query_blocks = query_row.reshape(query_parts, full_length // query_parts, head_width)

        def one_block(query_block):
            scores = score_block(query_block, key_row, bias_row)
            highest = jnp.max(scores, axis=1, keepdims=True)
            exponent = jnp.exp(scores - highest)
            total = jnp.sum(exponent, axis=1, keepdims=True)
            attention_weights = (exponent / total).astype(jnp.bfloat16)
            block_rows = jnp.dot(
                attention_weights, value_row, preferred_element_type=jnp.float32
            ).astype(jnp.bfloat16)
            return (block_rows, highest + jnp.log(total))

        block_rows, block_levels = lax.map(one_block, query_blocks)
        return (block_rows.reshape(full_length, head_width), block_levels.reshape(full_length, 1))

    head_rows, levels = lax.map(attend, (query_rows, key_rows, value_rows, bias_rows))
    head_local = lax.all_to_all(head_rows, "lon", split_axis=1, concat_axis=0, tiled=True)
    heads_field = from_items(head_local, row_count)
    output_field = (
        inner_float + jnp.dot(heads_field, attention_out, preferred_element_type=jnp.float32)
    ).astype(jnp.bfloat16)
    out_grad_local = cross_cells(heads_field, cotangent) * norm_factor
    back_heads = times_transpose(cotangent, attention_out).astype(jnp.bfloat16)
    back_rows = lax.all_to_all(
        to_items(back_heads, head_count), "lon", split_axis=0, concat_axis=1, tiled=True
    )

    def attend_back(operands):
        query_row, key_row, value_row, bias_row, level_row, back_row = operands
        full_length = query_row.shape[0]
        block_length = full_length // query_parts
        query_blocks = query_row.reshape(query_parts, block_length, head_width)
        level_blocks = level_row.reshape(query_parts, block_length, 1)
        back_blocks = back_row.reshape(query_parts, block_length, head_width)

        def one_block(carry, block):
            key_total, value_total = carry
            query_block, level_block, back_block = block
            scores = score_block(query_block, key_row, bias_row)
            probs_float = jnp.exp(scores - level_block)
            probs_low = probs_float.astype(jnp.bfloat16)
            value_total = value_total + lax.dot_general(
                probs_low, back_block, (((0,), (0,)), ((), ())), preferred_element_type=jnp.float32
            )
            back_probs = jnp.einsum(
                "qd,kd->qk", back_block, value_row, preferred_element_type=jnp.float32
            )
            centred = jnp.sum(probs_float * back_probs, axis=1, keepdims=True)
            back_scores = (probs_float * (back_probs - centred)).astype(jnp.bfloat16)
            query_block_grads = (
                jnp.dot(back_scores, key_row, preferred_element_type=jnp.float32) * score_scale
            ).astype(jnp.bfloat16)
            key_total = key_total + lax.dot_general(
                back_scores,
                query_block,
                (((0,), (0,)), ((), ())),
                preferred_element_type=jnp.float32,
            )
            return ((key_total, value_total), query_block_grads)

        start_totals = (
            jnp.zeros((full_length, head_width), jnp.float32),
            jnp.zeros((full_length, head_width), jnp.float32),
        )
        final_totals, query_grad_blocks = lax.scan(
            one_block, start_totals, (query_blocks, level_blocks, back_blocks)
        )
        key_grads = (final_totals[0] * score_scale).astype(jnp.bfloat16)
        value_grads = final_totals[1].astype(jnp.bfloat16)
        return (query_grad_blocks.reshape(full_length, head_width), key_grads, value_grads)

    query_grads, key_grads, value_grads = lax.map(
        attend_back, (query_rows, key_rows, value_rows, bias_rows, levels, back_rows)
    )
    query_grads, key_grads, value_grads = (
        lax.all_to_all(query_grads, "lon", split_axis=1, concat_axis=0, tiled=True),
        lax.all_to_all(key_grads, "lon", split_axis=1, concat_axis=0, tiled=True),
        lax.all_to_all(value_grads, "lon", split_axis=1, concat_axis=0, tiled=True),
    )
    back_projected = jnp.concatenate(
        [
            from_items(query_grads, row_count),
            from_items(key_grads, row_count),
            from_items(value_grads, row_count),
        ],
        axis=-1,
    )
    in_grad_local = cross_cells(normed_second, back_projected) * norm_factor
    back_second = times_transpose(back_projected, attention_in)
    gain_two = jnp.sum(back_second * inner_float * inverse_second, axis=(0, 1)) * norm_factor
    back_inner = (
        cotangent.astype(jnp.float32)
        + norm_back(back_second, inner_float, inverse_second, attention_gain)
    ).astype(jnp.bfloat16)
    attention_part = (in_grad_local, out_grad_local)
    shrink_local = cross_cells(mixed, back_inner) * norm_factor
    back_convolved = (times_transpose(back_inner, shrink_weight) * silu_slope(convolved)).astype(
        jnp.bfloat16
    )
    back_pad = with_halo(back_convolved, (("lon", 1),), 1, True)
    back_pad = with_halo(back_pad, (("lat", 0),), 1, False)
    back_activated = transposed_sum(back_pad, depth_weight, row_count, lon_count)
    back_conv_float = back_convolved.astype(jnp.float32)
    depth_local = (
        jnp.stack(
            [
                jnp.stack(
                    [
                        jnp.sum(
                            padded[
                                lat_step : lat_step + row_count, lon_step : lon_step + lon_count
                            ].astype(jnp.float32)
                            * back_conv_float,
                            axis=(0, 1),
                        )
                        for lon_step in range(3)
                    ]
                )
                for lat_step in range(3)
            ]
        )
        * norm_factor
    )
    back_expanded = (back_activated * silu_slope(expanded)).astype(jnp.bfloat16)
    expand_local = cross_cells(normed, back_expanded) * norm_factor
    back_normed = times_transpose(back_expanded, expand_weight)
    gain_one = jnp.sum(back_normed * state_float * inverse_first, axis=(0, 1)) * norm_factor
    input_grad = (
        back_inner.astype(jnp.float32)
        + norm_back(back_normed, state_float, inverse_first, input_gain)
    ).astype(jnp.bfloat16)
    depth_grad, input_gain_grad, attention_gain_grad = lax.psum(
        (depth_local, gain_one, gain_two), ("lat", "lon")
    )
    results = (
        lax.psum_scatter(
            expand_local.astype(jnp.bfloat16), "lon", scatter_dimension=1, tiled=True
        ).astype(jnp.float32),
        lax.psum_scatter(
            shrink_local.astype(jnp.bfloat16), "lon", scatter_dimension=1, tiled=True
        ).astype(jnp.float32),
        lax.psum_scatter(
            attention_part[0].astype(jnp.bfloat16), "lon", scatter_dimension=1, tiled=True
        ).astype(jnp.float32),
        lax.psum_scatter(
            attention_part[1].astype(jnp.bfloat16), "lon", scatter_dimension=1, tiled=True
        ).astype(jnp.float32),
    )
    results = (
        lax.psum_scatter(
            results[0].astype(jnp.bfloat16), "lat", scatter_dimension=0, tiled=True
        ).astype(jnp.float32),
        lax.psum_scatter(
            results[1].astype(jnp.bfloat16), "lat", scatter_dimension=0, tiled=True
        ).astype(jnp.float32),
        lax.psum_scatter(
            results[2].astype(jnp.bfloat16), "lat", scatter_dimension=0, tiled=True
        ).astype(jnp.float32),
        lax.psum_scatter(
            results[3].astype(jnp.bfloat16), "lat", scatter_dimension=0, tiled=True
        ).astype(jnp.float32),
    )
    return (
        output_field,
        input_grad,
        results[0],
        results[1],
        results[2],
        results[3],
        depth_grad,
        input_gain_grad,
        attention_gain_grad,
    )


def solution(mesh):
    placed = (
        P("lat", "lon", None),
        P("lat", "lon", None),
        P("lat", "lon", None),
        P(),
        P(),
        P(),
        P(),
        P(),
        P(),
        P(),
    )
    return jax.shard_map(
        per_device,
        mesh=mesh,
        in_specs=placed,
        out_specs=(
            P("lat", "lon", None),
            P("lat", "lon", None),
            P("lat", "lon"),
            P("lat", "lon"),
            P("lat", "lon"),
            P("lat", "lon"),
            P(),
            P(),
            P(),
        ),
        check_vma=False,
    )
```

profile of v0, /device:TPU:1, one launch (start us, length us, event | category | flops | bytes accessed | tf_op | source)
XLA Modules:
  0.0 1127.3 jit_solution(6588735431925445145)
XLA Ops:
  16.7 10.6 all-to-all-start.2
  51.4 9.3 all-to-all-start.5
  77.6 10.6 all-to-all-done
  93.8 10.6 all-to-all-done.1
  125.7 26.1 %while.47 = (s32[]{:T(128)}, bf16[4,720,32]{1,2,0:T(8,128)(2,1)S(1)}, f32[4,720,1]{1,2,0:T(1,128)S(1)}, bf16[4,720,32]{2,1,0:T(8,128)(2,1)}, bf16[2880,32]{1,0:T...) while((s32[]{:T(128)}, bf16[4,720,32]{1,2,0:T(8,128)(2,1)S(1)}, ...), condition=%wide.region_5.6_spmd, body=%wide.region_2.5_spmd.sunk | while | flops 290329216 | bytes 27045752 | solution.py:169
  157.2 17.9 %reduce.3 = bf16[2880,32]{1,0:T(8,128)(2,1)} reduce(bf16[2880,1,32]{2,1,0:T(2,128)(2,1)} %bitcast.209, bf16[]{:T(256)} %broadcast.144), dimensions={1}, to_apply=%bitcast.151.reduce_sub_computation | reduce | bytes 368642
  184.2 112.0 %while.48 = (s32[]{:T(128)}, f32[2880,32]{0,1:T(8,128)}, f32[2880,32]{0,1:T(8,128)S(1)}, bf16[4,720,32]{1,2,0:T(8,128)(2,1)}, bf16[4,720,32]{2,1,0:T(8,128)(2,1)...) while((s32[]{:T(128)}, f32[2880,32]{0,1:T(8,128)}, ...), condition=%wide.region_8.9_spmd.clone, body=%wide.region_6.8_spmd.clone.sunk | while | flops 682631296 | bytes 131522432 | solution.py:221
  194.3 9.0 multiply_convert_fusion.10
  222.2 9.0 multiply_convert_fusion.10
  250.2 9.0 multiply_convert_fusion.10
  278.2 9.0 multiply_convert_fusion.10
  300.3 17.1 %reduce.6 = bf16[2880,32]{1,0:T(8,128)(2,1)S(1)} reduce(bf16[2880,1,32]{2,1,0:T(2,128)(2,1)} %bitcast.211, bf16[]{:T(256)} %broadcast.144), dimensions={1}, to_apply=%bitcast.149.reduce_sub_computation | reduce | bytes 368642
  318.7 8.4 all-to-all-start.6
  343.8 17.0 %reduce.5 = bf16[2880,32]{1,0:T(8,128)(2,1)S(1)} reduce(bf16[2880,1,32]{2,1,0:T(2,128)(2,1)} %bitcast.213, bf16[]{:T(256)} %broadcast.144), dimensions={1}, to_apply=%bitcast.147.reduce_sub_computation | reduce | bytes 368642
  362.1 8.6 all-to-all-start.7
  373.6 17.0 %reduce.4 = bf16[2880,32]{1,0:T(8,128)(2,1)S(1)} reduce(bf16[2880,1,32]{2,1,0:T(2,128)(2,1)} %bitcast.210, bf16[]{:T(256)} %broadcast.144), dimensions={1}, to_apply=%bitcast.145.reduce_sub_computation | reduce | bytes 368642
  391.9 8.3 all-to-all-start.8
  471.7 103.0 %reduce-scatter.21.cloned.1.call-done = bf16[512,48]{0,1:T(8,128)(2,1)} async-done(((bf16[512,1536]{0,1:T(8,128)(2,1)}), bf16[512,48]{0,1:T(8,128)(2,1)}) %reduce-scatter.21.cloned.1.call-update) | async-done | bytes 49168 | tf_op jit(solution)/shard_map/reduce_scatter | solution.py:298
  578.0 116.3 %reduce-scatter.17.cloned.1.call-done = bf16[2048,16]{0,1:T(8,128)(2,1)} async-done(((bf16[2048,512]{0,1:T(8,128)(2,1)}), bf16[2048,16]{0,1:T(8,128)(2,1)}) %reduce-scatter.17.cloned.1.call-update) | async-done | bytes 65552 | tf_op jit(solution)/shard_map/reduce_scatter | solution.py:295
  695.0 118.5 %reduce-scatter.15.cloned.1.call-done = bf16[512,64]{0,1:T(8,128)(2,1)} async-done(((bf16[512,2048]{0,1:T(8,128)(2,1)}), bf16[512,64]{0,1:T(8,128)(2,1)}) %reduce-scatter.15.cloned.1.call-update) | async-done | bytes 65552 | tf_op jit(solution)/shard_map/reduce_scatter | solution.py:292
  817.9 80.0 %all-reduce = (f32[512]{0:T(512)}, f32[512]{0:T(512)}) all-reduce(f32[512]{0:T(512)S(1)} %broadcast_multiply_fusion.1, f32[512]{0:T(512)S(1)} %broadcast_multiply_fusion), channel_id=1, replica_groups=mesh['lat'=8,'lon'=32] {'lat','lon'}, use_global_device_ids=true, to_apply=%region_30.31 | all-reduce | flops 1024 | bytes 8192 | tf_op jit(solution)/shard_map/psum | solution.py:288
  899.3 69.6 %reduce-scatter.27.cloned.1.call-done = bf16[64,48]{1,0:T(8,128)(2,1)} async-done(((bf16[512,48]{1,0:T(8,128)(2,1)}), bf16[64,48]{1,0:T(8,128)(2,1)}) %reduce-scatter.27.cloned.1.call-update) | async-done | bytes 6160
  970.3 68.6 %reduce-scatter.19.cloned.1.call-done = bf16[256,16]{0,1:T(8,128)(2,1)} async-done(((bf16[2048,16]{0,1:T(8,128)(2,1)}), bf16[256,16]{0,1:T(8,128)(2,1)}) %reduce-scatter.19.cloned.1.call-update) | async-done | bytes 8208 | tf_op jit(solution)/shard_map/reduce_scatter | solution.py:309
  1040.1 76.2 %reduce-scatter.25.cloned.1.call-done = bf16[64,64]{1,0:T(8,128)(2,1)} async-done(((bf16[512,64]{1,0:T(8,128)(2,1)}), bf16[64,64]{1,0:T(8,128)(2,1)}) %reduce-scatter.25.cloned.1.call-update) | async-done | bytes 8208
  (372 shorter events, 306.1 us)
Async XLA Ops:
  12.7 18.4 %collective-permute-start = (bf16[2,1,2048]{2,1,0:T(2,128)(2,1)S(1)}, bf16[2,1,2048]{2,1,0:T(2,128)(2,1)S(1)}, u32[]{:S(2)}, u32[]{:S(2)}) collective-permute-start(bf16[2,1,2048]{2,1,0:T(2,128)(2,1)S(1)} %get-tuple-element.346), channel_id=1, source_target_pairs={{0,1},{1,2},{2,3},{3,4},{4,5},{5,6},{6,7},{7,8},{8,9},{9,10},{10,1... | collective-permute-start | bytes 24584 | tf_op jit(solution)/shard_map/ppermute | solution.py:18
  15.4 15.7 %collective-permute-start.1 = (bf16[2,1,2048]{2,1,0:T(2,128)(2,1)S(1)}, bf16[2,1,2048]{2,1,0:T(2,128)(2,1)S(1)}, u32[]{:S(2)}, u32[]{:S(2)}) collective-permute-start(bf16[2,1,2048]{2,1,0:T(2,128)(2,1)S(1)} %get-tuple-element.347), channel_id=1, source_target_pairs={{1,0},{2,1},{3,2},{4,3},{5,4},{6,5},{7,6},{8,7},{9,8},{10,9},{11,1... | collective-permute-start | bytes 24584 | tf_op jit(solution)/shard_map/ppermute | solution.py:21
  16.7 34.7 %all-to-all-start.2 = ((bf16[32,1,90]{2,1,0:T(2,128)(2,1)}), bf16[32,1,90]{2,1,0:T(2,128)(2,1)S(1)}, u32[]{:S(2)}, u32[]{:S(2)}) async-start(bf16[32,1,90]{2,1,0:T(2,128)(2,1)} %copy.104), calls=%async_computation.2 | async-start | bytes 32768 | tf_op jit(solution)/shard_map/all_to_all | solution.py:143
  31.4 11.5 %collective-permute-start.2 = (bf16[1,92,2048]{2,1,0:T(8,128)(2,1)S(1)}, bf16[1,92,2048]{2,1,0:T(8,128)(2,1)S(1)}, u32[]{:S(2)}, u32[]{:S(2)}) collective-permute-start(bf16[1,92,2048]{2,1,0:T(8,128)(2,1)S(1)} %get-tuple-element.344), channel_id=1, source_target_pairs={{0,32},{32,64},{64,96},{96,128},{128,160},{160,192},{192,224},{1,3... | collective-permute-start | bytes 1130504 | tf_op jit(solution)/shard_map/ppermute | solution.py:18
  34.7 12.1 %collective-permute-start.3 = (bf16[1,92,2048]{2,1,0:T(8,128)(2,1)S(1)}, bf16[1,92,2048]{2,1,0:T(8,128)(2,1)S(1)}, u32[]{:S(2)}, u32[]{:S(2)}) collective-permute-start(bf16[1,92,2048]{2,1,0:T(8,128)(2,1)S(1)} %get-tuple-element.345), channel_id=1, source_target_pairs={{32,0},{64,32},{96,64},{128,96},{160,128},{192,160},{224,192},{33,... | collective-permute-start | bytes 1130504 | tf_op jit(solution)/shard_map/ppermute | solution.py:21
  51.4 20.7 %all-to-all-start.5 = ((bf16[32,90,32]{1,2,0:T(8,128)(2,1)}), bf16[32,90,32]{1,2,0:T(8,128)(2,1)S(1)}, u32[]{:S(2)}, u32[]{:S(2)}) async-start(bf16[32,90,32]{1,2,0:T(8,128)(2,1)} %bitcast.30), calls=%async_computation.5 | async-start | bytes 524288 | tf_op jit(solution)/shard_map/all_to_all | solution.py:180
  72.2 16.0 %all-to-all-start = ((bf16[32,90,32]{1,2,0:T(8,128)(2,1)}), bf16[32,90,32]{1,2,0:T(8,128)(2,1)S(1)}, u32[]{:S(2)}, u32[]{:S(2)}) async-start(bf16[32,90,32]{1,2,0:T(8,128)(2,1)} %bitcast.16), calls=%async_computation | async-start | bytes 524288 | tf_op jit(solution)/shard_map/all_to_all | solution.py:140
  88.2 16.2 %all-to-all-start.1 = ((bf16[32,90,32]{1,2,0:T(8,128)(2,1)}), bf16[32,90,32]{1,2,0:T(8,128)(2,1)S(1)}, u32[]{:S(2)}, u32[]{:S(2)}) async-start(bf16[32,90,32]{1,2,0:T(8,128)(2,1)} %bitcast.19), calls=%async_computation.1 | async-start | bytes 524288 | tf_op jit(solution)/shard_map/all_to_all | solution.py:141
  104.4 17.2 %all-to-all-start.3 = ((bf16[32,90,32]{1,2,0:T(8,128)(2,1)}), bf16[32,90,32]{1,2,0:T(8,128)(2,1)}, u32[]{:S(2)}, u32[]{:S(2)}) async-start(bf16[32,90,32]{1,2,0:T(8,128)(2,1)} %bitcast.24), calls=%async_computation.3 | async-start | bytes 524288 | tf_op jit(solution)/shard_map/all_to_all | solution.py:142
  177.5 141.2 %all-to-all-start.4 = ((bf16[32,2,1440]{2,1,0:T(2,128)(2,1)}), bf16[32,2,1440]{2,1,0:T(2,128)(2,1)}, u32[]{:S(2)}, u32[]{:S(2)}) async-start(bf16[32,2,1440]{2,1,0:T(2,128)(2,1)} %reshape.258), calls=%async_computation.4 | async-start | bytes 393216 | tf_op jit(solution)/shard_map/all_to_all | solution.py:173
  318.7 43.4 %all-to-all-start.6 = ((bf16[32,2,1440]{2,1,0:T(2,128)(2,1)}), bf16[32,2,1440]{2,1,0:T(2,128)(2,1)}, u32[]{:S(2)}, u32[]{:S(2)}) async-start(bf16[32,2,1440]{2,1,0:T(2,128)(2,1)} %reshape.256), calls=%async_computation.6 | async-start | bytes 393216 | tf_op jit(solution)/shard_map/all_to_all | solution.py:232
  327.2 142.2 %reduce-scatter.23.cloned.1.call-start = ((), (), s32[]{:S(2)}) async-start(), calls=%async_computation.21 | async-start | bytes 540672 | tf_op jit(solution)/shard_map/reduce_scatter | solution.py:301
  362.1 29.8 %all-to-all-start.7 = ((bf16[32,2,1440]{2,1,0:T(2,128)(2,1)}), bf16[32,2,1440]{2,1,0:T(2,128)(2,1)S(1)}, u32[]{:S(2)}, u32[]{:S(2)}) async-start(bf16[32,2,1440]{2,1,0:T(2,128)(2,1)} %reshape.254), calls=%async_computation.7 | async-start | bytes 393216 | tf_op jit(solution)/shard_map/all_to_all | solution.py:233
  391.9 25.0 %all-to-all-start.8 = ((bf16[32,2,1440]{2,1,0:T(2,128)(2,1)}), bf16[32,2,1440]{2,1,0:T(2,128)(2,1)S(1)}, u32[]{:S(2)}, u32[]{:S(2)}) async-start(bf16[32,2,1440]{2,1,0:T(2,128)(2,1)} %reshape.252), calls=%async_computation.8 | async-start | bytes 393216 | tf_op jit(solution)/shard_map/all_to_all | solution.py:234
  400.1 174.6 %reduce-scatter.21.cloned.1.call-start = ((), (), s32[]{:S(2)}) async-start(), calls=%async_computation.20 | async-start | bytes 1622016 | tf_op jit(solution)/shard_map/reduce_scatter | solution.py:298
  427.2 267.1 %reduce-scatter.17.cloned.1.call-start = ((), (), s32[]{:S(2)}) async-start(), calls=%async_computation.18 | async-start | bytes 2162688 | tf_op jit(solution)/shard_map/reduce_scatter | solution.py:295
  434.2 379.3 %reduce-scatter.15.cloned.1.call-start = ((), (), s32[]{:S(2)}) async-start(), calls=%async_computation.17 | async-start | bytes 2162688 | tf_op jit(solution)/shard_map/reduce_scatter | solution.py:292
  448.7 12.1 %collective-permute-start.6 = (bf16[1,92,2048]{2,1,0:T(8,128)(2,1)S(1)}, bf16[1,92,2048]{2,1,0:T(8,128)(2,1)S(1)}, u32[]{:S(2)}, u32[]{:S(2)}) collective-permute-start(bf16[1,92,2048]{2,1,0:T(8,128)(2,1)S(1)} %get-tuple-element.340), channel_id=1, source_target_pairs={{32,0},{64,32},{96,64},{128,96},{160,128},{192,160},{224,192},{33,... | collective-permute-start | bytes 1130504 | tf_op jit(solution)/shard_map/ppermute | solution.py:21
  450.1 11.8 %collective-permute-start.7 = (bf16[1,92,2048]{2,1,0:T(8,128)(2,1)S(1)}, bf16[1,92,2048]{2,1,0:T(8,128)(2,1)S(1)}, u32[]{:S(2)}, u32[]{:S(2)}) collective-permute-start(bf16[1,92,2048]{2,1,0:T(8,128)(2,1)S(1)} %get-tuple-element.341), channel_id=1, source_target_pairs={{0,32},{32,64},{64,96},{96,128},{128,160},{160,192},{192,224},{1,3... | collective-permute-start | bytes 1130504 | tf_op jit(solution)/shard_map/ppermute | solution.py:18
  467.9 430.0 %reduce-scatter.29.cloned.1.call-start = ((), (), s32[]{:S(2)}) async-start(), calls=%async_computation.25 | async-start | bytes 147456
  470.9 497.9 %reduce-scatter.27.cloned.1.call-start = ((), (), s32[]{:S(2)}) async-start(), calls=%async_computation.24 | async-start | bytes 147456
  576.4 462.5 %reduce-scatter.19.cloned.1.call-start = ((), (), s32[]{:S(2)}) async-start(), calls=%async_computation.19 | async-start | bytes 73728 | tf_op jit(solution)/shard_map/reduce_scatter | solution.py:309
  694.3 422.0 %reduce-scatter.25.cloned.1.call-start = ((), (), s32[]{:S(2)}) async-start(), calls=%async_computation.23 | async-start | bytes 147456
  815.1 302.7 %all-reduce.3.cloned.1.call-start = ((), (), s32[]{:S(2)}) async-start(), calls=%async_computation.22 | async-start | bytes 196608 | tf_op jit(solution)/shard_map/psum | solution.py:288
  (79 other events, 2531.6 us)
Sparse Core Ops, SparseCore 0:
  339.6 116.7 reduce-scatter.22
  459.0 115.7 reduce-scatter.20
  577.3 116.9 reduce-scatter.16
  696.8 116.6 reduce-scatter.14
  817.2 74.3 reduce-scatter.28
  895.2 73.6 reduce-scatter.26
  972.5 66.3 reduce-scatter.18
  1042.6 73.6 reduce-scatter.24
Sparse Core Ops, SparseCore 1:
  821.7 242.7 all-reduce.2
where the time goes:
time: 1140 us; the launch traced here: 1130 us
  waiting for transfers between devices  609 us (53%)
  other arithmetic  127 us (11%)
  matrix products  118 us (10%)
  local copies, waits for them, and re-layouts  93.8 us (8%)
  starting transfers between devices  82 us (7%)
  blocking collectives  80 us (7%)
  between operations  17.2 us (2%)
    unnamed x12, waiting for transfers between devices  146 us
    reduce_scatter x1, waiting for transfers between devices, per_device(): lax.psum_scatter(expand_local.astype(jnp.bfloat16), 'lon', scatter_dimens...  118 us
    reduce_scatter x1, waiting for transfers between devices, per_device(): lax.psum_scatter(shrink_local.astype(jnp.bfloat16), 'lon', scatter_dimens...  116 us
    reduce_scatter x1, waiting for transfers between devices, per_device(): lax.psum_scatter(attention_part[0].astype(jnp.bfloat16), 'lon', scatter_d...  103 us
    psum x1, blocking collectives, per_device(): lax.psum((depth_local, gain_one, gain_two), ('lat', 'lon'))  80 us
    unnamed x6, other arithmetic  69 us
    reduce_scatter x1, waiting for transfers between devices, per_device(): lax.psum_scatter(results[1].astype(jnp.bfloat16), 'lat', scatter_dimensio...  68.6 us
    unnamed x150, local copies, waits for them, and re-layouts  37.4 us
  transfers between devices with their start and end apart: 26, of which 16 were waited for; matrix products, arithmetic and copies ran while one was open for 24% of the time, Pallas kernels for 0%

commit v1 on v0

v1 whole, which is shorter than its diff:
```python
import functools
import math

import jax
import jax.numpy as jnp
from jax import lax
from jax.experimental import pallas as pl
from jax.experimental.pallas import tpu as pltpu
from jax.sharding import PartitionSpec as P

EPSILON = 1e-06


def with_halo(block, sides, width, periodic):
    for axis, dim in sides:
        count = lax.axis_size(axis)
        forward = [(i, i + 1) for i in range(count - 1)]
        if periodic:
            forward.append((count - 1, 0))
        backward = [(target, source) for source, target in forward]
        low = lax.ppermute(
            lax.slice_in_dim(block, block.shape[dim] - width, None, axis=dim), axis, forward
        )
        high = lax.ppermute(lax.slice_in_dim(block, 0, width, axis=dim), axis, backward)
        block = jnp.concatenate([low, block, high], axis=dim)
    return block


def inverse_rms(values):
    return lax.rsqrt(jnp.mean(values * values, axis=-1, keepdims=True) + EPSILON)


def silu_slope(values):
    sigmoid = jax.nn.sigmoid(values)
    return sigmoid * (1.0 + values * (1.0 - sigmoid))


def depthwise_sum(padded, weights, row_count, lon_count):
    total = jnp.zeros((row_count, lon_count, padded.shape[2]), jnp.float32)
    for lat_step in range(3):
        for lon_step in range(3):
            total = total + weights[lat_step, lon_step].astype(jnp.float32) * padded[
                lat_step : lat_step + row_count, lon_step : lon_step + lon_count
            ].astype(jnp.float32)
    return total


def transposed_sum(padded, weights, row_count, lon_count):
    total = jnp.zeros((row_count, lon_count, padded.shape[2]), jnp.float32)
    for lat_step in range(3):
        for lon_step in range(3):
            total = total + weights[lat_step, lon_step].astype(jnp.float32) * padded[
                2 - lat_step : 2 - lat_step + row_count, 2 - lon_step : 2 - lon_step + lon_count
            ].astype(jnp.float32)
    return total


def times_transpose(values, weights):
    return lax.dot_general(
        values, weights, (((values.ndim - 1,), (1,)), ((), ())), preferred_element_type=jnp.float32
    )


def norm_back(back_normed, state, inverse, gain):
    scaled = back_normed * gain
    return inverse * scaled - inverse * inverse * inverse * state * jnp.mean(
        scaled * state, axis=-1, keepdims=True
    )


CELLS = 96


def attend_kernel(valid, scale, x_ref, out_ref, xt_ref, kaug_ref, vaug_ref, t_ref, pb_ref, acc_ref, qo_ref):
    sources = x_ref.shape[0]
    total = sources * CELLS
    block = 256
    step = 512 if total % 512 == 0 else 256
    log2e = 1.4426950408889634
    to_log2 = scale * log2e
    f32, bf16 = jnp.float32, jnp.bfloat16

    def prepare(index, carry):
        raw = x_ref[index].astype(f32)
        row = lax.broadcasted_iota(jnp.int32, (CELLS, 128), 0)
        lane = lax.broadcasted_iota(jnp.int32, (CELLS, 128), 1)
        bias_row = jnp.broadcast_to(raw[valid : valid + 1, :], (CELLS, 128))
        bias = jnp.sum(jnp.where(row == lane, bias_row, 0.0), axis=1, keepdims=True) * log2e
        bias = jnp.broadcast_to(bias, (CELLS, 128))
        first = bias.astype(bf16).astype(f32)
        second = (bias - first).astype(bf16).astype(f32)
        third = bias - first - second
        first = jnp.where(row < valid, first, -1e30)
        second = jnp.where(row < valid, second, 0.0)
        third = jnp.where(row < valid, third, 0.0)
        cell = jnp.where(row < valid, raw, 0.0)
        key = jnp.where((lane >= 32) & (lane < 64), cell, 0.0)
        value = jnp.where((lane >= 64) & (lane < 96), cell, 0.0)
        keys = pltpu.roll(key, 96, 1) + key + pltpu.roll(key, 32, 1)
        keys = jnp.where(lane == 96, first, keys)
        keys = jnp.where(lane == 97, second, keys)
        keys = jnp.where(lane == 98, third, keys)
        values = pltpu.roll(value, 64, 1) + pltpu.roll(value, 96, 1)
        values = jnp.where((lane >= 64) & (lane < 67), 1.0, values)
        start = pl.multiple_of(index * CELLS, 32)
        kaug_ref[pl.ds(start, CELLS), :] = keys.astype(bf16)
        vaug_ref[pl.ds(start, CELLS), :] = values.astype(bf16)
        qo_ref[pl.ds(start, CELLS), :] = cell
        return carry

    lax.fori_loop(0, sources, prepare, 0)

    def turn(index, carry):
        start = pl.multiple_of(index * block, block)
        xt_ref[:, pl.ds(start, block)] = qo_ref[pl.ds(start, block), :].T.astype(bf16)
        acc_ref[pl.ds(start, block), :] = jnp.zeros((block, 128), f32)
        return carry

    lax.fori_loop(0, total // block, turn, 0)

    def one_block(index, carry):
        start = pl.multiple_of(index * block, block)
        xq = qo_ref[pl.ds(start, block), :]
        xt = xt_ref[:, pl.ds(start, block)].astype(f32)
        query = xt[0:32] * to_log2
        first = query.astype(bf16).astype(f32)
        second = (query - first).astype(bf16).astype(f32)
        third = query - first - second
        qaug = jnp.concatenate([first, second, third, jnp.ones((32, block), f32)], axis=0).astype(bf16)

        def scores(part, highest):
            begin = pl.multiple_of(part * step, step)
            t = jnp.dot(kaug_ref[pl.ds(begin, step), :], qaug, preferred_element_type=f32)
            t_ref[pl.ds(begin, step), :] = t
            return jnp.maximum(highest, jnp.max(t.reshape(step // 8, 8, block), axis=0))

        highest = lax.fori_loop(0, total // step, scores, jnp.full((8, block), -jnp.inf, f32))
        highest = jnp.max(highest, axis=0, keepdims=True)

        def weigh(part, carry):
            norm, heads = carry
            begin = pl.multiple_of(part * step, step)
            p = jnp.exp2(t_ref[pl.ds(begin, step), :] - highest)
            t_ref[pl.ds(begin, step), :] = p
            low = p.astype(bf16)
            pb_ref[pl.ds(begin, step), :] = low
            norm = norm + jnp.sum(p.reshape(step // 8, 8, block), axis=0)
            heads = heads + jnp.dot(
                xt_ref[64:96, pl.ds(begin, step)], low, preferred_element_type=f32
            )
            return norm, heads

        norm, heads = lax.fori_loop(
            0, total // step, weigh, (jnp.zeros((8, block), f32), jnp.zeros((32, block), f32))
        )
        inverse = 1.0 / jnp.sum(norm, axis=0, keepdims=True)
        heads = heads * inverse
        back = xt[96:128]
        centred = jnp.sum(back * heads, axis=0, keepdims=True) * inverse
        back = back * inverse
        back_first = back.astype(bf16).astype(f32)
        back_second = back - back_first
        cen_first = centred.astype(bf16).astype(f32)
        cen_second = (centred - cen_first).astype(bf16).astype(f32)
        cen_third = centred - cen_first - cen_second
        sub = lax.broadcasted_iota(jnp.int32, (64, block), 0)
        cen = jnp.where(sub == 0, cen_first, jnp.where(sub == 1, cen_second, jnp.where(sub == 2, cen_third, 0.0)))
        baug = jnp.concatenate([back_first, back_second, -cen], axis=0).astype(bf16)
        zeros = jnp.zeros((32, block), f32)
        back_cells = jnp.concatenate([zeros, zeros, back_first, zeros], axis=0).T.astype(bf16)
        lane = lax.broadcasted_iota(jnp.int32, (block, 128), 1)
        query_cells = pltpu.roll(jnp.where(lane < 32, xq, 0.0), 32, 1).astype(bf16)

        def grads(part, back_queries):
            begin = pl.multiple_of(part * step, step)
            dp = jnp.dot(vaug_ref[pl.ds(begin, step), :], baug, preferred_element_type=f32)
            ds = (t_ref[pl.ds(begin, step), :] * dp).astype(bf16)
            acc_ref[pl.ds(begin, step), :] += jnp.dot(
                pb_ref[pl.ds(begin, step), :], back_cells, preferred_element_type=f32
            ) + jnp.dot(ds, query_cells, preferred_element_type=f32)
            return back_queries + jnp.dot(
                xt_ref[32:64, pl.ds(begin, step)], ds, preferred_element_type=f32
            )

        back_queries = lax.fori_loop(0, total // step, grads, zeros)
        turned = jnp.concatenate([back_queries * scale, zeros, zeros, heads], axis=0).T
        out_ref[pl.ds(start, block), :] = turned.astype(bf16)
        return carry

    lax.fori_loop(0, total // block, one_block, 0)

    def finish(index, carry):
        start = pl.multiple_of(index * block, block)
        lane = lax.broadcasted_iota(jnp.int32, (block, 128), 1)
        both = acc_ref[pl.ds(start, block), :]
        both = jnp.where(lane < 64, both * scale, both)
        both = jnp.where((lane >= 32) & (lane < 96), both, out_ref[pl.ds(start, block), :].astype(f32))
        out_ref[pl.ds(start, block), :] = both.astype(bf16)
        return carry

    lax.fori_loop(0, total // block, finish, 0)


def attend_items(items, valid, scale):
    sources = items.shape[0]
    total = sources * CELLS
    f32, bf16 = jnp.float32, jnp.bfloat16
    out = pl.pallas_call(
        functools.partial(attend_kernel, valid, scale),
        out_shape=jax.ShapeDtypeStruct((total, 128), bf16),
        in_specs=[pl.BlockSpec(memory_space=pltpu.VMEM)],
        out_specs=pl.BlockSpec(memory_space=pltpu.VMEM),
        scratch_shapes=[
            pltpu.VMEM((128, total), bf16),
            pltpu.VMEM((total, 128), bf16),
            pltpu.VMEM((total, 128), bf16),
            pltpu.VMEM((total, 256), f32),
            pltpu.VMEM((total, 256), bf16),
            pltpu.VMEM((total, 128), f32),
            pltpu.VMEM((total, 128), f32),
        ],
        compiler_params=pltpu.CompilerParams(vmem_limit_bytes=40 * 1024 * 1024),
        name="attend",
    )(items)
    return out.reshape(sources, CELLS, 128)


MESH = pl.DeviceIdType.MESH
SMALL = 80


def reduce_kernel(
    factor,
    normed_ref,
    expand_ref,
    mixed_ref,
    inner_ref,
    second_ref,
    project_ref,
    heads_ref,
    cot_ref,
    small_ref,
    out_ref,
    sums_ref,
    ga,
    gb,
    ra0,
    rb0,
    ra1,
    rb1,
    a1,
    b1,
    ra2,
    rb2,
    ab2,
    rz,
    s0,
    small0,
    smallz,
    smally,
    smallx,
    send_sems,
    recv_sems,
):
    f32, bf16 = jnp.float32, jnp.bfloat16
    lat, lon = lax.axis_index("lat"), lax.axis_index("lon")
    x_hi, y = lat // 4, lat % 4
    z, x_lo, core = lon // 4, (lon // 2) % 2, lon % 2
    x = x_hi * 2 + x_lo

    def place(px, py, pz, pc):
        return ((px // 2) * 4 + py, pz * 4 + (px % 2) * 2 + pc)

    other = 1 - core
    sibling = place(x, y, z, other)
    x_peers = [place((x + d) % 4, y, z, core) for d in range(1, 4)]
    y_peers = [place(x, (y + d) % 4, z, core) for d in range(1, 4)]
    z_peers = [place(x, y, (z + d) % 8, core) for d in range(1, 8)]
    barrier = pltpu.get_barrier_semaphore()
    peers = [sibling] + x_peers + y_peers + z_peers
    for peer in peers:
        pl.semaphore_signal(barrier, inc=1, device_id=peer, device_id_type=MESH)

    def half_lanes(top, bottom):
        lane = lax.broadcasted_iota(jnp.int32, top.shape, 1)
        even = jnp.where(lane < 64, top, pltpu.roll(bottom, 64, 1))
        odd = jnp.where(lane < 64, pltpu.roll(top, 64, 1), bottom)
        return even, odd

    def cross(left, right):
        return (
            lax.dot_general(left, right, (((0,), (0,)), ((), ())), preferred_element_type=f32)
            * factor
        )

    def expand_part(pz, carry):
        columns = pl.ds(pl.multiple_of(pz * 256, 256), 256)
        grad = cross(expand_ref[:, columns], normed_ref[...])
        for sub in range(4):
            plo, pc = sub // 2, sub % 2
            for pair in range(4):
                tile = slice(pair * 128, pair * 128 + 128)
                parts = half_lanes(
                    grad[sub * 64 : sub * 64 + 32, tile], grad[sub * 64 + 32 : sub * 64 + 64, tile]
                )
                for odd in range(2):
                    plat = pair * 2 + odd
                    px, py = (plat // 4) * 2 + plo, plat % 4
                    ga[pc, (px * 4 + py) * 8 + pz, 0:32, :] = parts[odd].astype(bf16)
        return carry

    def other_part(zz, carry):
        columns = pl.ds(pl.multiple_of(zz * 128, 128), 128)
        shrink = cross(inner_ref[:, columns], mixed_ref[...])
        grad_in = cross(
            project_ref[:, pl.ds(pl.multiple_of(zz * 384, 128), 384)], second_ref[...]
        )
        grad_out = cross(cot_ref[:, columns], heads_ref[...])
        for sub in range(8):
            pz, plo, pc = zz * 2 + sub // 4, (sub // 2) % 2, sub % 2
            for plat in range(8):
                px, py = (plat // 4) * 2 + plo, plat % 4
                rows = slice(sub * 16, sub * 16 + 16)
                ga[pc, (px * 4 + py) * 8 + pz, 32:48, :] = shrink[
                    rows, plat * 256 : plat * 256 + 128
                ].astype(bf16)
                gb[pc, (py * 4 + px) * 8 + pz, 0:16, :] = shrink[
                    rows, plat * 256 + 128 : plat * 256 + 256
                ].astype(bf16)
            for pair in range(4):
                tile = slice(pair * 128, pair * 128 + 128)
                top = jnp.concatenate(
                    [grad_in[sub * 48 : sub * 48 + 24, tile], grad_out[sub * 16 : sub * 16 + 8, tile]],
                    axis=0,
                )
                bottom = jnp.concatenate(
                    [
                        grad_in[sub * 48 + 24 : sub * 48 + 48, tile],
                        grad_out[sub * 16 + 8 : sub * 16 + 16, tile],
                    ],
                    axis=0,
                )
                parts = half_lanes(top, bottom)
                for odd in range(2):
                    plat = pair * 2 + odd
                    px, py = (plat // 4) * 2 + plo, plat % 4
                    gb[pc, (py * 4 + px) * 8 + pz, 16:48, :] = parts[odd].astype(bf16)
        return carry

    lax.fori_loop(0, 4, other_part, 0)
    lax.fori_loop(0, 8, expand_part, 0)
    pl.semaphore_wait(barrier, len(peers))

    count = [0]

    def copy(source, target, peer):
        index = count[0]
        count[0] += 1
        made = pltpu.make_async_remote_copy(
            src_ref=source,
            dst_ref=target,
            send_sem=send_sems.at[index],
            recv_sem=recv_sems.at[index],
            device_id=peer,
            device_id_type=MESH,
        )
        made.start()
        return made

    sent = []
    small_core = copy(small_ref.at[other], small0, sibling)
    first_a, first_b = [], []
    for d in (1, 2, 3, 0):
        rows = pl.ds(((x + d) % 4) * 32, 32)
        first_a.append((rows, copy(ga.at[other, rows], ra0.at[rows], sibling)))
        rows = pl.ds(((y + d) % 4) * 32, 32)
        first_b.append((rows, copy(gb.at[other, rows], rb0.at[rows], sibling)))

    small_core.wait_recv()
    s0[...] = small_ref[core] + small0[...]
    smallz[z] = s0[...]
    small_z = [copy(s0, smallz.at[z], peer) for peer in z_peers]

    def add_pair(mine, theirs, base):
        def body(step, carry):
            index = base + step * 4
            mine[core, pl.ds(index, 4)] = (
                mine[core, pl.ds(index, 4)].astype(f32) + theirs[pl.ds(index, 4)].astype(f32)
            ).astype(bf16)
            return carry

        lax.fori_loop(0, 8, body, 0)

    next_a, next_b = [], []
    for order, d in enumerate((1, 2, 3, 0)):
        rows, made = first_a[order]
        made.wait_recv()
        base = ((x + d) % 4) * 32
        add_pair(ga, ra0, base)
        if d:
            next_a.append(copy(ga.at[core, pl.ds(base, 32)], ra1.at[d - 1], x_peers[d - 1]))
        rows, made = first_b[order]
        made.wait_recv()
        base = ((y + d) % 4) * 32
        add_pair(gb, rb0, base)
        if d:
            next_b.append(copy(gb.at[core, pl.ds(base, 32)], rb1.at[d - 1], y_peers[d - 1]))

    def add_four(mine, theirs, total, base, blocks):
        def body(step, carry):
            index = step * 2
            value = mine(base + index).astype(f32)
            for d in range(3):
                value = value + theirs[d, pl.ds(index, 2)].astype(f32)
            total[pl.ds(index, 2)] = value.astype(bf16)
            return carry

        lax.fori_loop(0, blocks // 2, body, 0)

    for made in next_a:
        made.wait_recv()
    add_four(lambda i: ga[core, pl.ds(i, 2)], ra1, a1, x * 32, 32)
    last_a = [
        copy(a1.at[pl.ds(((y + d) % 4) * 8, 8)], ra2.at[d - 1], y_peers[d - 1]) for d in (1, 2, 3)
    ]
    for made in next_b:
        made.wait_recv()
    add_four(lambda i: gb[core, pl.ds(i, 2)], rb1, b1, y * 32, 32)
    last_b = [
        copy(b1.at[pl.ds(((x + d) % 4) * 8, 8)], rb2.at[d - 1], x_peers[d - 1]) for d in (1, 2, 3)
    ]

    for made in small_z:
        made.wait_recv()
    total = smallz[0]
    for index in range(1, 8):
        total = total + smallz[index]
    smally[y] = total
    small_y = [copy(smally.at[y], smally.at[y], peer) for peer in y_peers]

    def finish_pair(mine, theirs, first_row, base):
        def body(step, carry):
            value = mine[base + step].astype(f32)
            for d in range(3):
                value = value + theirs[d, step].astype(f32)
            ab2[step, first_row : first_row + 48, :] = value.astype(bf16)
            return carry

        lax.fori_loop(0, 8, body, 0)

    for made in last_a:
        made.wait_recv()
    finish_pair(a1, ra2, 0, y * 8)
    for made in last_b:
        made.wait_recv()
    finish_pair(b1, rb2, 48, x * 8)
    last = [copy(ab2.at[(z + d) % 8], rz.at[d - 1], z_peers[d - 1]) for d in range(1, 8)]

    for made in small_y:
        made.wait_recv()
    total = (smally[0] + smally[1]) + (smally[2] + smally[3])
    smallx[x] = total
    small_x = [copy(smallx.at[x], smallx.at[x], peer) for peer in x_peers]

    for made in last:
        made.wait_recv()
    value = ab2[z].astype(f32)
    for d in range(7):
        value = value + rz[d].astype(f32)
    out_ref[...] = value

    for made in small_x:
        made.wait_recv()
    s0_final = (smallx[0] + smallx[1]) + (smallx[2] + smallx[3])
    sums_ref[core] = s0_final
    final = copy(sums_ref.at[core], sums_ref.at[core], sibling)
    final.wait_recv()
    everything = (
        [small_core, final]
        + [made for _, made in first_a]
        + [made for _, made in first_b]
        + next_a
        + next_b
        + last_a
        + last_b
        + last
        + small_z
        + small_y
        + small_x
    )
    for made in everything:
        made.wait_send()


def reduce_all(factor, operands, small):
    f32, bf16 = jnp.float32, jnp.bfloat16
    vmem = pl.BlockSpec(memory_space=pltpu.VMEM)
    copies = 1 + 8 + 7 + 6 + 6 + 3 + 7 + 3 + 1
    return pl.pallas_call(
        functools.partial(reduce_kernel, factor),
        out_shape=(
            jax.ShapeDtypeStruct((96, 128), f32),
            jax.ShapeDtypeStruct((2, SMALL, 128), f32),
        ),
        in_specs=[vmem] * 9,
        out_specs=(vmem, vmem),
        scratch_shapes=[
            pltpu.VMEM((2, 128, 48, 128), bf16),
            pltpu.VMEM((2, 128, 48, 128), bf16),
            pltpu.VMEM((128, 48, 128), bf16),
            pltpu.VMEM((128, 48, 128), bf16),
            pltpu.VMEM((3, 32, 48, 128), bf16),
            pltpu.VMEM((3, 32, 48, 128), bf16),
            pltpu.VMEM((32, 48, 128), bf16),
            pltpu.VMEM((32, 48, 128), bf16),
            pltpu.VMEM((3, 8, 48, 128), bf16),
            pltpu.VMEM((3, 8, 48, 128), bf16),
            pltpu.VMEM((8, 96, 128), bf16),
            pltpu.VMEM((7, 96, 128), bf16),
            pltpu.VMEM((SMALL, 128), f32),
            pltpu.VMEM((SMALL, 128), f32),
            pltpu.VMEM((8, SMALL, 128), f32),
            pltpu.VMEM((4, SMALL, 128), f32),
            pltpu.VMEM((4, SMALL, 128), f32),
            pltpu.SemaphoreType.DMA((copies,)),
            pltpu.SemaphoreType.DMA((copies,)),
        ],
        compiler_params=pltpu.CompilerParams(
            vmem_limit_bytes=48 * 1024 * 1024, collective_id=1, has_side_effects=True
        ),
        name="reduce_grads",
    )(*operands, small)


def owner_blocks(block):
    def unfold(part):
        return jnp.concatenate([part[:, :64], part[:, 64:]], axis=0).T

    expand = unfold(block[0:32])
    shrink = jnp.concatenate([block[32:48], block[48:64]], axis=1).T
    grad_in = unfold(block[64:88])
    grad_out = unfold(block[88:96])
    return expand, shrink, grad_in, grad_out


def per_device(
    state_field,
    cotangent,
    key_bias,
    input_gain,
    expand_weight,
    depth_weight,
    shrink_weight,
    attention_gain,
    attention_in,
    attention_out,
):
    row_count, lon_count, channels = state_field.shape
    head_count = key_bias.shape[2]
    head_width = channels // head_count
    norm_factor = 1.0 / math.sqrt(
        row_count * lon_count * lax.axis_size("lat") * lax.axis_size("lon")
    )
    score_scale = 1.0 / math.sqrt(head_width)
    state_float = state_field.astype(jnp.float32)
    inverse_first = inverse_rms(state_float)
    normed = (state_float * inverse_first * input_gain).astype(jnp.bfloat16)
    expanded = jnp.dot(normed, expand_weight, preferred_element_type=jnp.float32)
    activated = jax.nn.silu(expanded).astype(jnp.bfloat16)
    padded = with_halo(activated, (("lon", 1),), 1, True)
    padded = with_halo(padded, (("lat", 0),), 1, False)
    convolved = depthwise_sum(padded, depth_weight, row_count, lon_count)
    mixed = jax.nn.silu(convolved).astype(jnp.bfloat16)
    inner_state = (
        state_float + jnp.dot(mixed, shrink_weight, preferred_element_type=jnp.float32)
    ).astype(jnp.bfloat16)
    inner_float = inner_state.astype(jnp.float32)
    inverse_second = inverse_rms(inner_float)
    normed_second = (inner_float * inverse_second * attention_gain).astype(jnp.bfloat16)
    wide_in = attention_in.reshape(channels, 3, head_count, head_width).transpose(0, 2, 1, 3)
    wide_in = wide_in.reshape(channels, head_count, 3 * head_width)
    wide_in = jnp.pad(wide_in, ((0, 0), (0, 0), (0, head_width)))
    wide_out = attention_out.T.reshape(channels, head_count, head_width)
    wide_out = jnp.pad(wide_out, ((0, 0), (0, 0), (3 * head_width, 0)))
    wide = jnp.concatenate([wide_in, wide_out], axis=0).reshape(2 * channels, -1)
    items = jnp.dot(
        jnp.concatenate([normed_second, cotangent], axis=-1),
        wide,
        preferred_element_type=jnp.float32,
    ).astype(jnp.bfloat16)
    items = items.reshape(row_count, lon_count, head_count, 4 * head_width)
    items = items.transpose(0, 2, 1, 3).reshape(row_count * head_count, lon_count, -1)
    bias_items = key_bias.transpose(0, 2, 1).reshape(row_count * head_count, 1, lon_count)
    bias_items = jnp.pad(bias_items, ((0, 0), (0, 0), (0, 4 * head_width - lon_count)))
    items = jnp.concatenate([items, bias_items], axis=1)
    items = jnp.pad(items, ((0, 0), (0, CELLS - lon_count - 1), (0, 0)))
    items = lax.all_to_all(items, "lon", split_axis=0, concat_axis=0, tiled=True)
    answers = attend_items(items, lon_count, score_scale)
    answers = lax.all_to_all(answers, "lon", split_axis=0, concat_axis=0, tiled=True)
    answers = answers.reshape(row_count, head_count, CELLS, 4, head_width)[:, :, :lon_count]
    answers = answers.transpose(0, 2, 3, 1, 4).reshape(row_count, lon_count, 4 * channels)
    back_projected = answers[..., : 3 * channels]
    heads_field = answers[..., 3 * channels :]
    output_field = (
        inner_float + jnp.dot(heads_field, attention_out, preferred_element_type=jnp.float32)
    ).astype(jnp.bfloat16)
    back_second = times_transpose(back_projected, attention_in)
    gain_two = jnp.sum(back_second * inner_float * inverse_second, axis=(0, 1)) * norm_factor
    back_inner = (
        cotangent.astype(jnp.float32)
        + norm_back(back_second, inner_float, inverse_second, attention_gain)
    ).astype(jnp.bfloat16)
    back_convolved = (times_transpose(back_inner, shrink_weight) * silu_slope(convolved)).astype(
        jnp.bfloat16
    )
    back_pad = with_halo(back_convolved, (("lon", 1),), 1, True)
    back_pad = with_halo(back_pad, (("lat", 0),), 1, False)
    back_activated = transposed_sum(back_pad, depth_weight, row_count, lon_count)
    back_conv_float = back_convolved.astype(jnp.float32)
    depth_local = (
        jnp.stack(
            [
                jnp.stack(
                    [
                        jnp.sum(
                            padded[
                                lat_step : lat_step + row_count, lon_step : lon_step + lon_count
                            ].astype(jnp.float32)
                            * back_conv_float,
                            axis=(0, 1),
                        )
                        for lon_step in range(3)
                    ]
                )
                for lat_step in range(3)
            ]
        )
        * norm_factor
    )
    back_expanded = (back_activated * silu_slope(expanded)).astype(jnp.bfloat16)
    back_normed = times_transpose(back_expanded, expand_weight)
    gain_one = jnp.sum(back_normed * state_float * inverse_first, axis=(0, 1)) * norm_factor
    input_grad = (
        back_inner.astype(jnp.float32)
        + norm_back(back_normed, state_float, inverse_first, input_gain)
    ).astype(jnp.bfloat16)
    wide_count = depth_local.shape[2]
    small = jnp.concatenate([depth_local.reshape(-1), gain_one, gain_two])
    small = jnp.pad(small, (0, 2 * SMALL * 128 - small.shape[0])).reshape(2, SMALL, 128)

    def flat(values):
        values = jnp.pad(values, ((0, 0), (0, CELLS - lon_count), (0, 0)))
        return values.reshape(row_count * CELLS, values.shape[2])

    block, sums = reduce_all(
        norm_factor,
        [
            flat(values)
            for values in (
                normed,
                back_expanded,
                mixed,
                back_inner,
                normed_second,
                back_projected,
                heads_field,
                cotangent,
            )
        ],
        small,
    )
    results = owner_blocks(block)
    sums = sums.reshape(-1)
    depth_grad = sums[: 9 * wide_count].reshape(3, 3, wide_count)
    input_gain_grad = sums[9 * wide_count : 9 * wide_count + channels]
    attention_gain_grad = sums[9 * wide_count + channels : 9 * wide_count + 2 * channels]
    return (
        output_field,
        input_grad,
        results[0],
        results[1],
        results[2],
        results[3],
        depth_grad,
        input_gain_grad,
        attention_gain_grad,
    )


def solution(mesh):
    placed = (
        P("lat", "lon", None),
        P("lat", "lon", None),
        P("lat", "lon", None),
        P(),
        P(),
        P(),
        P(),
        P(),
        P(),
        P(),
    )
    return jax.shard_map(
        per_device,
        mesh=mesh,
        in_specs=placed,
        out_specs=(
            P("lat", "lon", None),
            P("lat", "lon", None),
            P("lat", "lon"),
            P("lat", "lon"),
            P("lat", "lon"),
            P("lat", "lon"),
            P(),
            P(),
            P(),
        ),
        check_vma=False,
    )
```

time: 1140 us -> 281 us (0.25); the launches traced: 1130 us -> 280 us
  waiting for transfers between devices: 609 us -> 33.2 us
  Pallas kernels: 0 us -> 127 us
  other arithmetic: 127 us -> 15.7 us
  matrix products: 118 us -> 11.3 us
  starting transfers between devices: 82 us -> 21.7 us
  local copies, waits for them, and re-layouts: 93.8 us -> 33.8 us
  blocking collectives: 80 us -> 36.2 us
  between operations: 17.2 us -> 1.65 us
    reduce_scatter x5 -> x0, waiting for transfers between devices: 406 us -> none  [the longest x1 118 us: per_device(): lax.psum_scatter(expand_local.astype(jnp.bfloat16), 'lon', scatter_dimens...]
    unnamed x12 -> x0, waiting for transfers between devices: 146 us -> none
    pallas_call x0 -> x2, Pallas kernels: none -> 127 us  [the longest x1 71.2 us: attend_items(): pl.pallas_call(functools.partial(attend_kernel, valid, scale), out_shape=...]
    dot_general x33 -> x1, matrix products: 101 us -> 1.52 us  [per_device(): jnp.dot(jnp.concatenate([normed_second, cotangent], axis=-1), wide, prefe...]
    psum x1 -> x0, blocking collectives: 80 us -> none  [per_device(): lax.psum((depth_local, gain_one, gain_two), ('lat', 'lon'))]
    unnamed x6 -> x0, other arithmetic: 69 us -> none
    all_to_all x9 -> x1, starting transfers between devices: 66.3 us -> 5.36 us  [per_device(): lax.all_to_all(answers, 'lon', split_axis=0, concat_axis=0, tiled=True)]
    all_to_all x0 -> x1, blocking collectives: none -> 36.2 us  [per_device(): lax.all_to_all(items, 'lon', split_axis=0, concat_axis=0, tiled=True)]
  transfers between devices with their start and end apart: 26 -> 9, of which waited for: 16 -> 5; matrix products, arithmetic and copies ran while one was open for 24% -> 7% of each run, Pallas kernels for 0% -> 0%
where the time goes in v1:
time: 281 us; the launch traced here: 280 us
  Pallas kernels  127 us (45%)
  blocking collectives  36.2 us (13%)
  local copies, waits for them, and re-layouts  33.8 us (12%)
  waiting for transfers between devices  33.2 us (12%)
  starting transfers between devices  21.7 us (8%)
  other arithmetic  15.7 us (6%)
  matrix products  11.3 us (4%)
    pallas_call x1, Pallas kernels, attend_items(): pl.pallas_call(functools.partial(attend_kernel, valid, scale), out_shape=...  71.2 us
    pallas_call x1, Pallas kernels, reduce_all(): pl.pallas_call(functools.partial(reduce_kernel, factor), out_shape=(jax.S...  55.3 us
    all_to_all x1, blocking collectives, per_device(): lax.all_to_all(items, 'lon', split_axis=0, concat_axis=0, tiled=True)  36.2 us
    all_to_all x1, waiting for transfers between devices, per_device(): lax.all_to_all(answers, 'lon', split_axis=0, concat_axis=0, tiled=True)  19.6 us
    unnamed x137, local copies, waits for them, and re-layouts  15 us
    ppermute x4, waiting for transfers between devices, with_halo(): lax.ppermute(lax.slice_in_dim(block, 0, width, axis=dim), axis, backward)  9.12 us
    ppermute x4, starting transfers between devices, with_halo(): lax.ppermute(lax.slice_in_dim(block, block.shape[dim] - width, None, axis...  8.68 us
    ppermute x4, starting transfers between devices, with_halo(): lax.ppermute(lax.slice_in_dim(block, 0, width, axis=dim), axis, backward)  7.64 us
  transfers between devices with their start and end apart: 9, of which 5 were waited for; matrix products, arithmetic and copies ran while one was open for 7% of the time, Pallas kernels for 0%

profile of v1, /device:TPU:1, one launch (start us, length us, event | category | flops | bytes accessed | tf_op | source)
XLA Modules:
  0.0 279.9 jit_solution(8134394699685450430)
XLA Ops:
  2.4 2.8 multiply_convert_fusion.1
  5.2 3.3 %collective-permute-start.1 = (bf16[2,1,2048]{2,1,0:T(2,128)(2,1)S(1)}, bf16[2,1,2048]{2,1,0:T(2,128)(2,1)S(1)}, u32[]{:S(2)}, u32[]{:S(2)}) collective-permute-start(bf16[2,1,2048]{2,1,0:T(2,128)(2,1)S(1)} %get-tuple-element.72), channel_id=1, source_target_pairs={{1,0},{2,1},{3,2},{4,3},{5,4},{6,5},{7,6},{8,7},{9,8},{10,9},{11,1... | collective-permute-start | bytes 24584 | tf_op jit(solution)/shard_map/ppermute | solution.py:24
  8.6 2.6 copy.49
  11.2 1.6 copy.50
  14.4 2.8 %collective-permute-start.2 = (bf16[1,92,2048]{2,1,0:T(8,128)(2,1)S(1)}, bf16[1,92,2048]{2,1,0:T(8,128)(2,1)S(1)}, u32[]{:S(2)}, u32[]{:S(2)}) collective-permute-start(bf16[1,92,2048]{2,1,0:T(8,128)(2,1)S(1)} %get-tuple-element.69), channel_id=1, source_target_pairs={{0,32},{32,64},{64,96},{96,128},{128,160},{160,192},{192,224},{1,3... | collective-permute-start | bytes 1130504 | tf_op jit(solution)/shard_map/ppermute | solution.py:21
  18.7 3.2 %collective-permute-done.2 = bf16[1,92,2048]{2,1,0:T(8,128)(2,1)S(1)} collective-permute-done((bf16[1,92,2048]{2,1,0:T(8,128)(2,1)S(1)}, bf16[1,92,2048]{2,1,0:T(8,128)(2,1)S(1)}, u32[]{:S(2)}, u32[]{:S(2)}) %collective-permute-start.2) | collective-permute-done | bytes 376864 | tf_op jit(solution)/shard_map/ppermute | solution.py:21
  21.9 3.8 %collective-permute-done.3 = bf16[1,92,2048]{2,1,0:T(8,128)(2,1)S(1)} collective-permute-done((bf16[1,92,2048]{2,1,0:T(8,128)(2,1)S(1)}, bf16[1,92,2048]{2,1,0:T(8,128)(2,1)S(1)}, u32[]{:S(2)}, u32[]{:S(2)}) %collective-permute-start.3) | collective-permute-done | bytes 376864 | tf_op jit(solution)/shard_map/ppermute | solution.py:24
  26.3 3.0 %multiply_convert_fusion = (bf16[2,90,2048]{2,1,0:T(8,128)(2,1)S(1)}, f32[2,90,2048]{2,1,0:T(8,128)}) fusion(bf16[3,92,2048]{2,1,0:T(8,128)(2,1)S(1)} %get-tuple-element.64, f32[2048]{0:T(1024)S(1)} %bitcast.136, f32[2048]{0:T(1024)S(1)} %bitcast.138, f32[2048]{0:T(1024)S(1)} %bitcast.124, bf16[2,1,2048]{2,1,0:T(2,128)(2,1)S(1)} %collective-permute-done.1, ...), kind=kLoop, calls=%fused_computation.61 | loop fusion | flops 13639680 | bytes 7462912 | tf_op jit(solution)/shard_map/convert_element_type | solution.py:573
  30.5 1.5 convolution_convert_fusion
  34.8 36.2 %all_to_all.10.x_ref = bf16[32,96,128]{2,1,0:T(8,128)(2,1)S(1)} all-to-all(bf16[32,96,128]{2,1,0:T(8,128)(2,1)S(1)} %pad.50), channel_id=1, replica_groups=mesh['lat'=8,'lon'=32] {'lon'}, dimensions={0} | all-to-all | bytes 1572864 | tf_op jit(solution)/shard_map/all_to_all | solution.py:597
  71.0 71.2 %attend.1 = bf16[3072,128]{1,0:T(8,128)(2,1)} custom-call(bf16[32,96,128]{2,1,0:T(8,128)(2,1)S(1)} %all_to_all.10.x_ref), custom_call_target="tpu_custom_call" | custom-call | tf_op jit(solution)/shard_map/attend/pallas_call | solution.py:208
  142.2 5.4 %all-to-all-start.1 = ((bf16[32,96,128]{2,1,0:T(8,128)(2,1)}), bf16[32,96,128]{2,1,0:T(8,128)(2,1)}, u32[]{:S(2)}, u32[]{:S(2)}) async-start(bf16[32,96,128]{2,1,0:T(8,128)(2,1)} %bitcast.23), calls=%async_computation.1 | async-start | bytes 1572864 | tf_op jit(solution)/shard_map/all_to_all | solution.py:599
  150.2 19.6 %all-to-all-done.1 = bf16[32,96,128]{2,1,0:T(8,128)(2,1)} async-done(((bf16[32,96,128]{2,1,0:T(8,128)(2,1)}), bf16[32,96,128]{2,1,0:T(8,128)(2,1)}, u32[]{:S(2)}, u32[]{:S(2)}) %all-to-all-start.1) | async-done | bytes 786464 | tf_op jit(solution)/shard_map/all_to_all | solution.py:599
  169.8 2.3 copy.55
  177.2 3.8 %fusion.26 = (f32[2048]{0:T(1024)S(1)}, f32[2048]{0:T(1024)S(1)}, f32[2048]{0:T(1024)S(1)}, f32[2048]{0:T(1024)S(1)}, f32[2048]{0:T(1024)S(1)}, /*index=5*/f32[2...) fusion(bf16[3,92,2048]{2,1,0:T(8,128)(2,1)S(1)} %copy-done.6, ...), kind=kOutput, calls=%fused_computation.49 | convolution fusion | flops 393320448 | bytes 9744384 | tf_op jit(solution)/shard_map/dot_general | solution.py:59
  182.5 1.8 collective-permute-start.5
  189.2 2.3 copy.68
  192.6 1.8 copy.67
  194.4 1.6 pad.57
  199.7 4.8 %collective-permute-start.7 = (bf16[1,92,2048]{2,1,0:T(8,128)(2,1)}, bf16[1,92,2048]{2,1,0:T(8,128)(2,1)}, u32[]{:S(2)}, u32[]{:S(2)}) collective-permute-start(bf16[1,92,2048]{2,1,0:T(8,128)(2,1)} %get-tuple-element.66), channel_id=1, source_target_pairs={{0,32},{32,64},{64,96},{96,128},{128,160},{160,192},{192,224},{1,3... | collective-permute-start | bytes 1130504 | tf_op jit(solution)/shard_map/ppermute | solution.py:21
  206.3 5.3 %collective-permute-done.6 = bf16[1,92,2048]{2,1,0:T(8,128)(2,1)} collective-permute-done((bf16[1,92,2048]{2,1,0:T(8,128)(2,1)}, bf16[1,92,2048]{2,1,0:T(8,128)(2,1)}, u32[]{:S(2)}, u32[]{:S(2)}) %collective-permute-start.6) | collective-permute-done | bytes 376864 | tf_op jit(solution)/shard_map/ppermute | solution.py:24
  212.8 2.1 pad_maximum_fusion.1
  215.0 2.3 fusion.25
  219.7 55.3 %reduce_grads.1 = (f32[96,128]{1,0:T(8,128)S(1)}, f32[2,80,128]{2,1,0:T(8,128)S(1)}) custom-call(bf16[192,512]{1,0:T(8,128)(2,1)S(1)} %bitcast.107, bf16[192,2048]{1,0:T(8,128)(2,1)S(1)} %bitcast.101, bf16[192,2048]{1,0:T(8,128)(2,1)S(1)} %bitcast.100, bf16[192,512]{1,0:T(8,128)(2,1)S(1)} %bitcast.105, bf16[192,512]{1,0:T(8,128)(2,1)S(1)} %bitcast.104, ...), custom_call_target="tpu_custom_call" | custom-call | tf_op jit(solution)/shard_map/reduce_grads/pallas_call | solution.py:499
  (195 shorter events, 37.8 us)
Async XLA Ops:
  5.2 21.0 %copy-start.9 = (bf16[2,90,2048]{2,1,0:T(8,128)(2,1)}, bf16[2,90,2048]{2,1,0:T(8,128)(2,1)S(1)}, u32[]{:S(2)}) copy-start(bf16[2,90,2048]{2,1,0:T(8,128)(2,1)S(1)} %get-tuple-element.98) | copy-start | bytes 2211844
  5.2 8.9 %collective-permute-start.1 = (bf16[2,1,2048]{2,1,0:T(2,128)(2,1)S(1)}, bf16[2,1,2048]{2,1,0:T(2,128)(2,1)S(1)}, u32[]{:S(2)}, u32[]{:S(2)}) collective-permute-start(bf16[2,1,2048]{2,1,0:T(2,128)(2,1)S(1)} %get-tuple-element.72), channel_id=1, source_target_pairs={{1,0},{2,1},{3,2},{4,3},{5,4},{6,5},{7,6},{8,7},{9,8},{10,9},{11,1... | collective-permute-start | bytes 24584 | tf_op jit(solution)/shard_map/ppermute | solution.py:24
  8.6 5.6 %collective-permute-start = (bf16[2,1,2048]{2,1,0:T(2,128)(2,1)S(1)}, bf16[2,1,2048]{2,1,0:T(2,128)(2,1)S(1)}, u32[]{:S(2)}, u32[]{:S(2)}) collective-permute-start(bf16[2,1,2048]{2,1,0:T(2,128)(2,1)S(1)} %get-tuple-element.71), channel_id=1, source_target_pairs={{0,1},{1,2},{2,3},{3,4},{4,5},{5,6},{6,7},{7,8},{8,9},{9,10},{10,1... | collective-permute-start | bytes 24584 | tf_op jit(solution)/shard_map/ppermute | solution.py:21
  14.1 16.4 %copy-start.25 = (bf16[2,90,512]{2,1,0:T(8,128)(2,1)}, bf16[2,90,512]{2,1,0:T(8,128)(2,1)S(1)}, u32[]{:S(2)}) copy-start(bf16[2,90,512]{2,1,0:T(8,128)(2,1)S(1)} %copy.48) | copy-start | bytes 552964
  14.4 7.5 %collective-permute-start.2 = (bf16[1,92,2048]{2,1,0:T(8,128)(2,1)S(1)}, bf16[1,92,2048]{2,1,0:T(8,128)(2,1)S(1)}, u32[]{:S(2)}, u32[]{:S(2)}) collective-permute-start(bf16[1,92,2048]{2,1,0:T(8,128)(2,1)S(1)} %get-tuple-element.69), channel_id=1, source_target_pairs={{0,32},{32,64},{64,96},{96,128},{128,160},{160,192},{192,224},{1,3... | collective-permute-start | bytes 1130504 | tf_op jit(solution)/shard_map/ppermute | solution.py:21
  17.2 8.5 %collective-permute-start.3 = (bf16[1,92,2048]{2,1,0:T(8,128)(2,1)S(1)}, bf16[1,92,2048]{2,1,0:T(8,128)(2,1)S(1)}, u32[]{:S(2)}, u32[]{:S(2)}) collective-permute-start(bf16[1,92,2048]{2,1,0:T(8,128)(2,1)S(1)} %get-tuple-element.70), channel_id=1, source_target_pairs={{32,0},{64,32},{96,64},{128,96},{160,128},{192,160},{224,192},{33,... | collective-permute-start | bytes 1130504 | tf_op jit(solution)/shard_map/ppermute | solution.py:24
  71.0 76.6 %copy-start.26 = (bf16[2,90,512]{2,1,0:T(8,128)(2,1)S(1)}, bf16[2,90,512]{2,1,0:T(8,128)(2,1)}, u32[]{:S(2)}) copy-start(bf16[2,90,512]{2,1,0:T(8,128)(2,1)} %copy-done.25) | copy-start | bytes 552964
  142.2 27.6 %all-to-all-start.1 = ((bf16[32,96,128]{2,1,0:T(8,128)(2,1)}), bf16[32,96,128]{2,1,0:T(8,128)(2,1)}, u32[]{:S(2)}, u32[]{:S(2)}) async-start(bf16[32,96,128]{2,1,0:T(8,128)(2,1)} %bitcast.23), calls=%async_computation.1 | async-start | bytes 1572864 | tf_op jit(solution)/shard_map/all_to_all | solution.py:599
  176.5 9.5 %copy-start.18 = (bf16[2,90,512]{2,1,0:T(8,128)(2,1)}, bf16[2,90,512]{2,1,0:T(8,128)(2,1)S(1)}, u32[]{:S(2)}) copy-start(bf16[2,90,512]{2,1,0:T(8,128)(2,1)S(1)} %add_convert_fusion) | copy-start | bytes 552964
  182.5 13.6 %collective-permute-start.5 = (bf16[2,1,2048]{2,1,0:T(2,128)(2,1)}, bf16[2,1,2048]{2,1,0:T(2,128)(2,1)S(1)}, u32[]{:S(2)}, u32[]{:S(2)}) collective-permute-start(bf16[2,1,2048]{2,1,0:T(2,128)(2,1)} %get-tuple-element.68), channel_id=1, source_target_pairs={{1,0},{2,1},{3,2},{4,3},{5,4},{6,5},{7,6},{8,7},{9,8},{10,9},{11,1... | collective-permute-start | bytes 24584 | tf_op jit(solution)/shard_map/ppermute | solution.py:24
  184.3 11.8 %collective-permute-start.4 = (bf16[2,1,2048]{2,1,0:T(2,128)(2,1)}, bf16[2,1,2048]{2,1,0:T(2,128)(2,1)S(1)}, u32[]{:S(2)}, u32[]{:S(2)}) collective-permute-start(bf16[2,1,2048]{2,1,0:T(2,128)(2,1)} %get-tuple-element.67), channel_id=1, source_target_pairs={{0,1},{1,2},{2,3},{3,4},{4,5},{5,6},{6,7},{7,8},{8,9},{9,10},{10,1... | collective-permute-start | bytes 24584 | tf_op jit(solution)/shard_map/ppermute | solution.py:21
  198.4 13.1 %collective-permute-start.6 = (bf16[1,92,2048]{2,1,0:T(8,128)(2,1)}, bf16[1,92,2048]{2,1,0:T(8,128)(2,1)}, u32[]{:S(2)}, u32[]{:S(2)}) collective-permute-start(bf16[1,92,2048]{2,1,0:T(8,128)(2,1)} %get-tuple-element.65), channel_id=1, source_target_pairs={{32,0},{64,32},{96,64},{128,96},{160,128},{192,160},{224,192},{33,... | collective-permute-start | bytes 1130504 | tf_op jit(solution)/shard_map/ppermute | solution.py:24
  199.7 13.0 %collective-permute-start.7 = (bf16[1,92,2048]{2,1,0:T(8,128)(2,1)}, bf16[1,92,2048]{2,1,0:T(8,128)(2,1)}, u32[]{:S(2)}, u32[]{:S(2)}) collective-permute-start(bf16[1,92,2048]{2,1,0:T(8,128)(2,1)} %get-tuple-element.66), channel_id=1, source_target_pairs={{0,32},{32,64},{64,96},{96,128},{128,160},{160,192},{192,224},{1,3... | collective-permute-start | bytes 1130504 | tf_op jit(solution)/shard_map/ppermute | solution.py:21
  206.2 8.7 %copy-start.12 = (bf16[2,90,2048]{2,1,0:T(8,128)(2,1)S(1)}, bf16[2,90,2048]{2,1,0:T(8,128)(2,1)}, u32[]{:S(2)}) copy-start(bf16[2,90,2048]{2,1,0:T(8,128)(2,1)} %copy-done.11) | copy-start | bytes 2211844
  206.2 8.7 %copy-start.23 = (f32[2,90,2048]{2,1,0:T(8,128)S(1)}, f32[2,90,2048]{2,1,0:T(8,128)}, u32[]{:S(2)}) copy-start(f32[2,90,2048]{2,1,0:T(8,128)} %get-tuple-element.99) | copy-start | bytes 4423684
  206.2 8.7 %copy-start.32 = (bf16[2,1,2048]{2,1,0:T(2,128)(2,1)S(1)}, bf16[2,1,2048]{2,1,0:T(2,128)(2,1)}, u32[]{:S(2)}) copy-start(bf16[2,1,2048]{2,1,0:T(2,128)(2,1)} %copy-done.31) | copy-start | bytes 24580
  206.2 8.7 %copy-start.34 = (bf16[2,1,2048]{2,1,0:T(2,128)(2,1)S(1)}, bf16[2,1,2048]{2,1,0:T(2,128)(2,1)}, u32[]{:S(2)}) copy-start(bf16[2,1,2048]{2,1,0:T(2,128)(2,1)} %copy-done.33) | copy-start | bytes 24580
  206.2 8.7 %copy-start.38 = (f32[1,1,2048]{2,1,0:T(1,128)S(1)}, f32[1,1,2048]{2,1,0:T(1,128)}, u32[]{:S(2)}) copy-start(f32[1,1,2048]{2,1,0:T(1,128)} %copy-done.37) | copy-start | bytes 24580
  206.2 8.7 %copy-start.40 = (f32[1,1,2048]{2,1,0:T(1,128)S(1)}, f32[1,1,2048]{2,1,0:T(1,128)}, u32[]{:S(2)}) copy-start(f32[1,1,2048]{2,1,0:T(1,128)} %copy-done.39) | copy-start | bytes 24580
  206.3 8.7 %copy-start.42 = (f32[1,1,2048]{2,1,0:T(1,128)S(1)}, f32[1,1,2048]{2,1,0:T(1,128)}, u32[]{:S(2)}) copy-start(f32[1,1,2048]{2,1,0:T(1,128)} %copy-done.41) | copy-start | bytes 24580
  206.3 8.7 %copy-start.44 = (f32[1,1,2048]{2,1,0:T(1,128)S(1)}, f32[1,1,2048]{2,1,0:T(1,128)}, u32[]{:S(2)}) copy-start(f32[1,1,2048]{2,1,0:T(1,128)} %copy-done.43) | copy-start | bytes 24580
  206.3 8.7 %copy-start.46 = (f32[1,1,2048]{2,1,0:T(1,128)S(1)}, f32[1,1,2048]{2,1,0:T(1,128)}, u32[]{:S(2)}) copy-start(f32[1,1,2048]{2,1,0:T(1,128)} %copy-done.45) | copy-start | bytes 24580
  206.3 8.7 %copy-start.48 = (f32[1,1,2048]{2,1,0:T(1,128)S(1)}, f32[1,1,2048]{2,1,0:T(1,128)}, u32[]{:S(2)}) copy-start(f32[1,1,2048]{2,1,0:T(1,128)} %copy-done.47) | copy-start | bytes 24580
  206.3 8.7 %copy-start.50 = (f32[1,1,2048]{2,1,0:T(1,128)S(1)}, f32[1,1,2048]{2,1,0:T(1,128)}, u32[]{:S(2)}) copy-start(f32[1,1,2048]{2,1,0:T(1,128)} %copy-done.49) | copy-start | bytes 24580
  (49 other events, 173.4 us)

commit v2 on v1

--- a/solution.py
+++ b/solution.py
@@ -69,18 +69,81 @@
 
 
 CELLS = 96
-
-
-def attend_kernel(valid, scale, x_ref, out_ref, xt_ref, kaug_ref, vaug_ref, t_ref, pb_ref, acc_ref, qo_ref):
-    sources = x_ref.shape[0]
+MESH = pl.DeviceIdType.MESH
+
+
+def attend_kernel(
+    valid,
+    scale,
+    items_ref,
+    near_ref,
+    last_ref,
+    x_ref,
+    near_send,
+    last_send,
+    xt_ref,
+    kaug_ref,
+    vaug_ref,
+    t_ref,
+    pb_ref,
+    acc_ref,
+    cell_ref,
+    in_send,
+    in_recv,
+    near_send_sem,
+    near_recv_sem,
+    last_send_sem,
+    last_recv_sem,
+):
+    sources = items_ref.shape[0]
     total = sources * CELLS
-    block = 256
-    step = 512 if total % 512 == 0 else 256
+    block = t_ref.shape[1]
+    group = block // CELLS
     log2e = 1.4426950408889634
     to_log2 = scale * log2e
     f32, bf16 = jnp.float32, jnp.bfloat16
-
-    def prepare(index, carry):
+    lat, lon = lax.axis_index("lat"), lax.axis_index("lon")
+    z, low = lon // 4, lon % 4
+
+    def partner(k, sign):
+        ring, side = k // 4, 3 - k % 4
+        half = (ring + 1) // 2
+        shift = 4 + (1 - 2 * (ring % 2)) * half
+        x_lo, core = low // 2, low % 2
+        x_lo = x_lo + (side // 2) * (1 - 2 * x_lo)
+        core = core + (side % 2) * (1 - 2 * core)
+        return ((z + sign * shift + 8) % 8) * 4 + x_lo * 2 + core
+
+    barrier = pltpu.get_barrier_semaphore()
+
+    def greet(k, carry):
+        pl.semaphore_signal(
+            barrier, inc=1, device_id=(lat, partner(k, 1)), device_id_type=MESH
+        )
+        return carry
+
+    lax.fori_loop(0, sources - 1, greet, 0)
+    pl.semaphore_wait(barrier, sources - 1)
+
+    def incoming(k, slot):
+        to = partner(k, 1)
+        return pltpu.make_async_remote_copy(
+            src_ref=items_ref.at[to],
+            dst_ref=x_ref.at[slot],
+            send_sem=in_send.at[k],
+            recv_sem=in_recv.at[k],
+            device_id=(lat, to),
+            device_id_type=MESH,
+        )
+
+    def push(k, carry):
+        incoming(k, lon).start()
+        return carry
+
+    lax.fori_loop(0, sources - 1, push, 0)
+    x_ref[lon] = items_ref[lon]
+
+    def prepare(index):
         raw = x_ref[index].astype(f32)
         row = lax.broadcasted_iota(jnp.int32, (CELLS, 128), 0)
         lane = lax.broadcasted_iota(jnp.int32, (CELLS, 128), 1)
@@ -105,54 +168,59 @@
         start = pl.multiple_of(index * CELLS, 32)
         kaug_ref[pl.ds(start, CELLS), :] = keys.astype(bf16)
         vaug_ref[pl.ds(start, CELLS), :] = values.astype(bf16)
-        qo_ref[pl.ds(start, CELLS), :] = cell
-        return carry
-
-    lax.fori_loop(0, sources, prepare, 0)
+        cell_ref[pl.ds(start, CELLS), :] = cell
+
+    prepare(lon)
+
+    def arrive(k, carry):
+        source = partner(k, -1)
+        incoming(k, source).wait_recv()
+        prepare(source)
+        return carry
+
+    lax.fori_loop(0, sources - 1, arrive, 0)
 
     def turn(index, carry):
         start = pl.multiple_of(index * block, block)
-        xt_ref[:, pl.ds(start, block)] = qo_ref[pl.ds(start, block), :].T.astype(bf16)
-        acc_ref[pl.ds(start, block), :] = jnp.zeros((block, 128), f32)
+        xt_ref[:, pl.ds(start, block)] = cell_ref[pl.ds(start, block), :].T.astype(bf16)
+        acc_ref[:, pl.ds(start, block)] = jnp.zeros((64, block), f32)
         return carry
 
     lax.fori_loop(0, total // block, turn, 0)
 
-    def one_block(index, carry):
+    def packed(cells):
+        return (cells[:48] + pltpu.roll(cells[48:], 64, 1)).astype(bf16)
+
+    def nearby(source, slot):
+        return pltpu.make_async_remote_copy(
+            src_ref=near_send.at[source],
+            dst_ref=near_ref.at[slot],
+            send_sem=near_send_sem.at[source],
+            recv_sem=near_recv_sem.at[slot],
+            device_id=(lat, source),
+            device_id_type=MESH,
+        )
+
+    def one_block(turn_index, carry):
+        index = (turn_index + lon // group) % (sources // group)
         start = pl.multiple_of(index * block, block)
-        xq = qo_ref[pl.ds(start, block), :]
         xt = xt_ref[:, pl.ds(start, block)].astype(f32)
         query = xt[0:32] * to_log2
         first = query.astype(bf16).astype(f32)
         second = (query - first).astype(bf16).astype(f32)
         third = query - first - second
-        qaug = jnp.concatenate([first, second, third, jnp.ones((32, block), f32)], axis=0).astype(bf16)
-
-        def scores(part, highest):
-            begin = pl.multiple_of(part * step, step)
-            t = jnp.dot(kaug_ref[pl.ds(begin, step), :], qaug, preferred_element_type=f32)
-            t_ref[pl.ds(begin, step), :] = t
-            return jnp.maximum(highest, jnp.max(t.reshape(step // 8, 8, block), axis=0))
-
-        highest = lax.fori_loop(0, total // step, scores, jnp.full((8, block), -jnp.inf, f32))
-        highest = jnp.max(highest, axis=0, keepdims=True)
-
-        def weigh(part, carry):
-            norm, heads = carry
-            begin = pl.multiple_of(part * step, step)
-            p = jnp.exp2(t_ref[pl.ds(begin, step), :] - highest)
-            t_ref[pl.ds(begin, step), :] = p
-            low = p.astype(bf16)
-            pb_ref[pl.ds(begin, step), :] = low
-            norm = norm + jnp.sum(p.reshape(step // 8, 8, block), axis=0)
-            heads = heads + jnp.dot(
-                xt_ref[64:96, pl.ds(begin, step)], low, preferred_element_type=f32
-            )
-            return norm, heads
-
-        norm, heads = lax.fori_loop(
-            0, total // step, weigh, (jnp.zeros((8, block), f32), jnp.zeros((32, block), f32))
-        )
+        qaug = jnp.concatenate(
+            [first, second, third, jnp.ones((32, block), f32)], axis=0
+        ).astype(bf16)
+        t = jnp.dot(kaug_ref[...], qaug, preferred_element_type=f32)
+        t_ref[...] = t
+        highest = jnp.max(jnp.max(t.reshape(total // 8, 8, block), axis=0), axis=0, keepdims=True)
+        p = jnp.exp2(t_ref[...] - highest)
+        t_ref[...] = p
+        low_p = p.astype(bf16)
+        pb_ref[...] = low_p
+        norm = jnp.sum(p.reshape(total // 8, 8, block), axis=0)
+        heads = jnp.dot(xt_ref[64:96, :], low_p, preferred_element_type=f32)
         inverse = 1.0 / jnp.sum(norm, axis=0, keepdims=True)
         heads = heads * inverse
         back = xt[96:128]
@@ -164,68 +232,116 @@
         cen_second = (centred - cen_first).astype(bf16).astype(f32)
         cen_third = centred - cen_first - cen_second
         sub = lax.broadcasted_iota(jnp.int32, (64, block), 0)
-        cen = jnp.where(sub == 0, cen_first, jnp.where(sub == 1, cen_second, jnp.where(sub == 2, cen_third, 0.0)))
+        cen = jnp.where(
+            sub == 0,
+            cen_first,
+            jnp.where(sub == 1, cen_second, jnp.where(sub == 2, cen_third, 0.0)),
+        )
         baug = jnp.concatenate([back_first, back_second, -cen], axis=0).astype(bf16)
-        zeros = jnp.zeros((32, block), f32)
-        back_cells = jnp.concatenate([zeros, zeros, back_first, zeros], axis=0).T.astype(bf16)
-        lane = lax.broadcasted_iota(jnp.int32, (block, 128), 1)
-        query_cells = pltpu.roll(jnp.where(lane < 32, xq, 0.0), 32, 1).astype(bf16)
-
-        def grads(part, back_queries):
-            begin = pl.multiple_of(part * step, step)
-            dp = jnp.dot(vaug_ref[pl.ds(begin, step), :], baug, preferred_element_type=f32)
-            ds = (t_ref[pl.ds(begin, step), :] * dp).astype(bf16)
-            acc_ref[pl.ds(begin, step), :] += jnp.dot(
-                pb_ref[pl.ds(begin, step), :], back_cells, preferred_element_type=f32
-            ) + jnp.dot(ds, query_cells, preferred_element_type=f32)
-            return back_queries + jnp.dot(
-                xt_ref[32:64, pl.ds(begin, step)], ds, preferred_element_type=f32
-            )
-
-        back_queries = lax.fori_loop(0, total // step, grads, zeros)
-        turned = jnp.concatenate([back_queries * scale, zeros, zeros, heads], axis=0).T
-        out_ref[pl.ds(start, block), :] = turned.astype(bf16)
+        nt = (((1,), (1,)), ((), ()))
+        dp = jnp.dot(vaug_ref[...], baug, preferred_element_type=f32)
+        ds = (t_ref[...] * dp).astype(bf16)
+        acc_ref[32:64, :] += lax.dot_general(
+            back_first.astype(bf16), pb_ref[...], nt, preferred_element_type=f32
+        )
+        acc_ref[0:32, :] += lax.dot_general(
+            xt_ref[0:32, pl.ds(start, block)], ds, nt, preferred_element_type=f32
+        )
+        back_queries = jnp.dot(xt_ref[32:64, :], ds, preferred_element_type=f32)
+        zeros = jnp.zeros((64, block), f32)
+        done = jnp.concatenate([back_queries * scale, heads, zeros], axis=0).T
+        for part in range(group):
+            source = index * group + part
+            near_send[source] = packed(done[part * CELLS : part * CELLS + CELLS])
+
+            @pl.when(source != lon)
+            def _():
+                nearby(source, lon).start()
+
         return carry
 
     lax.fori_loop(0, total // block, one_block, 0)
+    near_ref[lon] = near_send[lon]
 
     def finish(index, carry):
         start = pl.multiple_of(index * block, block)
-        lane = lax.broadcasted_iota(jnp.int32, (block, 128), 1)
-        both = acc_ref[pl.ds(start, block), :]
-        both = jnp.where(lane < 64, both * scale, both)
-        both = jnp.where((lane >= 32) & (lane < 96), both, out_ref[pl.ds(start, block), :].astype(f32))
-        out_ref[pl.ds(start, block), :] = both.astype(bf16)
+        both = acc_ref[:, pl.ds(start, block)]
+        zeros = jnp.zeros((64, block), f32)
+        both = jnp.concatenate([both[0:32] * scale, both[32:64], zeros], axis=0)
+        cell_ref[pl.ds(start, block), :] = both.T
         return carry
 
     lax.fori_loop(0, total // block, finish, 0)
+
+    def final(k, to, slot):
+        return pltpu.make_async_remote_copy(
+            src_ref=last_send.at[to],
+            dst_ref=last_ref.at[slot],
+            send_sem=last_send_sem.at[k],
+            recv_sem=last_recv_sem.at[k],
+            device_id=(lat, to),
+            device_id_type=MESH,
+        )
+
+    def pack_last(source):
+        start = pl.multiple_of(source * CELLS, 32)
+        last_send[source] = packed(cell_ref[pl.ds(start, CELLS), :])
+
+    def leave(k, carry):
+        to = partner(k, 1)
+        pack_last(to)
+        final(k, to, lon).start()
+        return carry
+
+    lax.fori_loop(0, sources - 1, leave, 0)
+    pack_last(lon)
+    last_ref[lon] = last_send[lon]
+
+    def settle(k, carry):
+        to, source = partner(k, 1), partner(k, -1)
+        incoming(k, lon).wait_send()
+        nearby(to, lon).wait_send()
+        nearby(source, source).wait_recv()
+        made = final(k, to, source)
+        made.wait_send()
+        made.wait_recv()
+        return carry
+
+    lax.fori_loop(0, sources - 1, settle, 0)
 
 
 def attend_items(items, valid, scale):
     sources = items.shape[0]
     total = sources * CELLS
+    block = 768
     f32, bf16 = jnp.float32, jnp.bfloat16
-    out = pl.pallas_call(
+    vmem = pl.BlockSpec(memory_space=pltpu.VMEM)
+    answer = jax.ShapeDtypeStruct((sources, 48, 128), bf16)
+    return pl.pallas_call(
         functools.partial(attend_kernel, valid, scale),
-        out_shape=jax.ShapeDtypeStruct((total, 128), bf16),
-        in_specs=[pl.BlockSpec(memory_space=pltpu.VMEM)],
-        out_specs=pl.BlockSpec(memory_space=pltpu.VMEM),
+        out_shape=(answer, answer),
+        in_specs=[vmem],
+        out_specs=(vmem, vmem),
         scratch_shapes=[
+            pltpu.VMEM((sources, CELLS, 128), bf16),
+            pltpu.VMEM((sources, 48, 128), bf16),
+            pltpu.VMEM((sources, 48, 128), bf16),
             pltpu.VMEM((128, total), bf16),
             pltpu.VMEM((total, 128), bf16),
             pltpu.VMEM((total, 128), bf16),
-            pltpu.VMEM((total, 256), f32),
-            pltpu.VMEM((total, 256), bf16),
+            pltpu.VMEM((total, block), f32),
+            pltpu.VMEM((total, block), bf16),
+            pltpu.VMEM((64, total), f32),
             pltpu.VMEM((total, 128), f32),
-            pltpu.VMEM((total, 128), f32),
-        ],
-        compiler_params=pltpu.CompilerParams(vmem_limit_bytes=40 * 1024 * 1024),
+        ]
+        + [pltpu.SemaphoreType.DMA((sources,))] * 6,
+        compiler_params=pltpu.CompilerParams(
+            vmem_limit_bytes=48 * 1024 * 1024, collective_id=2, has_side_effects=True
+        ),
         name="attend",
     )(items)
-    return out.reshape(sources, CELLS, 128)
-
-
-MESH = pl.DeviceIdType.MESH
+
+
 SMALL = 80
 
 
@@ -594,13 +710,16 @@
     bias_items = jnp.pad(bias_items, ((0, 0), (0, 0), (0, 4 * head_width - lon_count)))
     items = jnp.concatenate([items, bias_items], axis=1)
     items = jnp.pad(items, ((0, 0), (0, CELLS - lon_count - 1), (0, 0)))
-    items = lax.all_to_all(items, "lon", split_axis=0, concat_axis=0, tiled=True)
-    answers = attend_items(items, lon_count, score_scale)
-    answers = lax.all_to_all(answers, "lon", split_axis=0, concat_axis=0, tiled=True)
-    answers = answers.reshape(row_count, head_count, CELLS, 4, head_width)[:, :, :lon_count]
-    answers = answers.transpose(0, 2, 3, 1, 4).reshape(row_count, lon_count, 4 * channels)
-    back_projected = answers[..., : 3 * channels]
-    heads_field = answers[..., 3 * channels :]
+    near, last = attend_items(items, lon_count, score_scale)
+
+    def unpack(parts):
+        parts = parts.reshape(row_count, head_count, CELLS // 2, 2, 2, head_width)
+        parts = parts.transpose(4, 0, 3, 2, 1, 5).reshape(2, row_count, CELLS, channels)
+        return parts[0, :, :lon_count], parts[1, :, :lon_count]
+
+    back_queries, heads_field = unpack(near)
+    back_keys, back_values = unpack(last)
+    back_projected = jnp.concatenate([back_queries, back_keys, back_values], axis=-1)
     output_field = (
         inner_float + jnp.dot(heads_field, attention_out, preferred_element_type=jnp.float32)
     ).astype(jnp.bfloat16)

time: 281 us -> 228 us (0.81)
  blocking collectives: 36.2 us -> 0 us
  waiting for transfers between devices: 33.2 us -> 9.64 us
  Pallas kernels: 127 us -> 137 us
  starting transfers between devices: 21.7 us -> 15.1 us
    all_to_all x1 -> x0, blocking collectives: 36.2 us -> none  [per_device(): lax.all_to_all(items, 'lon', split_axis=0, concat_axis=0, tiled=True)]
    all_to_all x1 -> x0, waiting for transfers between devices: 19.6 us -> none  [per_device(): lax.all_to_all(answers, 'lon', split_axis=0, concat_axis=0, tiled=True)]
    reshape x0 -> x4, local copies, waits for them, and re-layouts: none -> 11.7 us  [unpack(): parts.transpose(4, 0, 3, 2, 1, 5).reshape(2, row_count, CELLS, channels)]
    pallas_call x1, Pallas kernels: 71.2 us -> 78.8 us  [attend_items(): pl.pallas_call(functools.partial(attend_kernel, valid, scale), out_shape=...]
    all_to_all x1 -> x0, starting transfers between devices: 5.36 us -> none  [per_device(): lax.all_to_all(answers, 'lon', split_axis=0, concat_axis=0, tiled=True)]
    unnamed x137 -> x115, local copies, waits for them, and re-layouts: 15 us -> 10.2 us
    ppermute x4, waiting for transfers between devices: 9.12 us -> 5.51 us  [with_halo(): lax.ppermute(lax.slice_in_dim(block, 0, width, axis=dim), axis, backward)]
    pallas_call x1, Pallas kernels: 55.3 us -> 58.6 us  [reduce_all(): pl.pallas_call(functools.partial(reduce_kernel, factor), out_shape=(jax.S...]
  transfers between devices with their start and end apart: 9 -> 8, of which waited for: 5 -> 4; matrix products, arithmetic and copies ran while one was open for 7% -> 5% of each run, Pallas kernels for 0% -> 0%
where the time goes in v2:
time: 228 us; the launch traced here: 227 us
  Pallas kernels  137 us (60%)
  local copies, waits for them, and re-layouts  34.6 us (15%)
  other arithmetic  15.1 us (7%)
  starting transfers between devices  15.1 us (7%)
  matrix products  13.9 us (6%)
  waiting for transfers between devices  9.64 us (4%)
    pallas_call x1, Pallas kernels, attend_items(): pl.pallas_call(functools.partial(attend_kernel, valid, scale), out_shape=...  78.8 us
    pallas_call x1, Pallas kernels, reduce_all(): pl.pallas_call(functools.partial(reduce_kernel, factor), out_shape=(jax.S...  58.6 us
    reshape x4, local copies, waits for them, and re-layouts, unpack(): parts.transpose(4, 0, 3, 2, 1, 5).reshape(2, row_count, CELLS, channels)  11.7 us
    unnamed x115, local copies, waits for them, and re-layouts  10.2 us
    ppermute x4, starting transfers between devices, with_halo(): lax.ppermute(lax.slice_in_dim(block, block.shape[dim] - width, None, axis...  8.54 us
    dot_general x3, matrix products, times_transpose(): lax.dot_general(values, weights, (((values.ndim - 1,), (1,)), ((), ())),...  6.67 us
    ppermute x4, starting transfers between devices, with_halo(): lax.ppermute(lax.slice_in_dim(block, 0, width, axis=dim), axis, backward)  6.58 us
    ppermute x4, waiting for transfers between devices, with_halo(): lax.ppermute(lax.slice_in_dim(block, 0, width, axis=dim), axis, backward)  5.51 us
  transfers between devices with their start and end apart: 8, of which 4 were waited for; matrix products, arithmetic and copies ran while one was open for 5% of the time, Pallas kernels for 0%

profile of v2, /device:TPU:1, one launch (start us, length us, event | category | flops | bytes accessed | tf_op | source)
XLA Modules:
  0.0 227.5 jit_solution(7815307015649135977)
XLA Ops:
  2.4 2.8 %multiply_convert_fusion.1 = (bf16[2,90,2048]{2,1,0:T(8,128)(2,1)S(1)}, f32[2,90,2048]{2,1,0:T(8,128)}) fusion(bf16[512,2048]{1,0:T(8,128)(2,1)S(1)} %copy-done, f32[512]{0:T(512)} %param.13, f32[2,90]{1,0:T(2,128)S(1)} %get-tuple-element.94, bf16[2,90,512]{2,0,1:T(2,128)(2,1)} %param.10), kind=kOutput, calls=%fused_computation.63 | convolution fusion | flops 379699200 | bytes 4496080 | tf_op jit(solution)/shard_map/dot_general | solution.py:684
  5.3 3.3 %collective-permute-start.1 = (bf16[2,1,2048]{2,1,0:T(2,128)(2,1)S(1)}, bf16[2,1,2048]{2,1,0:T(2,128)(2,1)S(1)}, u32[]{:S(2)}, u32[]{:S(2)}) collective-permute-start(bf16[2,1,2048]{2,1,0:T(2,128)(2,1)S(1)} %get-tuple-element.67), channel_id=1, source_target_pairs={{1,0},{2,1},{3,2},{4,3},{5,4},{6,5},{7,6},{8,7},{9,8},{10,9},{11,1... | collective-permute-start | bytes 24584 | tf_op jit(solution)/shard_map/ppermute | solution.py:24
  8.6 2.6 %copy.33 = bf16[512,1536]{0,1:T(8,128)(2,1)} copy(bf16[512,1536]{1,0:T(8,128)(2,1)} %param.18) | data formatting | bytes 3145728 | tf_op args[8]
  11.2 1.6 copy.34
  14.7 2.7 %collective-permute-start.2 = (bf16[1,92,2048]{2,1,0:T(8,128)(2,1)S(1)}, bf16[1,92,2048]{2,1,0:T(8,128)(2,1)S(1)}, u32[]{:S(2)}, u32[]{:S(2)}) collective-permute-start(bf16[1,92,2048]{2,1,0:T(8,128)(2,1)S(1)} %get-tuple-element.64), channel_id=1, source_target_pairs={{0,32},{32,64},{64,96},{96,128},{128,160},{160,192},{192,224},{1,3... | collective-permute-start | bytes 1130504 | tf_op jit(solution)/shard_map/ppermute | solution.py:21
  18.9 3.2 %collective-permute-done.2 = bf16[1,92,2048]{2,1,0:T(8,128)(2,1)S(1)} collective-permute-done((bf16[1,92,2048]{2,1,0:T(8,128)(2,1)S(1)}, bf16[1,92,2048]{2,1,0:T(8,128)(2,1)S(1)}, u32[]{:S(2)}, u32[]{:S(2)}) %collective-permute-start.2) | collective-permute-done | bytes 376864 | tf_op jit(solution)/shard_map/ppermute | solution.py:21
  22.1 3.8 %collective-permute-done.3 = bf16[1,92,2048]{2,1,0:T(8,128)(2,1)S(1)} collective-permute-done((bf16[1,92,2048]{2,1,0:T(8,128)(2,1)S(1)}, bf16[1,92,2048]{2,1,0:T(8,128)(2,1)S(1)}, u32[]{:S(2)}, u32[]{:S(2)}) %collective-permute-start.3) | collective-permute-done | bytes 376864 | tf_op jit(solution)/shard_map/ppermute | solution.py:24
  26.5 3.2 %multiply_convert_fusion = (bf16[2,90,2048]{2,1,0:T(8,128)(2,1)S(1)}, f32[2,90,2048]{2,1,0:T(8,128)}) fusion(bf16[3,92,2048]{2,1,0:T(8,128)(2,1)S(1)} %get-tuple-element.59, f32[2048]{0:T(1024)S(1)} %bitcast.147, f32[2048]{0:T(1024)S(1)} %bitcast.149, f32[2048]{0:T(1024)S(1)} %bitcast.135, bf16[2,1,2048]{2,1,0:T(2,128)(2,1)S(1)} %collective-permute-done.1, ...), kind=kLoop, calls=%fused_computation.61 | loop fusion | flops 13639680 | bytes 7462912 | tf_op jit(solution)/shard_map/convert_element_type | solution.py:689
  31.4 2.5 %convolution_convert_fusion = bf16[2,90,2048]{2,1,0:T(8,128)(2,1)} fusion(bf16[1024,2048,1]{0,1,2:T(8,128)(2,1)S(1)} %bitcast.127, bf16[2,90,512]{2,1,0:T(8,128)(2,1)S(1)} %copy.32, bf16[2,90,512]{2,1,0:T(8,128)(2,1)S(1)} %multiply_convert_fusion.2), kind=kOutput, calls=%fused_computation.17 | convolution fusion | flops 756080640 | bytes 5300224 | tf_op jit(solution)/shard_map/dot_general | solution.py:702
  33.9 1.5 reshape.162
  35.8 78.8 %attend.1 = (bf16[32,48,128]{2,1,0:T(8,128)(2,1)S(1)}, bf16[32,48,128]{2,1,0:T(8,128)(2,1)S(1)}) custom-call(bf16[32,96,128]{2,1,0:T(8,128)(2,1)S(1)} %pad.50.items_ref), custom_call_target="tpu_custom_call" | custom-call | tf_op jit(solution)/shard_map/attend/pallas_call | solution.py:320
  114.6 1.4 copy.39
  116.1 3.1 %copy.55 = bf16[2,2,2,48,16,32]{5,4,3,2,1,0:T(8,128)(2,1)} copy(bf16[2,2,2,48,16,32]{3,5,0,2,4,1:T(8,128)(2,1)} %bitcast.128) | data formatting | bytes 786432 | tf_op jit(solution)/shard_map/reshape | solution.py:717
  119.2 2.7 %reshape.163 = bf16[2,2,96,512]{3,2,1,0:T(8,128)(2,1)S(1)} reshape(bf16[2,2,2,48,16,32]{5,4,3,2,1,0:T(8,128)(2,1)} %copy.55) | data formatting | bytes 786432 | tf_op jit(solution)/shard_map/reshape | solution.py:717
  123.2 1.4 copy.44
  124.7 3.1 %copy.57 = bf16[2,2,2,48,16,32]{5,4,3,2,1,0:T(8,128)(2,1)} copy(bf16[2,2,2,48,16,32]{3,5,0,2,4,1:T(8,128)(2,1)} %bitcast.129) | data formatting | bytes 786432 | tf_op jit(solution)/shard_map/reshape | solution.py:717
  127.8 2.7 %reshape.164 = bf16[2,2,96,512]{3,2,1,0:T(8,128)(2,1)S(1)} reshape(bf16[2,2,2,48,16,32]{5,4,3,2,1,0:T(8,128)(2,1)} %copy.57) | data formatting | bytes 786432 | tf_op jit(solution)/shard_map/reshape | solution.py:717
  130.6 1.3 copy-done.22
  135.1 4.4 %fusion.26 = (f32[2048]{0:T(1024)S(1)}, f32[2048]{0:T(1024)S(1)}, f32[2048]{0:T(1024)S(1)}, f32[2048]{0:T(1024)S(1)}, f32[2048]{0:T(1024)S(1)}, /*index=5*/f32[2...) fusion(bf16[3,92,2048]{2,1,0:T(8,128)(2,1)S(1)} %copy-done.6, ...), kind=kOutput, calls=%fused_computation.49 | convolution fusion | flops 393320448 | bytes 9744384 | tf_op jit(solution)/shard_map/dot_general | solution.py:59
  147.0 4.7 %collective-permute-start.7 = (bf16[1,92,2048]{2,1,0:T(8,128)(2,1)}, bf16[1,92,2048]{2,1,0:T(8,128)(2,1)}, u32[]{:S(2)}, u32[]{:S(2)}) collective-permute-start(bf16[1,92,2048]{2,1,0:T(8,128)(2,1)} %get-tuple-element.61), channel_id=1, source_target_pairs={{0,32},{32,64},{64,96},{96,128},{128,160},{160,192},{192,224},{1,3... | collective-permute-start | bytes 1130504 | tf_op jit(solution)/shard_map/ppermute | solution.py:21
  154.2 1.7 collective-permute-done.6
  156.7 2.1 pad_maximum_fusion.1
  159.0 2.6 %fusion.25 = bf16[2,90,2048]{2,1,0:T(8,128)(2,1)S(1)} fusion(bf16[2,90,2048]{2,1,0:T(8,128)(2,1)S(1)} %copy-done.12, f32[2,90,2048]{2,1,0:T(8,128)S(1)} %copy-done.23, bf16[3,92,2048]{2,1,0:T(8,128)(2,1)S(1)} %get-tuple-element.57, bf16[2,1,2048]{2,1,0:T(2,128)(2,1)S(1)} %copy-done.31, bf16[2,1,2048]{2,1,0:T(2,128)(2,1)S(1)} %copy-done.29, ...), kind=kLoop, calls=%fused_computation.48 | loop fusion | flops 15114240 | bytes 7462912 | tf_op jit(solution)/shard_map/convert_element_type | solution.py:759
  164.0 58.6 %reduce_grads.1 = (f32[96,128]{1,0:T(8,128)S(1)}, f32[2,80,128]{2,1,0:T(8,128)S(1)}) custom-call(bf16[192,512]{1,0:T(8,128)(2,1)S(1)} %bitcast.121, bf16[192,2048]{1,0:T(8,128)(2,1)S(1)} %bitcast.115, bf16[192,2048]{1,0:T(8,128)(2,1)S(1)} %bitcast.114, bf16[192,512]{1,0:T(8,128)(2,1)S(1)} %bitcast.118, bf16[192,512]{1,0:T(8,128)(2,1)S(1)} %bitcast.119, ...), custom_call_target="tpu_custom_call" | custom-call | tf_op jit(solution)/shard_map/reduce_grads/pallas_call | solution.py:615
  (177 shorter events, 29.9 us)
Async XLA Ops:
  5.2 21.1 %copy-start.9 = (bf16[2,90,2048]{2,1,0:T(8,128)(2,1)}, bf16[2,90,2048]{2,1,0:T(8,128)(2,1)S(1)}, u32[]{:S(2)}) copy-start(bf16[2,90,2048]{2,1,0:T(8,128)(2,1)S(1)} %get-tuple-element.97) | copy-start | bytes 2211844
  5.3 9.2 %collective-permute-start.1 = (bf16[2,1,2048]{2,1,0:T(2,128)(2,1)S(1)}, bf16[2,1,2048]{2,1,0:T(2,128)(2,1)S(1)}, u32[]{:S(2)}, u32[]{:S(2)}) collective-permute-start(bf16[2,1,2048]{2,1,0:T(2,128)(2,1)S(1)} %get-tuple-element.67), channel_id=1, source_target_pairs={{1,0},{2,1},{3,2},{4,3},{5,4},{6,5},{7,6},{8,7},{9,8},{10,9},{11,1... | collective-permute-start | bytes 24584 | tf_op jit(solution)/shard_map/ppermute | solution.py:24
  8.6 5.9 %collective-permute-start = (bf16[2,1,2048]{2,1,0:T(2,128)(2,1)S(1)}, bf16[2,1,2048]{2,1,0:T(2,128)(2,1)S(1)}, u32[]{:S(2)}, u32[]{:S(2)}) collective-permute-start(bf16[2,1,2048]{2,1,0:T(2,128)(2,1)S(1)} %get-tuple-element.66), channel_id=1, source_target_pairs={{0,1},{1,2},{2,3},{3,4},{4,5},{5,6},{6,7},{7,8},{8,9},{9,10},{10,1... | collective-permute-start | bytes 24584 | tf_op jit(solution)/shard_map/ppermute | solution.py:21
  14.7 7.4 %collective-permute-start.2 = (bf16[1,92,2048]{2,1,0:T(8,128)(2,1)S(1)}, bf16[1,92,2048]{2,1,0:T(8,128)(2,1)S(1)}, u32[]{:S(2)}, u32[]{:S(2)}) collective-permute-start(bf16[1,92,2048]{2,1,0:T(8,128)(2,1)S(1)} %get-tuple-element.64), channel_id=1, source_target_pairs={{0,32},{32,64},{64,96},{96,128},{128,160},{160,192},{192,224},{1,3... | collective-permute-start | bytes 1130504 | tf_op jit(solution)/shard_map/ppermute | solution.py:21
  17.4 8.5 %collective-permute-start.3 = (bf16[1,92,2048]{2,1,0:T(8,128)(2,1)S(1)}, bf16[1,92,2048]{2,1,0:T(8,128)(2,1)S(1)}, u32[]{:S(2)}, u32[]{:S(2)}) collective-permute-start(bf16[1,92,2048]{2,1,0:T(8,128)(2,1)S(1)} %get-tuple-element.65), channel_id=1, source_target_pairs={{32,0},{64,32},{96,64},{128,96},{160,128},{192,160},{224,192},{33,... | collective-permute-start | bytes 1130504 | tf_op jit(solution)/shard_map/ppermute | solution.py:24
  18.8 7.6 %copy-start.33 = (f32[1,1,2048]{2,1,0:T(1,128)}, f32[1,1,2048]{2,1,0:T(1,128)S(1)}, u32[]{:S(2)}) copy-start(f32[1,1,2048]{2,1,0:T(1,128)S(1)} %get-tuple-element.85) | copy-start | bytes 24580
  18.8 7.6 %copy-start.35 = (f32[1,1,2048]{2,1,0:T(1,128)}, f32[1,1,2048]{2,1,0:T(1,128)S(1)}, u32[]{:S(2)}) copy-start(f32[1,1,2048]{2,1,0:T(1,128)S(1)} %get-tuple-element.86) | copy-start | bytes 24580
  18.8 7.6 %copy-start.37 = (f32[1,1,2048]{2,1,0:T(1,128)}, f32[1,1,2048]{2,1,0:T(1,128)S(1)}, u32[]{:S(2)}) copy-start(f32[1,1,2048]{2,1,0:T(1,128)S(1)} %get-tuple-element.87) | copy-start | bytes 24580
  18.8 7.6 %copy-start.39 = (f32[1,1,2048]{2,1,0:T(1,128)}, f32[1,1,2048]{2,1,0:T(1,128)S(1)}, u32[]{:S(2)}) copy-start(f32[1,1,2048]{2,1,0:T(1,128)S(1)} %get-tuple-element.88) | copy-start | bytes 24580
  18.8 7.6 %copy-start.41 = (f32[1,1,2048]{2,1,0:T(1,128)}, f32[1,1,2048]{2,1,0:T(1,128)S(1)}, u32[]{:S(2)}) copy-start(f32[1,1,2048]{2,1,0:T(1,128)S(1)} %get-tuple-element.89) | copy-start | bytes 24580
  18.8 7.6 %copy-start.43 = (f32[1,1,2048]{2,1,0:T(1,128)}, f32[1,1,2048]{2,1,0:T(1,128)S(1)}, u32[]{:S(2)}) copy-start(f32[1,1,2048]{2,1,0:T(1,128)S(1)} %get-tuple-element.90) | copy-start | bytes 24580
  18.8 7.6 %copy-start.45 = (f32[1,1,2048]{2,1,0:T(1,128)}, f32[1,1,2048]{2,1,0:T(1,128)S(1)}, u32[]{:S(2)}) copy-start(f32[1,1,2048]{2,1,0:T(1,128)S(1)} %get-tuple-element.91) | copy-start | bytes 24580
  18.9 7.6 %copy-start.47 = (f32[1,1,2048]{2,1,0:T(1,128)}, f32[1,1,2048]{2,1,0:T(1,128)S(1)}, u32[]{:S(2)}) copy-start(f32[1,1,2048]{2,1,0:T(1,128)S(1)} %get-tuple-element.92) | copy-start | bytes 24580
  133.4 8.1 %copy-start.18 = (bf16[2,90,512]{2,1,0:T(8,128)(2,1)}, bf16[2,90,512]{2,1,0:T(8,128)(2,1)S(1)}, u32[]{:S(2)}) copy-start(bf16[2,90,512]{2,1,0:T(8,128)(2,1)S(1)} %add_convert_fusion) | copy-start | bytes 552964
  135.1 6.4 %copy-start.14 = (bf16[2,90,2048]{2,1,0:T(8,128)(2,1)S(1)}, bf16[2,90,2048]{2,1,0:T(8,128)(2,1)}, u32[]{:S(2)}) copy-start(bf16[2,90,2048]{2,1,0:T(8,128)(2,1)} %copy-done.13) | copy-start | bytes 2211844
  139.5 5.1 %copy-start.11 = (bf16[2,90,2048]{2,1,0:T(8,128)(2,1)}, bf16[2,90,2048]{2,1,0:T(8,128)(2,1)S(1)}, u32[]{:S(2)}) copy-start(bf16[2,90,2048]{2,1,0:T(8,128)(2,1)S(1)} %get-tuple-element.103) | copy-start | bytes 2211844
  139.5 5.0 %collective-permute-start.5 = (bf16[2,1,2048]{2,1,0:T(2,128)(2,1)S(1)}, bf16[2,1,2048]{2,1,0:T(2,128)(2,1)S(1)}, u32[]{:S(2)}, u32[]{:S(2)}) collective-permute-start(bf16[2,1,2048]{2,1,0:T(2,128)(2,1)S(1)} %get-tuple-element.63), channel_id=1, source_target_pairs={{1,0},{2,1},{3,2},{4,3},{5,4},{6,5},{7,6},{8,7},{9,8},{10,9},{11,1... | collective-permute-start | bytes 24584 | tf_op jit(solution)/shard_map/ppermute | solution.py:24
  140.2 4.3 %collective-permute-start.4 = (bf16[2,1,2048]{2,1,0:T(2,128)(2,1)S(1)}, bf16[2,1,2048]{2,1,0:T(2,128)(2,1)S(1)}, u32[]{:S(2)}, u32[]{:S(2)}) collective-permute-start(bf16[2,1,2048]{2,1,0:T(2,128)(2,1)S(1)} %get-tuple-element.62), channel_id=1, source_target_pairs={{0,1},{1,2},{2,3},{3,4},{4,5},{5,6},{6,7},{7,8},{8,9},{9,10},{10,1... | collective-permute-start | bytes 24584 | tf_op jit(solution)/shard_map/ppermute | solution.py:21
  145.8 10.1 %collective-permute-start.6 = (bf16[1,92,2048]{2,1,0:T(8,128)(2,1)}, bf16[1,92,2048]{2,1,0:T(8,128)(2,1)}, u32[]{:S(2)}, u32[]{:S(2)}) collective-permute-start(bf16[1,92,2048]{2,1,0:T(8,128)(2,1)} %get-tuple-element.60), channel_id=1, source_target_pairs={{32,0},{64,32},{96,64},{128,96},{160,128},{192,160},{224,192},{33,... | collective-permute-start | bytes 1130504 | tf_op jit(solution)/shard_map/ppermute | solution.py:24
  147.0 9.7 %collective-permute-start.7 = (bf16[1,92,2048]{2,1,0:T(8,128)(2,1)}, bf16[1,92,2048]{2,1,0:T(8,128)(2,1)}, u32[]{:S(2)}, u32[]{:S(2)}) collective-permute-start(bf16[1,92,2048]{2,1,0:T(8,128)(2,1)} %get-tuple-element.61), channel_id=1, source_target_pairs={{0,32},{32,64},{64,96},{96,128},{128,160},{160,192},{192,224},{1,3... | collective-permute-start | bytes 1130504 | tf_op jit(solution)/shard_map/ppermute | solution.py:21
  154.1 4.8 %copy-start.34 = (f32[1,1,2048]{2,1,0:T(1,128)S(1)}, f32[1,1,2048]{2,1,0:T(1,128)}, u32[]{:S(2)}) copy-start(f32[1,1,2048]{2,1,0:T(1,128)} %copy-done.33) | copy-start | bytes 24580
  154.1 4.8 %copy-start.36 = (f32[1,1,2048]{2,1,0:T(1,128)S(1)}, f32[1,1,2048]{2,1,0:T(1,128)}, u32[]{:S(2)}) copy-start(f32[1,1,2048]{2,1,0:T(1,128)} %copy-done.35) | copy-start | bytes 24580
  154.1 4.8 %copy-start.38 = (f32[1,1,2048]{2,1,0:T(1,128)S(1)}, f32[1,1,2048]{2,1,0:T(1,128)}, u32[]{:S(2)}) copy-start(f32[1,1,2048]{2,1,0:T(1,128)} %copy-done.37) | copy-start | bytes 24580
  154.1 4.8 %copy-start.40 = (f32[1,1,2048]{2,1,0:T(1,128)S(1)}, f32[1,1,2048]{2,1,0:T(1,128)}, u32[]{:S(2)}) copy-start(f32[1,1,2048]{2,1,0:T(1,128)} %copy-done.39) | copy-start | bytes 24580
  (39 other events, 95.9 us)

commit v3 on v2

v3 whole, which is shorter than its diff:
```python
import functools
import math

import jax
import jax.numpy as jnp
from jax import lax
from jax.experimental import pallas as pl
from jax.experimental.pallas import tpu as pltpu
from jax.sharding import PartitionSpec as P

EPSILON = 1e-06
CELLS = 96
MESH = pl.DeviceIdType.MESH


CHUNK = 256


def silu_parts(values):
    sigmoid = 1.0 / (1.0 + jnp.exp(-values))
    return values * sigmoid, sigmoid * (1.0 + values * (1.0 - sigmoid))


def halo_copies(rows, edges, row_slots, edge_slots, sends, recvs):
    lat, lon = lax.axis_index("lat"), lax.axis_index("lon")
    bands, sectors = lax.axis_size("lat"), lax.axis_size("lon")
    west, east = (lon + sectors - 1) % sectors, (lon + 1) % sectors

    def made(source, target, index, peer):
        return pltpu.make_async_remote_copy(
            src_ref=source,
            dst_ref=target,
            send_sem=sends.at[index],
            recv_sem=recvs.at[index],
            device_id=peer,
            device_id_type=MESH,
        )

    north, south = lat > 0, lat < bands - 1
    copies = [
        (north, south, made(rows.at[0], row_slots.at[1], 0, (lat - 1, lon))),
        (south, north, made(rows.at[1], row_slots.at[0], 1, (lat + 1, lon))),
    ]
    for side, column in ((0, west), (1, east)):
        for slot in range(3):
            step = 1 - slot
            sends_it = (None, south, north)[step]
            gets_it = (None, north, south)[step]
            copies.append(
                (
                    sends_it,
                    gets_it,
                    made(
                        edges.at[side],
                        edge_slots.at[side, slot],
                        2 + side * 3 + slot,
                        (lat + step, column),
                    ),
                )
            )
    return copies


def guarded(condition, action):
    if condition is None:
        action()
    else:
        pl.when(condition)(action)


def halo_start(copies):
    for sends_it, _, made in copies:
        guarded(sends_it, made.start)


def halo_arrive(copies):
    for _, gets_it, made in copies:
        guarded(gets_it, made.wait_recv)


def halo_leave(copies):
    for sends_it, _, made in copies:
        guarded(sends_it, made.wait_send)


def halo_greet(barrier):
    lat, lon = lax.axis_index("lat"), lax.axis_index("lon")
    bands, sectors = lax.axis_size("lat"), lax.axis_size("lon")
    west, east = (lon + sectors - 1) % sectors, (lon + 1) % sectors

    def signal(row, column):
        pl.semaphore_signal(barrier, inc=1, device_id=(row, column), device_id_type=MESH)

    signal(lat, west)
    signal(lat, east)

    @pl.when(lat > 0)
    def _():
        for column in (west, lon, east):
            signal(lat - 1, column)

    @pl.when(lat < bands - 1)
    def _():
        for column in (west, lon, east):
            signal(lat + 1, column)

    north, south = (lat + bands - 1) // bands, (2 * bands - 2 - lat) // bands
    return 2 + 3 * north + 3 * south


def edge_pair(top, bottom, last):
    sub = lax.broadcasted_iota(jnp.int32, (8, top.shape[1]), 0)
    west = jnp.where(sub == 0, top[0:1], bottom[0:1])
    east = jnp.where(sub == 0, top[last : last + 1], bottom[last : last + 1])
    return west, east


def halo_row(index, base, edge_slots, valid, lanes=slice(None)):
    slot, row = ((0, 1), (1, 0), (1, 1), (2, 0))[index]
    place = lax.broadcasted_iota(jnp.int32, base.shape, 0)
    east = edge_slots[0, slot, row : row + 1, lanes]
    west = edge_slots[1, slot, row : row + 1, lanes]
    value = jnp.where(place == valid, east, jnp.where(place == CELLS - 1, west, base))
    lat, bands = lax.axis_index("lat"), lax.axis_size("lat")
    if index == 0:
        value = jnp.where(lat > 0, value, 0.0)
    if index == 3:
        value = jnp.where(lat < bands - 1, value, 0.0)
    return value


def inside(shape, valid):
    return lax.broadcasted_iota(jnp.int32, shape, 0) < valid


def inverse_rms(values):
    return lax.rsqrt(jnp.mean(values * values, axis=-1, keepdims=True) + EPSILON)


def nt_dot(left, right):
    return lax.dot_general(
        left, right, (((1,), (1,)), ((), ())), preferred_element_type=jnp.float32
    )


def forward_kernel(
    state_ref,
    cot_ref,
    bias_ref,
    first_gain,
    expand_ref,
    depth_ref,
    shrink_ref,
    second_gain,
    in_ref,
    out_ref,
    items_ref,
    act_ref,
    slope_ref,
    slope_expanded_ref,
    mixed_ref,
    normed_ref,
    inner_ref,
    second_ref,
    slope_edges,
    rows,
    edges,
    row_slots,
    edge_slots,
    wide_normed,
    total_ref,
    project_ref,
    cot_pad,
    sends,
    recvs,
):
    f32, bf16 = jnp.float32, jnp.bfloat16
    valid = state_ref.shape[1]
    barrier = pltpu.get_barrier_semaphore()
    greetings = halo_greet(barrier)
    rows[...] = jnp.zeros(rows.shape, bf16)
    cot_pad[...] = jnp.zeros(cot_pad.shape, bf16)
    for i in range(2):
        rows[i, 0:valid, :] = state_ref[i]
        cot_pad[i * CELLS : i * CELLS + valid, :] = cot_ref[i]
    west, east = edge_pair(rows[0].astype(f32), rows[1].astype(f32), valid - 1)
    edges[0] = west
    edges[1] = east
    pl.semaphore_wait(barrier, greetings)
    copies = halo_copies(rows, edges, row_slots, edge_slots, sends, recvs)
    halo_start(copies)
    project_ref[:, 1536:2048] = nt_dot(cot_pad[...], out_ref[...]).astype(bf16)
    total_ref[...] = jnp.zeros(total_ref.shape, f32)
    halo_arrive(copies)
    for r in range(4):
        base = rows[r - 1] if r in (1, 2) else row_slots[r // 3]
        value = halo_row(r, base.astype(f32), edge_slots, valid)
        value = (value * inverse_rms(value) * first_gain[...]).astype(bf16)
        wide_normed[r * CELLS : r * CELLS + CELLS, :] = value
        if r in (1, 2):
            keep = inside(value.shape, valid)
            own = jnp.where(keep, value.astype(f32), 0.0).astype(bf16)
            normed_ref[(r - 1) * CELLS : r * CELLS, :] = own

    def chunk(index, carry):
        lanes = pl.ds(pl.multiple_of(index * CHUNK, CHUNK), CHUNK)
        expanded = jnp.dot(wide_normed[...], expand_ref[:, lanes], preferred_element_type=f32)
        activated, slope = silu_parts(expanded)
        activated = activated.astype(bf16)
        slope_expanded_ref[:, lanes] = slope[CELLS : 3 * CELLS].astype(bf16)
        planes = []
        for r in range(4):
            plane = activated[r * CELLS : r * CELLS + CELLS]
            act_ref[r, :, lanes] = plane
            planes.append(plane.astype(f32))
        mixes, slopes = [], []
        for i in range(2):
            sums = []
            for b in range(3):
                part = depth_ref[b : b + 1, lanes] * planes[i]
                for a in (1, 2):
                    part = part + depth_ref[a * 3 + b : a * 3 + b + 1, lanes] * planes[i + a]
                sums.append(part)
            convolved = pltpu.roll(sums[0], 1, 0) + sums[1] + pltpu.roll(sums[2], CELLS - 1, 0)
            mixed, slope = silu_parts(convolved)
            keep = inside(mixed.shape, valid)
            mixes.append(jnp.where(keep, mixed, 0.0).astype(bf16))
            slope = jnp.where(keep, slope, 0.0)
            slope_ref[i, :, lanes] = slope.astype(bf16)
            slopes.append(slope)
        west, east = edge_pair(slopes[0], slopes[1], valid - 1)
        slope_edges[0, :, lanes] = west
        slope_edges[1, :, lanes] = east
        mixed = jnp.concatenate(mixes, axis=0)
        mixed_ref[:, lanes] = mixed
        total_ref[...] += jnp.dot(
            mixed,
            shrink_ref[pl.ds(pl.multiple_of(index * CHUNK, CHUNK), CHUNK), :],
            preferred_element_type=f32,
        )
        return carry

    lax.fori_loop(0, expand_ref.shape[1] // CHUNK, chunk, 0)
    for i in range(2):
        inner = (rows[i].astype(f32) + total_ref[i * CELLS : i * CELLS + CELLS, :]).astype(bf16)
        inner_ref[i * CELLS : i * CELLS + CELLS, :] = inner
        inner = inner.astype(f32)
        second = (inner * inverse_rms(inner) * second_gain[...]).astype(bf16)
        second_ref[i * CELLS : i * CELLS + CELLS, :] = second
    project_ref[:, 0:1536] = jnp.dot(
        second_ref[...], in_ref[...], preferred_element_type=f32
    ).astype(bf16)
    lane = lax.broadcasted_iota(jnp.int32, (CELLS, 128), 1)
    row = lax.broadcasted_iota(jnp.int32, (CELLS, 128), 0)
    for i in range(2):
        for tile in range(4):
            parts = [
                project_ref[
                    i * CELLS : i * CELLS + CELLS, part * 512 + tile * 128 : part * 512 + tile * 128 + 128
                ].astype(f32)
                for part in range(4)
            ]
            for u in range(4):
                item = i * 16 + tile * 4 + u
                moved = [
                    value if part == u else pltpu.roll(value, ((part - u) * 32) % 128, 1)
                    for part, value in enumerate(parts)
                ]
                value = jnp.where(
                    lane < 64,
                    jnp.where(lane < 32, moved[0], moved[1]),
                    jnp.where(lane < 96, moved[2], moved[3]),
                )
                value = jnp.where(row == valid, bias_ref[item : item + 1, :], value)
                items_ref[item] = value.astype(bf16)
    halo_leave(copies)


def forward_pass(state, cotangent, bias, first_gain, expand, depth, shrink, second_gain, weight_in, weight_out):
    f32, bf16 = jnp.float32, jnp.bfloat16
    vmem = pl.BlockSpec(memory_space=pltpu.VMEM)
    cells, wide, channels = 2 * CELLS, expand.shape[1], expand.shape[0]
    shaped = jax.ShapeDtypeStruct
    return pl.pallas_call(
        forward_kernel,
        out_shape=(
            shaped((32, CELLS, 128), bf16),
            shaped((4, CELLS, wide), bf16),
            shaped((2, CELLS, wide), bf16),
            shaped((cells, wide), bf16),
            shaped((cells, wide), bf16),
            shaped((cells, channels), bf16),
            shaped((cells, channels), bf16),
            shaped((cells, channels), bf16),
            shaped((2, 8, wide), f32),
        ),
        in_specs=[vmem] * 10,
        out_specs=(vmem,) * 9,
        scratch_shapes=[
            pltpu.VMEM((2, CELLS, channels), bf16),
            pltpu.VMEM((2, 8, channels), f32),
            pltpu.VMEM((2, CELLS, channels), bf16),
            pltpu.VMEM((2, 3, 8, channels), f32),
            pltpu.VMEM((4 * CELLS, channels), bf16),
            pltpu.VMEM((cells, channels), f32),
            pltpu.VMEM((cells, 4 * channels), bf16),
            pltpu.VMEM((cells, channels), bf16),
            pltpu.SemaphoreType.DMA((8,)),
            pltpu.SemaphoreType.DMA((8,)),
        ],
        compiler_params=pltpu.CompilerParams(
            vmem_limit_bytes=40 * 1024 * 1024, collective_id=3, has_side_effects=True
        ),
        name="forward",
    )(state, cotangent, bias, first_gain, expand, depth, shrink, second_gain, weight_in, weight_out)


def attend_kernel(
    valid,
    scale,
    items_ref,
    slope_ref,
    slope_edges,
    near_ref,
    last_ref,
    slope_rows,
    slope_sides,
    x_ref,
    near_send,
    last_send,
    xt_ref,
    kaug_ref,
    vaug_ref,
    t_ref,
    pb_ref,
    acc_ref,
    cell_ref,
    in_send,
    in_recv,
    near_send_sem,
    near_recv_sem,
    last_send_sem,
    last_recv_sem,
    halo_sends,
    halo_recvs,
):
    sources = items_ref.shape[0]
    total = sources * CELLS
    block = t_ref.shape[1]
    group = block // CELLS
    log2e = 1.4426950408889634
    to_log2 = scale * log2e
    f32, bf16 = jnp.float32, jnp.bfloat16
    lat, lon = lax.axis_index("lat"), lax.axis_index("lon")
    z, low = lon // 4, lon % 4

    def partner(k, sign):
        ring, side = k // 4, 3 - k % 4
        half = (ring + 1) // 2
        shift = 4 + (1 - 2 * (ring % 2)) * half
        x_lo, core = low // 2, low % 2
        x_lo = x_lo + (side // 2) * (1 - 2 * x_lo)
        core = core + (side % 2) * (1 - 2 * core)
        return ((z + sign * shift + 8) % 8) * 4 + x_lo * 2 + core

    barrier = pltpu.get_barrier_semaphore()

    def greet(k, carry):
        pl.semaphore_signal(
            barrier, inc=1, device_id=(lat, partner(k, 1)), device_id_type=MESH
        )
        return carry

    lax.fori_loop(0, sources - 1, greet, 0)
    greetings = halo_greet(barrier)
    pl.semaphore_wait(barrier, greetings + sources - 1)

    def incoming(k, slot):
        to = partner(k, 1)
        return pltpu.make_async_remote_copy(
            src_ref=items_ref.at[to],
            dst_ref=x_ref.at[slot],
            send_sem=in_send.at[k],
            recv_sem=in_recv.at[k],
            device_id=(lat, to),
            device_id_type=MESH,
        )

    def push(k, carry):
        incoming(k, lon).start()
        return carry

    lax.fori_loop(0, sources - 1, push, 0)
    halo = halo_copies(slope_ref, slope_edges, slope_rows, slope_sides, halo_sends, halo_recvs)
    halo_start(halo)
    x_ref[lon] = items_ref[lon]

    def prepare(index):
        raw = x_ref[index].astype(f32)
        row = lax.broadcasted_iota(jnp.int32, (CELLS, 128), 0)
        lane = lax.broadcasted_iota(jnp.int32, (CELLS, 128), 1)
        bias_row = jnp.broadcast_to(raw[valid : valid + 1, :], (CELLS, 128))
        bias = jnp.sum(jnp.where(row == lane, bias_row, 0.0), axis=1, keepdims=True) * log2e
        bias = jnp.broadcast_to(bias, (CELLS, 128))
        first = bias.astype(bf16).astype(f32)
        second = (bias - first).astype(bf16).astype(f32)
        third = bias - first - second
        first = jnp.where(row < valid, first, -1e30)
        second = jnp.where(row < valid, second, 0.0)
        third = jnp.where(row < valid, third, 0.0)
        cell = jnp.where(row < valid, raw, 0.0)
        key = jnp.where((lane >= 32) & (lane < 64), cell, 0.0)
        value = jnp.where((lane >= 64) & (lane < 96), cell, 0.0)
        keys = pltpu.roll(key, 96, 1) + key + pltpu.roll(key, 32, 1)
        keys = jnp.where(lane == 96, first, keys)
        keys = jnp.where(lane == 97, second, keys)
        keys = jnp.where(lane == 98, third, keys)
        values = pltpu.roll(value, 64, 1) + pltpu.roll(value, 96, 1)
        values = jnp.where((lane >= 64) & (lane < 67), 1.0, values)
        start = pl.multiple_of(index * CELLS, 32)
        kaug_ref[pl.ds(start, CELLS), :] = keys.astype(bf16)
        vaug_ref[pl.ds(start, CELLS), :] = values.astype(bf16)
        cell_ref[pl.ds(start, CELLS), :] = cell

    prepare(lon)

    def arrive(k, carry):
        source = partner(k, -1)
        incoming(k, source).wait_recv()
        prepare(source)
        return carry

    lax.fori_loop(0, sources - 1, arrive, 0)

    def turn(index, carry):
        start = pl.multiple_of(index * block, block)
        xt_ref[:, pl.ds(start, block)] = cell_ref[pl.ds(start, block), :].T.astype(bf16)
        acc_ref[:, pl.ds(start, block)] = jnp.zeros((64, block), f32)
        return carry

    lax.fori_loop(0, total // block, turn, 0)

    def packed(cells):
        return (cells[:48] + pltpu.roll(cells[48:], 64, 1)).astype(bf16)

    def nearby(source, slot):
        return pltpu.make_async_remote_copy(
            src_ref=near_send.at[source],
            dst_ref=near_ref.at[slot],
            send_sem=near_send_sem.at[source],
            recv_sem=near_recv_sem.at[slot],
            device_id=(lat, source),
            device_id_type=MESH,
        )

    def one_block(turn_index, carry):
        index = (turn_index + lon // group) % (sources // group)
        start = pl.multiple_of(index * block, block)
        xt = xt_ref[:, pl.ds(start, block)].astype(f32)
        query = xt[0:32] * to_log2
        first = query.astype(bf16).astype(f32)
        second = (query - first).astype(bf16).astype(f32)
        third = query - first - second
        qaug = jnp.concatenate(
            [first, second, third, jnp.ones((32, block), f32)], axis=0
        ).astype(bf16)
        t = jnp.dot(kaug_ref[...], qaug, preferred_element_type=f32)
        t_ref[...] = t
        highest = jnp.max(jnp.max(t.reshape(total // 8, 8, block), axis=0), axis=0, keepdims=True)
        p = jnp.exp2(t_ref[...] - highest)
        t_ref[...] = p
        low_p = p.astype(bf16)
        pb_ref[...] = low_p
        norm = jnp.sum(p.reshape(total // 8, 8, block), axis=0)
        heads = jnp.dot(xt_ref[64:96, :], low_p, preferred_element_type=f32)
        inverse = 1.0 / jnp.sum(norm, axis=0, keepdims=True)
        heads = heads * inverse
        back = xt[96:128]
        centred = jnp.sum(back * heads, axis=0, keepdims=True) * inverse
        back = back * inverse
        back_first = back.astype(bf16).astype(f32)
        back_second = back - back_first
        cen_first = centred.astype(bf16).astype(f32)
        cen_second = (centred - cen_first).astype(bf16).astype(f32)
        cen_third = centred - cen_first - cen_second
        sub = lax.broadcasted_iota(jnp.int32, (64, block), 0)
        cen = jnp.where(
            sub == 0,
            cen_first,
            jnp.where(sub == 1, cen_second, jnp.where(sub == 2, cen_third, 0.0)),
        )
        baug = jnp.concatenate([back_first, back_second, -cen], axis=0).astype(bf16)
        nt = (((1,), (1,)), ((), ()))
        dp = jnp.dot(vaug_ref[...], baug, preferred_element_type=f32)
        ds = (t_ref[...] * dp).astype(bf16)
        acc_ref[32:64, :] += lax.dot_general(
            back_first.astype(bf16), pb_ref[...], nt, preferred_element_type=f32
        )
        acc_ref[0:32, :] += lax.dot_general(
            xt_ref[0:32, pl.ds(start, block)], ds, nt, preferred_element_type=f32
        )
        back_queries = jnp.dot(xt_ref[32:64, :], ds, preferred_element_type=f32)
        zeros = jnp.zeros((64, block), f32)
        done = jnp.concatenate([back_queries * scale, heads, zeros], axis=0).T
        for part in range(group):
            source = index * group + part
            near_send[source] = packed(done[part * CELLS : part * CELLS + CELLS])

            @pl.when(source != lon)
            def _():
                nearby(source, lon).start()

        return carry

    lax.fori_loop(0, total // block, one_block, 0)
    near_ref[lon] = near_send[lon]

    def finish(index, carry):
        start = pl.multiple_of(index * block, block)
        both = acc_ref[:, pl.ds(start, block)]
        zeros = jnp.zeros((64, block), f32)
        both = jnp.concatenate([both[0:32] * scale, both[32:64], zeros], axis=0)
        cell_ref[pl.ds(start, block), :] = both.T
        return carry

    lax.fori_loop(0, total // block, finish, 0)

    def final(k, to, slot):
        return pltpu.make_async_remote_copy(
            src_ref=last_send.at[to],
            dst_ref=last_ref.at[slot],
            send_sem=last_send_sem.at[k],
            recv_sem=last_recv_sem.at[k],
            device_id=(lat, to),
            device_id_type=MESH,
        )

    def pack_last(source):
        start = pl.multiple_of(source * CELLS, 32)
        last_send[source] = packed(cell_ref[pl.ds(start, CELLS), :])

    def leave(k, carry):
        to = partner(k, 1)
        pack_last(to)
        final(k, to, lon).start()
        return carry

    lax.fori_loop(0, sources - 1, leave, 0)
    pack_last(lon)
    last_ref[lon] = last_send[lon]

    def settle(k, carry):
        to, source = partner(k, 1), partner(k, -1)
        incoming(k, lon).wait_send()
        nearby(to, lon).wait_send()
        nearby(source, source).wait_recv()
        made = final(k, to, source)
        made.wait_send()
        made.wait_recv()
        return carry

    lax.fori_loop(0, sources - 1, settle, 0)
    halo_arrive(halo)
    halo_leave(halo)


def attend_items(items, slope, slope_edges, valid, scale):
    sources = items.shape[0]
    total = sources * CELLS
    block = 768
    f32, bf16 = jnp.float32, jnp.bfloat16
    vmem = pl.BlockSpec(memory_space=pltpu.VMEM)
    answer = jax.ShapeDtypeStruct((sources, 48, 128), bf16)
    return pl.pallas_call(
        functools.partial(attend_kernel, valid, scale),
        out_shape=(
            answer,
            answer,
            jax.ShapeDtypeStruct(slope.shape, bf16),
            jax.ShapeDtypeStruct((2, 3, 8, slope.shape[2]), f32),
        ),
        in_specs=[vmem] * 3,
        out_specs=(vmem,) * 4,
        scratch_shapes=[
            pltpu.VMEM((sources, CELLS, 128), bf16),
            pltpu.VMEM((sources, 48, 128), bf16),
            pltpu.VMEM((sources, 48, 128), bf16),
            pltpu.VMEM((128, total), bf16),
            pltpu.VMEM((total, 128), bf16),
            pltpu.VMEM((total, 128), bf16),
            pltpu.VMEM((total, block), f32),
            pltpu.VMEM((total, block), bf16),
            pltpu.VMEM((64, total), f32),
            pltpu.VMEM((total, 128), f32),
        ]
        + [pltpu.SemaphoreType.DMA((sources,))] * 6
        + [pltpu.SemaphoreType.DMA((8,))] * 2,
        compiler_params=pltpu.CompilerParams(
            vmem_limit_bytes=48 * 1024 * 1024, collective_id=2, has_side_effects=True
        ),
        name="attend",
    )(items, slope, slope_edges)


def backward_kernel(
    factor,
    near_ref,
    last_ref,
    cot_ref,
    state_ref,
    first_gain,
    expand_ref,
    depth_ref,
    shrink_ref,
    second_gain,
    in_ref,
    weight_out_ref,
    act_ref,
    slope_ref,
    slope_expanded_ref,
    mixed_ref,
    normed_ref,
    inner_ref,
    second_ref,
    slope_rows,
    slope_sides,
    field_ref,
    grad_ref,
    block_ref,
    sums_ref,
    ga,
    gb,
    ra0,
    rb0,
    ra1,
    rb1,
    a1,
    b1,
    ra2,
    rb2,
    ab2,
    rz,
    small,
    s0,
    small0,
    smallz,
    smally,
    smallx,
    cot_pad,
    heads_ref,
    project_ref,
    rows,
    edges,
    row_slots,
    edge_slots,
    wide_back,
    back_normed,
    halo_sends,
    halo_recvs,
    core_sends,
    core_recvs,
    send_sems,
    recv_sems,
):
    f32, bf16 = jnp.float32, jnp.bfloat16
    valid = state_ref.shape[1]
    lat, lon = lax.axis_index("lat"), lax.axis_index("lon")
    x_hi, y = lat // 4, lat % 4
    z, x_lo, core = lon // 4, (lon // 2) % 2, lon % 2
    x = x_hi * 2 + x_lo

    def place(px, py, pz, pc):
        return ((px // 2) * 4 + py, pz * 4 + (px % 2) * 2 + pc)

    other = 1 - core
    sibling = place(x, y, z, other)
    x_peers = [place((x + d) % 4, y, z, core) for d in range(1, 4)]
    y_peers = [place(x, (y + d) % 4, z, core) for d in range(1, 4)]
    z_peers = [place(x, y, (z + d) % 8, core) for d in range(1, 8)]
    barrier = pltpu.get_barrier_semaphore()
    greetings = halo_greet(barrier)
    peers = [sibling] + x_peers + y_peers + z_peers
    for peer in peers:
        pl.semaphore_signal(barrier, inc=1, device_id=peer, device_id_type=MESH)

    cot_pad[...] = jnp.zeros(cot_pad.shape, bf16)
    small[...] = jnp.zeros(small.shape, f32)
    for i in range(2):
        cot_pad[i * CELLS : i * CELLS + valid, :] = cot_ref[i]

    half_lane = lax.broadcasted_iota(jnp.int32, (48, 128), 1)

    def gather(parts, first, second, i, tile):
        cells = slice(tile * 128, tile * 128 + 128)
        for target, column, source in ((first[0], first[1], 0), (second[0], second[1], 32)):
            for half in range(2):
                value = None
                for u in range(4):
                    shift = (u * 32 - source - half * 64) % 128
                    moved = pltpu.roll(parts[u], shift, 1) if shift else parts[u]
                    value = moved if value is None else jnp.where(half_lane < u * 32, value, moved)
                start = i * CELLS + half * 48
                target[start : start + 48, column + cells.start : column + cells.stop] = value.astype(bf16)

    for i in range(2):
        for tile in range(4):
            items = [i * 16 + tile * 4 + u for u in range(4)]
            gather(
                [near_ref[item].astype(f32) for item in items],
                (project_ref, 0),
                (heads_ref, 0),
                i,
                tile,
            )
            gather(
                [last_ref[item].astype(f32) for item in items],
                (project_ref, 512),
                (project_ref, 1024),
                i,
                tile,
            )

    back_second = nt_dot(project_ref[...], in_ref[...])
    field = jnp.dot(heads_ref[...], weight_out_ref[...], preferred_element_type=f32)
    gain_two = jnp.zeros((1, field.shape[1]), f32)
    for i in range(2):
        part = slice(i * CELLS, i * CELLS + CELLS)
        inner = inner_ref[part, :].astype(f32)
        field_ref[i] = (inner + field[part]).astype(bf16)[0:valid]
        inverse = inverse_rms(inner)
        gain_two = gain_two + jnp.sum(back_second[part] * inner * inverse, axis=0, keepdims=True)
        scaled = back_second[part] * second_gain[...]
        back = (
            cot_pad[part, :].astype(f32)
            + inverse * scaled
            - inverse * inverse * inverse * inner * jnp.mean(scaled * inner, axis=-1, keepdims=True)
        )
        rows[i] = back.astype(bf16)
    west, east = edge_pair(rows[0].astype(f32), rows[1].astype(f32), valid - 1)
    edges[0] = west
    edges[1] = east
    pl.semaphore_wait(barrier, greetings + len(peers))
    halo = halo_copies(rows, edges, row_slots, edge_slots, halo_sends, halo_recvs)
    halo_start(halo)

    def half_lanes(top, bottom):
        lane = lax.broadcasted_iota(jnp.int32, top.shape, 1)
        even = jnp.where(lane < 64, top, pltpu.roll(bottom, 64, 1))
        odd = jnp.where(lane < 64, pltpu.roll(top, 64, 1), bottom)
        return even, odd

    def cross(left, right):
        return (
            lax.dot_general(left, right, (((0,), (0,)), ((), ())), preferred_element_type=f32)
            * factor
        )

    def core_copy(source, target, index):
        return pltpu.make_async_remote_copy(
            src_ref=source,
            dst_ref=target,
            send_sem=core_sends.at[index],
            recv_sem=core_recvs.at[index],
            device_id=sibling,
            device_id_type=MESH,
        )

    def core_a(pz):
        return core_copy(ga.at[other, pz], ra0.at[pz], pz)

    def core_b(zz):
        return core_copy(gb.at[other, pl.ds(zz * 2, 2)], rb0.at[pl.ds(zz * 2, 2)], 8 + zz)

    def other_part(zz, carry):
        columns = pl.ds(pl.multiple_of(zz * 128, 128), 128)
        own = jnp.concatenate([rows[0, :, columns], rows[1, :, columns]], axis=0)
        shrink = cross(own, mixed_ref[...])
        grad_in = cross(
            project_ref[:, pl.ds(pl.multiple_of(zz * 384, 128), 384)], second_ref[...]
        )
        grad_out = cross(cot_pad[:, columns], heads_ref[...])
        for sub in range(8):
            pz, plo, pc = zz * 2 + sub // 4, (sub // 2) % 2, sub % 2
            for plat in range(8):
                px, py = (plat // 4) * 2 + plo, plat % 4
                part = slice(sub * 16, sub * 16 + 16)
                ga[pc, pz, px, py, 32:48, :] = shrink[
                    part, plat * 256 : plat * 256 + 128
                ].astype(bf16)
                gb[pc, pz, py, px, 0:16, :] = shrink[
                    part, plat * 256 + 128 : plat * 256 + 256
                ].astype(bf16)
            for pair in range(4):
                tile = slice(pair * 128, pair * 128 + 128)
                top = jnp.concatenate(
                    [grad_in[sub * 48 : sub * 48 + 24, tile], grad_out[sub * 16 : sub * 16 + 8, tile]],
                    axis=0,
                )
                bottom = jnp.concatenate(
                    [
                        grad_in[sub * 48 + 24 : sub * 48 + 48, tile],
                        grad_out[sub * 16 + 8 : sub * 16 + 16, tile],
                    ],
                    axis=0,
                )
                parts = half_lanes(top, bottom)
                for odd in range(2):
                    plat = pair * 2 + odd
                    px, py = (plat // 4) * 2 + plo, plat % 4
                    gb[pc, pz, py, px, 16:48, :] = parts[odd].astype(bf16)
        core_b(zz).start()
        return carry

    lax.fori_loop(0, 4, other_part, 0)
    halo_arrive(halo)
    for r in range(4):
        base = rows[r - 1] if r in (1, 2) else row_slots[r // 3]
        value = halo_row(r, base.astype(f32), edge_slots, valid)
        wide_back[r * CELLS : r * CELLS + CELLS, :] = value.astype(bf16)
    back_normed[...] = jnp.zeros(back_normed.shape, f32)

    def chunk(pz, carry):
        start = pl.multiple_of(pz * CHUNK, CHUNK)
        lanes = pl.ds(start, CHUNK)
        product = nt_dot(wide_back[...], shrink_ref[lanes, :])
        planes = []
        for r in range(4):
            base = slope_ref[r - 1, :, lanes] if r in (1, 2) else slope_rows[r // 3, :, lanes]
            slope = halo_row(r, base.astype(f32), slope_sides, valid, lanes)
            plane = product[r * CELLS : r * CELLS + CELLS] * slope
            planes.append(plane.astype(bf16).astype(f32))
        grads = []
        for b in range(3):
            turned = []
            for i in range(2):
                centre = planes[i + 1]
                centre = jnp.where(inside(centre.shape, valid), centre, 0.0)
                turned.append(pltpu.roll(centre, (CELLS + b - 1) % CELLS, 0) if b != 1 else centre)
            for a in range(3):
                value = act_ref[a, :, lanes].astype(f32) * turned[0]
                value = value + act_ref[a + 1, :, lanes].astype(f32) * turned[1]
                small[a * 3 + b : a * 3 + b + 1, lanes] = (
                    jnp.sum(value, axis=0, keepdims=True) * factor
                )
        outs = []
        for i in range(2):
            sums = []
            for b in range(3):
                part = depth_ref[b : b + 1, lanes] * planes[i + 2]
                for a in (1, 2):
                    part = part + depth_ref[a * 3 + b : a * 3 + b + 1, lanes] * planes[i + 2 - a]
                sums.append(part)
            total = pltpu.roll(sums[0], CELLS - 1, 0) + sums[1] + pltpu.roll(sums[2], 1, 0)
            total = total * slope_expanded_ref[i * CELLS : i * CELLS + CELLS, lanes].astype(f32)
            outs.append(jnp.where(inside(total.shape, valid), total, 0.0).astype(bf16))
        back = jnp.concatenate(outs, axis=0)
        back_normed[...] += nt_dot(back, expand_ref[:, lanes])
        grad = cross(back, normed_ref[...])
        for sub in range(4):
            plo, pc = sub // 2, sub % 2
            for pair in range(4):
                tile = slice(pair * 128, pair * 128 + 128)
                parts = half_lanes(
                    grad[sub * 64 : sub * 64 + 32, tile], grad[sub * 64 + 32 : sub * 64 + 64, tile]
                )
                for odd in range(2):
                    plat = pair * 2 + odd
                    px, py = (plat // 4) * 2 + plo, plat % 4
                    ga[pc, pz, px, py, 0:32, :] = parts[odd].astype(bf16)
        core_a(pz).start()
        return carry

    count = [0]

    def copy(source, target, peer):
        index = count[0]
        count[0] += 1
        made = pltpu.make_async_remote_copy(
            src_ref=source,
            dst_ref=target,
            send_sem=send_sems.at[index],
            recv_sem=recv_sems.at[index],
            device_id=peer,
            device_id_type=MESH,
        )
        made.start()
        return made

    def add_pair(mine, theirs, pz):
        for q in range(4):
            mine[core, pz, q] = (mine[core, pz, q].astype(f32) + theirs[pz, q].astype(f32)).astype(bf16)

    def arrive_b(zz, carry):
        core_b(zz).wait_recv()
        add_pair(gb, rb0, zz * 2)
        add_pair(gb, rb0, zz * 2 + 1)
        return carry

    def arrive_a(pz, carry):
        core_a(pz).wait_recv()
        add_pair(ga, ra0, pz)
        return carry

    lax.fori_loop(0, 4, chunk, 0)
    lax.fori_loop(0, 4, arrive_b, 0)
    next_b = [
        copy(gb.at[core, :, (y + d) % 4], rb1.at[d - 1], y_peers[d - 1]) for d in (1, 2, 3)
    ]
    lax.fori_loop(4, 8, chunk, 0)
    lax.fori_loop(0, 8, arrive_a, 0)
    next_a = [
        copy(ga.at[core, :, (x + d) % 4], ra1.at[d - 1], x_peers[d - 1]) for d in (1, 2, 3)
    ]

    gain_one = jnp.zeros((1, back_normed.shape[1]), f32)
    for i in range(2):
        part = slice(i * CELLS, i * CELLS + valid)
        state = state_ref[i].astype(f32)
        inverse = inverse_rms(state)
        back = back_normed[part, :]
        gain_one = gain_one + jnp.sum(back * state * inverse, axis=0, keepdims=True)
        scaled = back * first_gain[...]
        grad_ref[i] = (
            rows[i, 0:valid, :].astype(f32)
            + inverse * scaled
            - inverse * inverse * inverse * state * jnp.mean(scaled * state, axis=-1, keepdims=True)
        ).astype(bf16)
    width = small.shape[1]
    small[9:10, :] = jnp.concatenate(
        [gain_one * factor, gain_two * factor, jnp.zeros((1, width - 1024), f32)], axis=1
    )
    half = width // 2
    small_lanes = pl.ds(pl.multiple_of(other * half, half), half)
    s0[...] = small[0:16, small_lanes]
    small_core = copy(s0, small0, sibling)
    small_core.wait_recv()
    total = small[0:16, pl.ds(pl.multiple_of(core * half, half), half)] + small0[...]
    smallz[z] = total
    small_z = [copy(smallz.at[z], smallz.at[z], peer) for peer in z_peers]

    def add_four(mine, theirs, total):
        def body(pz, carry):
            value = mine(pz).astype(f32)
            for d in range(3):
                value = value + theirs[d, pz].astype(f32)
            total[pz] = value.astype(bf16)
            return carry

        lax.fori_loop(0, 8, body, 0)

    for made in next_b:
        made.wait_recv()
    add_four(lambda pz: gb[core, pz, y], rb1, b1)
    last_b = [copy(b1.at[:, (x + d) % 4], rb2.at[d - 1], x_peers[d - 1]) for d in (1, 2, 3)]
    for made in next_a:
        made.wait_recv()
    add_four(lambda pz: ga[core, pz, x], ra1, a1)
    last_a = [copy(a1.at[:, (y + d) % 4], ra2.at[d - 1], y_peers[d - 1]) for d in (1, 2, 3)]

    for made in small_z:
        made.wait_recv()
    total = smallz[0]
    for index in range(1, 8):
        total = total + smallz[index]
    smally[y] = total
    small_y = [copy(smally.at[y], smally.at[y], peer) for peer in y_peers]

    def finish_pair(mine, theirs, first_row):
        def body(pz, carry):
            value = mine(pz).astype(f32)
            for d in range(3):
                value = value + theirs[d, pz].astype(f32)
            ab2[pz, first_row : first_row + 48, :] = value.astype(bf16)
            return carry

        lax.fori_loop(0, 8, body, 0)

    for made in last_b:
        made.wait_recv()
    finish_pair(lambda pz: b1[pz, x], rb2, 48)
    for made in last_a:
        made.wait_recv()
    finish_pair(lambda pz: a1[pz, y], ra2, 0)
    last = [copy(ab2.at[(z + d) % 8], rz.at[d - 1], z_peers[d - 1]) for d in range(1, 8)]

    for made in small_y:
        made.wait_recv()
    total = (smally[0] + smally[1]) + (smally[2] + smally[3])
    smallx[x] = total
    small_x = [copy(smallx.at[x], smallx.at[x], peer) for peer in x_peers]

    for made in last:
        made.wait_recv()
    value = ab2[z].astype(f32)
    for d in range(7):
        value = value + rz[d].astype(f32)
    block_ref[...] = value

    for made in small_x:
        made.wait_recv()
    sums_ref[core] = (smallx[0] + smallx[1]) + (smallx[2] + smallx[3])
    final = copy(sums_ref.at[core], sums_ref.at[core], sibling)
    final.wait_recv()
    for made in [small_core, final] + next_a + next_b + last_a + last_b + last + small_z + small_y + small_x:
        made.wait_send()
    halo_leave(halo)

    def leave_a(pz, carry):
        core_a(pz).wait_send()
        return carry

    def leave_b(zz, carry):
        core_b(zz).wait_send()
        return carry

    lax.fori_loop(0, 8, leave_a, 0)
    lax.fori_loop(0, 4, leave_b, 0)


def backward_pass(factor, *operands):
    f32, bf16 = jnp.float32, jnp.bfloat16
    vmem = pl.BlockSpec(memory_space=pltpu.VMEM)
    state = operands[3]
    channels, wide = operands[5].shape
    cells = 2 * CELLS
    half = wide // 2
    copies = 1 + 1 + 12 + 7 + 7 + 3 + 3
    shaped = jax.ShapeDtypeStruct
    return pl.pallas_call(
        functools.partial(backward_kernel, factor),
        out_shape=(
            shaped(state.shape, bf16),
            shaped(state.shape, bf16),
            shaped((96, 128), f32),
            shaped((2, 16, half), f32),
        ),
        in_specs=[vmem] * len(operands),
        out_specs=(vmem,) * 4,
        scratch_shapes=[
            pltpu.VMEM((2, 8, 4, 4, 48, 128), bf16),
            pltpu.VMEM((2, 8, 4, 4, 48, 128), bf16),
            pltpu.VMEM((8, 4, 4, 48, 128), bf16),
            pltpu.VMEM((8, 4, 4, 48, 128), bf16),
            pltpu.VMEM((3, 8, 4, 48, 128), bf16),
            pltpu.VMEM((3, 8, 4, 48, 128), bf16),
            pltpu.VMEM((8, 4, 48, 128), bf16),
            pltpu.VMEM((8, 4, 48, 128), bf16),
            pltpu.VMEM((3, 8, 48, 128), bf16),
            pltpu.VMEM((3, 8, 48, 128), bf16),
            pltpu.VMEM((8, 96, 128), bf16),
            pltpu.VMEM((7, 96, 128), bf16),
            pltpu.VMEM((16, wide), f32),
            pltpu.VMEM((16, half), f32),
            pltpu.VMEM((16, half), f32),
            pltpu.VMEM((8, 16, half), f32),
            pltpu.VMEM((4, 16, half), f32),
            pltpu.VMEM((4, 16, half), f32),
            pltpu.VMEM((cells, channels), bf16),
            pltpu.VMEM((cells, channels), bf16),
            pltpu.VMEM((cells, 3 * channels), bf16),
            pltpu.VMEM((2, CELLS, channels), bf16),
            pltpu.VMEM((2, 8, channels), f32),
            pltpu.VMEM((2, CELLS, channels), bf16),
            pltpu.VMEM((2, 3, 8, channels), f32),
            pltpu.VMEM((4 * CELLS, channels), bf16),
            pltpu.VMEM((cells, channels), f32),
            pltpu.SemaphoreType.DMA((8,)),
            pltpu.SemaphoreType.DMA((8,)),
            pltpu.SemaphoreType.DMA((12,)),
            pltpu.SemaphoreType.DMA((12,)),
            pltpu.SemaphoreType.DMA((copies,)),
            pltpu.SemaphoreType.DMA((copies,)),
        ],
        compiler_params=pltpu.CompilerParams(
            vmem_limit_bytes=52 * 1024 * 1024, collective_id=4, has_side_effects=True
        ),
        name="backward",
    )(*operands)


def owner_blocks(block):
    def unfold(part):
        return jnp.concatenate([part[:, :64], part[:, 64:]], axis=0).T

    expand = unfold(block[0:32])
    shrink = jnp.concatenate([block[32:48], block[48:64]], axis=1).T
    grad_in = unfold(block[64:88])
    grad_out = unfold(block[88:96])
    return expand, shrink, grad_in, grad_out


def per_device(
    state_field,
    cotangent,
    key_bias,
    input_gain,
    expand_weight,
    depth_weight,
    shrink_weight,
    attention_gain,
    attention_in,
    attention_out,
):
    row_count, lon_count, channels = state_field.shape
    head_count = key_bias.shape[2]
    wide_count = expand_weight.shape[1]
    norm_factor = 1.0 / math.sqrt(
        row_count * lon_count * lax.axis_size("lat") * lax.axis_size("lon")
    )
    score_scale = 1.0 / math.sqrt(channels // head_count)
    bias = key_bias.astype(jnp.float32).transpose(0, 2, 1)
    bias = bias.reshape(row_count * head_count, lon_count)
    bias = jnp.pad(bias, ((0, 0), (0, 128 - lon_count)))
    depth = depth_weight.astype(jnp.float32).reshape(9, wide_count)
    first_gain = input_gain.reshape(1, channels)
    second_gain = attention_gain.reshape(1, channels)
    items, act, slope, slope_expanded, mixed, normed, inner, second, slope_edges = forward_pass(
        state_field,
        cotangent,
        bias,
        first_gain,
        expand_weight,
        depth,
        shrink_weight,
        second_gain,
        attention_in,
        attention_out,
    )
    near, last, slope_rows, slope_sides = attend_items(
        items, slope, slope_edges, lon_count, score_scale
    )
    output_field, input_grad, block, sums = backward_pass(
        norm_factor,
        near,
        last,
        cotangent,
        state_field,
        first_gain,
        expand_weight,
        depth,
        shrink_weight,
        second_gain,
        attention_in,
        attention_out,
        act,
        slope,
        slope_expanded,
        mixed,
        normed,
        inner,
        second,
        slope_rows,
        slope_sides,
    )
    depth_grad = jnp.concatenate([sums[0, :9], sums[1, :9]], axis=1).reshape(3, 3, wide_count)
    gains = sums[0, 9]
    return (
        output_field,
        input_grad,
        *owner_blocks(block),
        depth_grad,
        gains[:channels],
        gains[channels : 2 * channels],
    )


def solution(mesh):
    placed = (
        P("lat", "lon", None),
        P("lat", "lon", None),
        P("lat", "lon", None),
        P(),
        P(),
        P(),
        P(),
        P(),
        P(),
        P(),
    )
    return jax.shard_map(
        per_device,
        mesh=mesh,
        in_specs=placed,
        out_specs=(
            P("lat", "lon", None),
            P("lat", "lon", None),
            P("lat", "lon"),
            P("lat", "lon"),
            P("lat", "lon"),
            P("lat", "lon"),
            P(),
            P(),
            P(),
        ),
        check_vma=False,
    )
```

time: 228 us -> 180 us (0.79)
  Pallas kernels: 137 us -> 156 us
  local copies, waits for them, and re-layouts: 34.6 us -> 19.1 us
  starting transfers between devices: 15.1 us -> 0 us
  matrix products: 13.9 us -> 0 us
  other arithmetic: 15.1 us -> 3.2 us
  waiting for transfers between devices: 9.64 us -> 0 us
    pallas_call x1 -> x2, Pallas kernels: 58.6 us -> 85.8 us  [the longest x1 65.6 us: backward_pass(): pl.pallas_call(functools.partial(backward_kernel, factor), out_shape=(sha...]
    ppermute x8 -> x0, starting transfers between devices: 15.1 us -> none  [the longest x4 8.54 us: with_halo(): lax.ppermute(lax.slice_in_dim(block, block.shape[dim] - width, None, axis...]
    dot_general x7 -> x0, matrix products: 13.9 us -> none  [the longest x3 6.67 us: times_transpose(): lax.dot_general(values, weights, (((values.ndim - 1,), (1,)), ((), ())),...]
    reshape x7 -> x1, local copies, waits for them, and re-layouts: 13.8 us -> 0.83 us  [per_device(): depth = depth_weight.astype(jnp.float32).reshape(9, wide_count)]
    ppermute x8 -> x0, waiting for transfers between devices: 9.64 us -> none  [the longest x4 5.51 us: with_halo(): lax.ppermute(lax.slice_in_dim(block, 0, width, axis=dim), axis, backward)]
    pallas_call x1, Pallas kernels: 78.8 us -> 70.5 us  [attend_items(): pl.pallas_call(functools.partial(attend_kernel, valid, scale), out_shape=...]
    unnamed x115 -> x37, local copies, waits for them, and re-layouts: 10.2 us -> 17.4 us
    convert_element_type x5 -> x0, other arithmetic: 6.36 us -> none  [the longest x1 3.24 us: per_device(): mixed = jax.nn.silu(convolved).astype(jnp.bfloat16)]
  transfers between devices with their start and end apart: 8 -> 0, of which waited for: 4 -> 0; matrix products, arithmetic and copies ran while one was open for 5% -> 0% of each run, Pallas kernels for 0% -> 0%
where the time goes in v3:
time: 180 us; the launch traced here: 179 us
  Pallas kernels  156 us (87%)
  local copies, waits for them, and re-layouts  19.1 us (11%)
  other arithmetic  3.2 us (2%)
    pallas_call x1, Pallas kernels, attend_items(): pl.pallas_call(functools.partial(attend_kernel, valid, scale), out_shape=...  70.5 us
    pallas_call x1, Pallas kernels, backward_pass(): pl.pallas_call(functools.partial(backward_kernel, factor), out_shape=(sha...  65.6 us
    pallas_call x1, Pallas kernels, forward_pass(): pl.pallas_call(forward_kernel, out_shape=(shaped((32, CELLS, 128), bf16),...  20.1 us
    unnamed x37, local copies, waits for them, and re-layouts  17.4 us

profile of v3, /device:TPU:1, one launch (start us, length us, event | category | flops | bytes accessed | tf_op | source)
XLA Modules:
  0.0 179.3 jit_solution(12793237569224823208)
XLA Ops:
  0.6 0.7 pad_convert_fusion.bias_ref
  1.3 0.8 reshape.46.depth_ref
  2.2 0.9 copy.26.state_ref
  3.1 0.9 copy.27.cot_ref
  4.1 1.6 copy-done
  5.7 1.6 copy-done.1
  7.3 1.4 copy-done.2
  8.7 1.0 copy-done.4
  9.7 0.7 copy-done.12
  10.4 0.7 copy-done.14
  11.1 20.1 %forward.1 = (bf16[32,96,128]{2,1,0:T(8,128)(2,1)S(1)}, bf16[4,96,2048]{2,1,0:T(8,128)(2,1)S(1)}, bf16[2,96,2048]{2,1,0:T(8,128)(2,1)S(1)}, bf16[192,2048]{1,0:T...) custom-call(bf16[2,90,512]{2,1,0:T(8,128)(2,1)S(1)} %copy.26.state_r, ...), custom_call_target="tpu_custom_call" | custom-call | tf_op jit(solution)/shard_map/forward/pallas_call | solution.py:284
  31.2 1.1 copy-done.5
  32.4 0.9 copy-done.6
  33.3 0.9 copy-done.7
  34.2 70.5 %attend.1 = (bf16[32,48,128]{2,1,0:T(8,128)(2,1)S(1)}, bf16[32,48,128]{2,1,0:T(8,128)(2,1)S(1)}, bf16[2,96,2048]{2,1,0:T(8,128)(2,1)S(1)}, f32[2,3,8,2048]{3,2,1,0:T(8,128)S(1)}) custom-call(bf16[32,96,128]{2,1,0:T(8,128)(2,1)S(1)} %get-tuple-element.26.items_ref, bf16[2,96,2048]{2,1,0:T(8,128)(2,1)S(1)} %get-tuple-element.27.slope_ref, ...), custom_call_target="tpu_custom_call" | custom-call | tf_op jit(solution)/shard_map/attend/pallas_call | solution.py:574
  104.7 0.9 copy-done.8
  105.5 0.8 copy-done.9
  106.3 0.8 copy-done.10
  107.1 0.8 copy-done.11
  107.9 65.6 %backward.1 = (bf16[2,90,512]{2,1,0:T(8,128)(2,1)S(1)}, bf16[2,90,512]{2,1,0:T(8,128)(2,1)S(1)}, f32[96,128]{1,0:T(8,128)S(1)}, f32[2,16,1024]{2,1,0:T(8,128)S(1)}) custom-call(bf16[32,48,128]{2,1,0:T(8,128)(2,1)} %copy-done.9, bf16[32,48,128]{2,1,0:T(8,128)(2,1)} %copy-done.10, bf16[2,90,512]{2,1,0:T(8,128)(2,1)S(1)} %copy.27.cot_ref, ...), custom_call_target="tpu_custom_call" | custom-call | tf_op jit(solution)/shard_map/backward/pallas_call | solution.py:1029
  173.5 0.9 copy.30
  176.4 0.7 copy.32
  177.8 0.7 pad_maximum_fusion
  178.4 0.9 copy.31
  (31 shorter events, 2.7 us)
Async XLA Ops:
  4.1 1.6 copy-start
  5.7 1.6 copy-start.1
  7.3 1.4 copy-start.2
  8.7 1.0 copy-start.4
  9.7 0.7 copy-start.12
  10.4 0.7 copy-start.14
  11.1 96.8 %copy-start.13 = (f32[512]{0:T(512)S(1)}, f32[512]{0:T(512)}, u32[]{:S(2)}) copy-start(f32[512]{0:T(512)} %param.13) | copy-start | bytes 6148
  11.1 96.8 %copy-start.15 = (f32[512]{0:T(512)S(1)}, f32[512]{0:T(512)}, u32[]{:S(2)}) copy-start(f32[512]{0:T(512)} %param.17) | copy-start | bytes 6148
  31.2 1.2 copy-start.5
  32.4 0.9 copy-start.6
  33.3 0.9 copy-start.7
  34.2 73.7 %copy-start.3 = (bf16[2,96,2048]{2,1,0:T(8,128)(2,1)}, bf16[2,96,2048]{2,1,0:T(8,128)(2,1)S(1)}, u32[]{:S(2)}) copy-start(bf16[2,96,2048]{2,1,0:T(8,128)(2,1)S(1)} %get-tuple-element.27.slope_ref) | copy-start | bytes 2359300
  104.6 0.9 copy-start.8
  105.5 0.8 copy-start.9
  106.3 0.8 copy-start.10
  107.1 0.8 copy-start.11

commit v4 on v0

v4 whole, which is shorter than its diff:
```python
import functools
import math

import jax
import jax.numpy as jnp
from jax import lax
from jax.experimental import pallas as pl
from jax.experimental.pallas import tpu as pltpu
from jax.sharding import PartitionSpec as P

EPSILON = 1e-06
CELLS = 96
MESH = pl.DeviceIdType.MESH
VMEM_MIB = 60


CHUNK = 256


def silu_parts(values):
    sigmoid = 1.0 / (1.0 + jnp.exp(-values))
    return values * sigmoid, sigmoid * (1.0 + values * (1.0 - sigmoid))


def halo_copies(rows, edges, row_slots, edge_slots, sends, recvs):
    lat, lon = lax.axis_index("lat"), lax.axis_index("lon")
    bands, sectors = lax.axis_size("lat"), lax.axis_size("lon")
    west, east = (lon + sectors - 1) % sectors, (lon + 1) % sectors

    def made(source, target, index, peer):
        return pltpu.make_async_remote_copy(
            src_ref=source,
            dst_ref=target,
            send_sem=sends.at[index],
            recv_sem=recvs.at[index],
            device_id=peer,
            device_id_type=MESH,
        )

    north, south = lat > 0, lat < bands - 1
    copies = [
        (north, south, made(rows.at[0], row_slots.at[1], 0, (lat - 1, lon))),
        (south, north, made(rows.at[1], row_slots.at[0], 1, (lat + 1, lon))),
    ]
    for side, column in ((0, west), (1, east)):
        for slot in range(3):
            step = 1 - slot
            sends_it = (None, south, north)[step]
            gets_it = (None, north, south)[step]
            copies.append(
                (
                    sends_it,
                    gets_it,
                    made(
                        edges.at[side],
                        edge_slots.at[side, slot],
                        2 + side * 3 + slot,
                        (lat + step, column),
                    ),
                )
            )
    return copies


def guarded(condition, action):
    if condition is None:
        action()
    else:
        pl.when(condition)(action)


def halo_start(copies):
    for sends_it, _, made in copies:
        guarded(sends_it, made.start)


def halo_arrive(copies):
    for _, gets_it, made in copies:
        guarded(gets_it, made.wait_recv)


def halo_leave(copies):
    for sends_it, _, made in copies:
        guarded(sends_it, made.wait_send)


def halo_greet(barrier):
    lat, lon = lax.axis_index("lat"), lax.axis_index("lon")
    bands, sectors = lax.axis_size("lat"), lax.axis_size("lon")
    west, east = (lon + sectors - 1) % sectors, (lon + 1) % sectors

    def signal(row, column):
        pl.semaphore_signal(barrier, inc=1, device_id=(row, column), device_id_type=MESH)

    signal(lat, west)
    signal(lat, east)

    @pl.when(lat > 0)
    def _():
        for column in (west, lon, east):
            signal(lat - 1, column)

    @pl.when(lat < bands - 1)
    def _():
        for column in (west, lon, east):
            signal(lat + 1, column)

    north, south = (lat + bands - 1) // bands, (2 * bands - 2 - lat) // bands
    return 2 + 3 * north + 3 * south


def edge_pair(top, bottom, last):
    sub = lax.broadcasted_iota(jnp.int32, (8, top.shape[1]), 0)
    west = jnp.where(sub == 0, top[0:1], bottom[0:1])
    east = jnp.where(sub == 0, top[last : last + 1], bottom[last : last + 1])
    return west, east


def halo_row(index, base, edge_slots, valid, lanes=slice(None)):
    slot, row = ((0, 1), (1, 0), (1, 1), (2, 0))[index]
    place = lax.broadcasted_iota(jnp.int32, base.shape, 0)
    east = edge_slots[0, slot, row : row + 1, lanes]
    west = edge_slots[1, slot, row : row + 1, lanes]
    value = jnp.where(place == valid, east, jnp.where(place == CELLS - 1, west, base))
    lat, bands = lax.axis_index("lat"), lax.axis_size("lat")
    if index == 0:
        value = jnp.where(lat > 0, value, 0.0)
    if index == 3:
        value = jnp.where(lat < bands - 1, value, 0.0)
    return value


def inside(shape, valid):
    return lax.broadcasted_iota(jnp.int32, shape, 0) < valid


def inverse_rms(values):
    return lax.rsqrt(jnp.mean(values * values, axis=-1, keepdims=True) + EPSILON)


def nt_dot(left, right):
    return lax.dot_general(
        left, right, (((1,), (1,)), ((), ())), preferred_element_type=jnp.float32
    )


class Refs:
    def __init__(self, names, refs):
        for name, ref in zip(names, refs, strict=True):
            setattr(self, name, ref)


def exchange(source, target, sends, recvs, index, peer, landing=None):
    return pltpu.make_async_remote_copy(
        src_ref=source,
        dst_ref=target,
        send_sem=sends.at[index],
        recv_sem=recvs.at[index if landing is None else landing],
        device_id=peer,
        device_id_type=MESH,
    )


def partner(k, sign):
    lon = lax.axis_index("lon")
    z, low = lon // 4, lon % 4
    ring, side = k // 4, 3 - k % 4
    half = (ring + 1) // 2
    shift = 4 + (1 - 2 * (ring % 2)) * half
    x_lo, core = low // 2, low % 2
    x_lo = x_lo + (side // 2) * (1 - 2 * x_lo)
    core = core + (side % 2) * (1 - 2 * core)
    return ((z + sign * shift + 8) % 8) * 4 + x_lo * 2 + core


def packed(cells):
    return (cells[:48] + pltpu.roll(cells[48:], 64, 1)).astype(jnp.bfloat16)


def unpacked(pair):
    lane = lax.broadcasted_iota(jnp.int32, (48, 128), 1)
    pair = pair.astype(jnp.float32)
    top = jnp.where(lane < 64, pair, 0.0)
    bottom = jnp.where(lane < 64, pltpu.roll(pair, 64, 1), 0.0)
    return jnp.concatenate([top, bottom], axis=0)


def forward_phase(r, load, valid, greetings):
    f32, bf16 = jnp.float32, jnp.bfloat16
    r.rows[...] = jnp.zeros(r.rows.shape, bf16)
    r.cot_pad[...] = jnp.zeros(r.cot_pad.shape, bf16)
    load["state"].wait()
    for i in range(2):
        r.rows[i, 0:valid, :] = r.state[i]
    west, east = edge_pair(r.rows[0].astype(f32), r.rows[1].astype(f32), valid - 1)
    r.edges[0] = west
    r.edges[1] = east
    pl.semaphore_wait(pltpu.get_barrier_semaphore(), greetings)
    copies = halo_copies(r.rows, r.edges, r.row_slots, r.edge_slots, r.state_sends, r.state_recvs)
    halo_start(copies)
    load["cot"].wait()
    load["out"].wait()
    for i in range(2):
        r.cot_pad[i * CELLS : i * CELLS + valid, :] = r.cot[i]
    r.projected[:, 1536:2048] = nt_dot(r.cot_pad[...], r.weight_out[...]).astype(bf16)
    r.total[...] = jnp.zeros(r.total.shape, f32)
    load["expand"].wait()
    load["shrink"].wait()
    halo_arrive(copies)
    for row in range(4):
        base = r.rows[row - 1] if row in (1, 2) else r.row_slots[row // 3]
        value = halo_row(row, base.astype(f32), r.edge_slots, valid)
        value = (value * inverse_rms(value) * r.first_gain[...]).astype(bf16)
        r.wide_normed[row * CELLS : row * CELLS + CELLS, :] = value
        if row in (1, 2):
            own = jnp.where(inside(value.shape, valid), value.astype(f32), 0.0).astype(bf16)
            r.normed[(row - 1) * CELLS : row * CELLS, :] = own

    def chunk(index, carry):
        start = pl.multiple_of(index * CHUNK, CHUNK)
        lanes = pl.ds(start, CHUNK)
        expanded = jnp.dot(r.wide_normed[...], r.expand[:, lanes], preferred_element_type=f32)
        activated, slope = silu_parts(expanded)
        activated = activated.astype(bf16)
        r.slope_expanded[:, lanes] = slope[CELLS : 3 * CELLS].astype(bf16)
        planes = []
        for row in range(4):
            plane = activated[row * CELLS : row * CELLS + CELLS]
            r.act[row, :, lanes] = plane
            planes.append(plane.astype(f32))
        mixes, slopes = [], []
        for i in range(2):
            sums = []
            for b in range(3):
                part = r.depth[b : b + 1, lanes] * planes[i]
                for a in (1, 2):
                    part = part + r.depth[a * 3 + b : a * 3 + b + 1, lanes] * planes[i + a]
                sums.append(part)
            convolved = pltpu.roll(sums[0], 1, 0) + sums[1] + pltpu.roll(sums[2], CELLS - 1, 0)
            mixed, slope = silu_parts(convolved)
            keep = inside(mixed.shape, valid)
            mixes.append(jnp.where(keep, mixed, 0.0).astype(bf16))
            slope = jnp.where(keep, slope, 0.0)
            r.slope[i, :, lanes] = slope.astype(bf16)
            slopes.append(slope)
        west, east = edge_pair(slopes[0], slopes[1], valid - 1)
        r.slope_edges[0, :, lanes] = west
        r.slope_edges[1, :, lanes] = east
        mixed = jnp.concatenate(mixes, axis=0)
        r.mixed[:, lanes] = mixed
        r.total[...] += jnp.dot(
            mixed, r.shrink[pl.ds(start, CHUNK), :], preferred_element_type=f32
        )
        return carry

    lax.fori_loop(0, r.expand.shape[1] // CHUNK, chunk, 0)
    for i in range(2):
        part = slice(i * CELLS, i * CELLS + CELLS)
        inner = (r.rows[i].astype(f32) + r.total[part, :]).astype(bf16)
        r.inner[part, :] = inner
        inner = inner.astype(f32)
        r.second[part, :] = (inner * inverse_rms(inner) * r.second_gain[...]).astype(bf16)
    load["in"].wait()
    return copies


def project_and_pack(r, valid, first, last, target, with_bias):
    f32, bf16 = jnp.float32, jnp.bfloat16
    lane = lax.broadcasted_iota(jnp.int32, (CELLS, 128), 1)
    row = lax.broadcasted_iota(jnp.int32, (CELLS, 128), 0)
    for i in range(2):
        cells = slice(i * CELLS, i * CELLS + CELLS)
        for tile in range(4):
            parts = [
                r.projected[cells, base + tile * 128 : base + tile * 128 + 128].astype(f32)
                for base in (first, last)
            ]
            for u in range(4):
                item = i * 16 + tile * 4 + u
                moved = [
                    value if side == u else pltpu.roll(value, ((side - u) * 32) % 128, 1)
                    for side, value in enumerate(parts)
                ]
                value = jnp.where(lane < 32, moved[0], jnp.where(lane < 64, moved[1], 0.0))
                if with_bias:
                    value = jnp.where(row == valid, r.bias[2 * item : 2 * item + 1, :], value)
                    value = jnp.where(row == valid + 1, r.bias[2 * item + 1 : 2 * item + 2, :], value)
                target[item] = packed(value)


def attention_phase(r, valid, scale):
    sources = r.kv_in.shape[0]
    total = sources * CELLS
    block = r.scores.shape[1]
    group = block // CELLS
    log2e = 1.4426950408889634
    to_log2 = scale * log2e
    f32, bf16 = jnp.float32, jnp.bfloat16
    lat, lon = lax.axis_index("lat"), lax.axis_index("lon")
    groups = sources // group

    def key_copy(k, to, slot):
        return exchange(
            r.kv_out.at[to], r.kv_in.at[slot], r.kv_sends, r.kv_recvs, k, (lat, to)
        )

    def query_copy(to, slot):
        return exchange(
            r.qd_out.at[to], r.qd_in.at[slot], r.qd_sends, r.qd_recvs, to, (lat, to), slot
        )

    def near_copy(to, slot):
        return exchange(
            r.near_out.at[to], r.near_in.at[slot], r.near_sends, r.near_recvs, to, (lat, to), slot
        )

    def last_copy(k, to, slot):
        return exchange(
            r.last_out.at[to], r.last_in.at[slot], r.last_sends, r.last_recvs, k, (lat, to)
        )

    r.projected[:, 512:1536] = jnp.dot(
        r.second[...], r.weight_in[:, 512:1536], preferred_element_type=f32
    ).astype(bf16)
    project_and_pack(r, valid, 512, 1024, r.kv_out, True)

    def push_keys(k, carry):
        key_copy(k, partner(k, 1), lon).start()
        return carry

    lax.fori_loop(0, sources - 1, push_keys, 0)
    r.projected[:, 0:512] = jnp.dot(
        r.second[...], r.weight_in[:, 0:512], preferred_element_type=f32
    ).astype(bf16)
    project_and_pack(r, valid, 0, 1536, r.qd_out, False)

    def push_queries(step, carry):
        to = ((lon // group + groups - step // group) % groups) * group + step % group

        @pl.when(to != lon)
        def _():
            query_copy(to, lon).start()

        return carry

    lax.fori_loop(0, sources, push_queries, 0)
    halo = halo_copies(
        r.slope, r.slope_edges, r.slope_rows, r.slope_sides, r.slope_sends, r.slope_recvs
    )
    halo_start(halo)
    r.kv_in[lon] = r.kv_out[lon]
    r.qd_in[lon] = r.qd_out[lon]

    def prepare(index):
        raw = unpacked(r.kv_in[index])
        row = lax.broadcasted_iota(jnp.int32, (CELLS, 128), 0)
        lane = lax.broadcasted_iota(jnp.int32, (CELLS, 128), 1)
        bias_row = jnp.where(row < 48, raw[valid : valid + 1, :], raw[valid + 1 : valid + 2, :])
        wanted = jnp.where(row < 48, row, row - 48)
        bias = jnp.sum(jnp.where(wanted == lane, bias_row, 0.0), axis=1, keepdims=True) * log2e
        bias = jnp.broadcast_to(bias, (CELLS, 128))
        first = bias.astype(bf16).astype(f32)
        second = (bias - first).astype(bf16).astype(f32)
        third = bias - first - second
        first = jnp.where(row < valid, first, -1e30)
        second = jnp.where(row < valid, second, 0.0)
        third = jnp.where(row < valid, third, 0.0)
        cell = jnp.where(row < valid, raw, 0.0)
        key = jnp.where(lane < 32, cell, 0.0)
        value = jnp.where(lane >= 32, cell, 0.0)
        keys = key + pltpu.roll(key, 32, 1) + pltpu.roll(key, 64, 1)
        keys = jnp.where(lane == 96, first, keys)
        keys = jnp.where(lane == 97, second, keys)
        keys = jnp.where(lane == 98, third, keys)
        values = value + pltpu.roll(value, 96, 1)
        values = jnp.where((lane >= 64) & (lane < 67), 1.0, values)
        start = pl.multiple_of(index * CELLS, 32)
        r.kaug[pl.ds(start, CELLS), :] = keys.astype(bf16)
        r.vaug[pl.ds(start, CELLS), :] = values.astype(bf16)
        r.cell[pl.ds(start, CELLS), :] = cell

    prepare(lon)

    def arrive(k, carry):
        source = partner(k, -1)
        key_copy(k, source, source).wait_recv()
        prepare(source)
        return carry

    lax.fori_loop(0, sources - 1, arrive, 0)

    def turn(index, carry):
        start = pl.multiple_of(index * block, block)
        r.xt[:, pl.ds(start, block)] = r.cell[pl.ds(start, block), :].T[0:64].astype(bf16)
        r.acc[:, pl.ds(start, block)] = jnp.zeros((64, block), f32)
        return carry

    lax.fori_loop(0, total // block, turn, 0)

    def one_block(turn_index, carry):
        index = (turn_index + lon // group) % groups
        for part in range(group):
            source = index * group + part

            @pl.when(source != lon)
            def _():
                query_copy(source, source).wait_recv()

            r.qd_cell[part * CELLS : part * CELLS + CELLS, :] = unpacked(r.qd_in[source])
        xt = r.qd_cell[...].T
        query = xt[0:32] * to_log2
        first = query.astype(bf16).astype(f32)
        second = (query - first).astype(bf16).astype(f32)
        third = query - first - second
        qaug = jnp.concatenate(
            [first, second, third, jnp.ones((32, block), f32)], axis=0
        ).astype(bf16)
        t = jnp.dot(r.kaug[...], qaug, preferred_element_type=f32)
        r.scores[...] = t
        highest = jnp.max(jnp.max(t.reshape(total // 8, 8, block), axis=0), axis=0, keepdims=True)
        p = jnp.exp2(r.scores[...] - highest)
        r.scores[...] = p
        low_p = p.astype(bf16)
        r.low[...] = low_p
        norm = jnp.sum(p.reshape(total // 8, 8, block), axis=0)
        heads = jnp.dot(r.xt[32:64, :], low_p, preferred_element_type=f32)
        inverse = 1.0 / jnp.sum(norm, axis=0, keepdims=True)
        heads = heads * inverse
        back = xt[32:64]
        centred = jnp.sum(back * heads, axis=0, keepdims=True) * inverse
        back = back * inverse
        back_first = back.astype(bf16).astype(f32)
        back_second = back - back_first
        cen_first = centred.astype(bf16).astype(f32)
        cen_second = (centred - cen_first).astype(bf16).astype(f32)
        cen_third = centred - cen_first - cen_second
        sub = lax.broadcasted_iota(jnp.int32, (64, block), 0)
        cen = jnp.where(
            sub == 0,
            cen_first,
            jnp.where(sub == 1, cen_second, jnp.where(sub == 2, cen_third, 0.0)),
        )
        baug = jnp.concatenate([back_first, back_second, -cen], axis=0).astype(bf16)
        dp = jnp.dot(r.vaug[...], baug, preferred_element_type=f32)
        ds = (r.scores[...] * dp).astype(bf16)
        r.acc[32:64, :] += nt_dot(back_first.astype(bf16), r.low[...])
        r.acc[0:32, :] += nt_dot(xt[0:32].astype(bf16), ds)
        back_queries = jnp.dot(r.xt[0:32, :], ds, preferred_element_type=f32)
        zeros = jnp.zeros((64, block), f32)
        done = jnp.concatenate([back_queries * scale, heads, zeros], axis=0).T
        for part in range(group):
            source = index * group + part
            r.near_out[source] = packed(done[part * CELLS : part * CELLS + CELLS])

            @pl.when(source != lon)
            def _():
                near_copy(source, lon).start()

        return carry

    lax.fori_loop(0, groups, one_block, 0)
    r.near_in[lon] = r.near_out[lon]

    def finish(index, carry):
        start = pl.multiple_of(index * block, block)
        both = r.acc[:, pl.ds(start, block)]
        zeros = jnp.zeros((64, block), f32)
        both = jnp.concatenate([both[0:32] * scale, both[32:64], zeros], axis=0)
        r.cell[pl.ds(start, block), :] = both.T
        return carry

    lax.fori_loop(0, total // block, finish, 0)

    def pack_last(source):
        start = pl.multiple_of(source * CELLS, 32)
        r.last_out[source] = packed(r.cell[pl.ds(start, CELLS), :])

    def leave(k, carry):
        to = partner(k, 1)
        pack_last(to)
        last_copy(k, to, lon).start()
        return carry

    lax.fori_loop(0, sources - 1, leave, 0)
    pack_last(lon)
    r.last_in[lon] = r.last_out[lon]

    def near_arrive(k, carry):
        source = partner(k, -1)
        near_copy(source, source).wait_recv()
        return carry

    def last_arrive(k, carry):
        source = partner(k, -1)
        last_copy(k, source, source).wait_recv()
        return carry

    def settle(k, carry):
        to = partner(k, 1)
        key_copy(k, to, lon).wait_send()
        query_copy(to, lon).wait_send()
        near_copy(to, lon).wait_send()
        last_copy(k, to, lon).wait_send()
        return carry

    return (
        halo,
        lambda: lax.fori_loop(0, sources - 1, near_arrive, 0),
        lambda: lax.fori_loop(0, sources - 1, last_arrive, 0),
        lambda: lax.fori_loop(0, sources - 1, settle, 0),
    )


def gather_heads(source, first, second, i, tile):
    half_lane = lax.broadcasted_iota(jnp.int32, (48, 128), 1)
    parts = [source[i * 16 + tile * 4 + u].astype(jnp.float32) for u in range(4)]
    for (target, column), lane in ((first, 0), (second, 32)):
        for half in range(2):
            value = None
            for u in range(4):
                shift = (u * 32 - lane - half * 64) % 128
                moved = pltpu.roll(parts[u], shift, 1) if shift else parts[u]
                value = moved if value is None else jnp.where(half_lane < u * 32, value, moved)
            start, column_start = i * CELLS + half * 48, column + tile * 128
            target[start : start + 48, column_start : column_start + 128] = value.astype(
                jnp.bfloat16
            )


def backward_phase(r, valid, factor, slope_halo, near_arrive, last_arrive, peers):
    f32, bf16 = jnp.float32, jnp.bfloat16
    sibling, x_peers, y_peers, z_peers = peers
    lat, lon = lax.axis_index("lat"), lax.axis_index("lon")
    y = lat % 4
    z, x_lo, core = lon // 4, (lon // 2) % 2, lon % 2
    x = (lat // 4) * 2 + x_lo
    other = 1 - core
    r.small[...] = jnp.zeros(r.small.shape, f32)
    near_arrive()
    for i in range(2):
        for tile in range(4):
            gather_heads(r.near_in, (r.back_project, 0), (r.heads, 0), i, tile)
    field = jnp.dot(r.heads[...], r.weight_out[...], preferred_element_type=f32)
    for i in range(2):
        part = slice(i * CELLS, i * CELLS + CELLS)
        r.field[i] = (r.inner[part, :].astype(f32) + field[part]).astype(bf16)[0:valid]
    back_second = nt_dot(r.back_project[:, 0:512], r.weight_in[:, 0:512])
    last_arrive()
    for i in range(2):
        for tile in range(4):
            gather_heads(r.last_in, (r.back_project, 512), (r.back_project, 1024), i, tile)
    back_second = back_second + nt_dot(r.back_project[:, 512:1536], r.weight_in[:, 512:1536])
    gain_two = jnp.zeros((1, field.shape[1]), f32)
    for i in range(2):
        part = slice(i * CELLS, i * CELLS + CELLS)
        inner = r.inner[part, :].astype(f32)
        inverse = inverse_rms(inner)
        gain_two = gain_two + jnp.sum(back_second[part] * inner * inverse, axis=0, keepdims=True)
        scaled = back_second[part] * r.second_gain[...]
        back = (
            r.cot_pad[part, :].astype(f32)
            + inverse * scaled
            - inverse * inverse * inverse * inner * jnp.mean(scaled * inner, axis=-1, keepdims=True)
        )
        r.back_rows[i] = back.astype(bf16)
    west, east = edge_pair(r.back_rows[0].astype(f32), r.back_rows[1].astype(f32), valid - 1)
    r.back_edges[0] = west
    r.back_edges[1] = east
    halo = halo_copies(
        r.back_rows, r.back_edges, r.back_slots, r.back_sides, r.back_sends, r.back_recvs
    )
    halo_start(halo)

    def half_lanes(top, bottom):
        lane = lax.broadcasted_iota(jnp.int32, top.shape, 1)
        even = jnp.where(lane < 64, top, pltpu.roll(bottom, 64, 1))
        odd = jnp.where(lane < 64, pltpu.roll(top, 64, 1), bottom)
        return even, odd

    def cross(left, right):
        return (
            lax.dot_general(left, right, (((0,), (0,)), ((), ())), preferred_element_type=f32)
            * factor
        )

    def core_copy(mine, theirs, first, width, index):
        rows = pl.ds(first, width)
        return exchange(
            mine.at[other, rows], theirs.at[rows], r.core_sends, r.core_recvs, index, sibling
        )

    def early_x(zz):
        return core_copy(r.ex, r.ex0, zz * 2, 2, zz)

    def early_y(zz):
        return core_copy(r.ey, r.ey0, zz * 2, 2, 4 + zz)

    def late_x(pz):
        return core_copy(r.lx, r.lx0, pz, 1, 8 + pz)

    def late_y(pz):
        return core_copy(r.ly, r.ly0, pz, 1, 16 + pz)

    def early_part(zz, carry):
        columns = pl.ds(pl.multiple_of(zz * 128, 128), 128)
        own = jnp.concatenate([r.back_rows[0, :, columns], r.back_rows[1, :, columns]], axis=0)
        shrink = cross(own, r.mixed[...])
        grad_in = cross(
            r.back_project[:, pl.ds(pl.multiple_of(zz * 384, 128), 384)], r.second[...]
        )
        grad_out = cross(r.cot_pad[:, columns], r.heads[...])
        for sub in range(8):
            pz, plo, pc = zz * 2 + sub // 4, (sub // 2) % 2, sub % 2
            for plat in range(8):
                px, py = (plat // 4) * 2 + plo, plat % 4
                part = slice(sub * 16, sub * 16 + 16)
                for side in range(2):
                    column = plat * 256 + side * 128
                    r.ex[pc, pz, px, py, side * 16 : side * 16 + 16, :] = shrink[
                        part, column : column + 128
                    ].astype(bf16)
            for pair in range(4):
                tile = slice(pair * 128, pair * 128 + 128)
                top = jnp.concatenate(
                    [grad_in[sub * 48 : sub * 48 + 24, tile], grad_out[sub * 16 : sub * 16 + 8, tile]],
                    axis=0,
                )
                bottom = jnp.concatenate(
                    [
                        grad_in[sub * 48 + 24 : sub * 48 + 48, tile],
                        grad_out[sub * 16 + 8 : sub * 16 + 16, tile],
                    ],
                    axis=0,
                )
                parts = half_lanes(top, bottom)
                for odd in range(2):
                    plat = pair * 2 + odd
                    px, py = (plat // 4) * 2 + plo, plat % 4
                    r.ey[pc, pz, py, px] = parts[odd].astype(bf16)
        early_x(zz).start()
        early_y(zz).start()
        return carry

    lax.fori_loop(0, 4, early_part, 0)

    def add_pair(mine, theirs, pz):
        for q in range(4):
            mine[core, pz, q] = (mine[core, pz, q].astype(f32) + theirs[pz, q].astype(f32)).astype(bf16)

    def early_arrive(zz, carry):
        early_x(zz).wait_recv()
        early_y(zz).wait_recv()
        for step in range(2):
            add_pair(r.ex, r.ex0, zz * 2 + step)
            add_pair(r.ey, r.ey0, zz * 2 + step)
        return carry

    lax.fori_loop(0, 4, early_arrive, 0)
    count = [0]

    def copy(source, target, peer):
        index = count[0]
        count[0] += 1
        made = exchange(source, target, r.sends, r.recvs, index, peer)
        made.start()
        return made

    def stage_one(mine, slots, targets, here):
        return [
            copy(mine.at[core, :, (here + d) % 4], slots.at[d - 1], targets[d - 1])
            for d in (1, 2, 3)
        ]

    early_one_x = stage_one(r.ex, r.ex1, x_peers, x)
    early_one_y = stage_one(r.ey, r.ey1, y_peers, y)
    halo_arrive(slope_halo)
    halo_arrive(halo)
    for row in range(4):
        base = r.back_rows[row - 1] if row in (1, 2) else r.back_slots[row // 3]
        value = halo_row(row, base.astype(f32), r.back_sides, valid)
        r.wide_back[row * CELLS : row * CELLS + CELLS, :] = value.astype(bf16)
    r.back_normed[...] = jnp.zeros(r.back_normed.shape, f32)

    def chunk(pz, carry):
        start = pl.multiple_of(pz * CHUNK, CHUNK)
        lanes = pl.ds(start, CHUNK)
        product = nt_dot(r.wide_back[...], r.shrink[lanes, :])
        planes = []
        for row in range(4):
            base = r.slope[row - 1, :, lanes] if row in (1, 2) else r.slope_rows[row // 3, :, lanes]
            slope = halo_row(row, base.astype(f32), r.slope_sides, valid, lanes)
            plane = product[row * CELLS : row * CELLS + CELLS] * slope
            planes.append(plane.astype(bf16).astype(f32))
        for b in range(3):
            turned = []
            for i in range(2):
                centre = planes[i + 1]
                centre = jnp.where(inside(centre.shape, valid), centre, 0.0)
                turned.append(pltpu.roll(centre, (CELLS + b - 1) % CELLS, 0) if b != 1 else centre)
            for a in range(3):
                value = r.act[a, :, lanes].astype(f32) * turned[0]
                value = value + r.act[a + 1, :, lanes].astype(f32) * turned[1]
                r.small[a * 3 + b : a * 3 + b + 1, lanes] = (
                    jnp.sum(value, axis=0, keepdims=True) * factor
                )
        outs = []
        for i in range(2):
            sums = []
            for b in range(3):
                part = r.depth[b : b + 1, lanes] * planes[i + 2]
                for a in (1, 2):
                    part = part + r.depth[a * 3 + b : a * 3 + b + 1, lanes] * planes[i + 2 - a]
                sums.append(part)
            total = pltpu.roll(sums[0], CELLS - 1, 0) + sums[1] + pltpu.roll(sums[2], 1, 0)
            total = total * r.slope_expanded[i * CELLS : i * CELLS + CELLS, lanes].astype(f32)
            outs.append(jnp.where(inside(total.shape, valid), total, 0.0).astype(bf16))
        back = jnp.concatenate(outs, axis=0)
        r.back_normed[...] += nt_dot(back, r.expand[:, lanes])
        grad = cross(back, r.normed[...])
        for sub in range(4):
            plo, pc = sub // 2, sub % 2
            for pair in range(4):
                tile = slice(pair * 128, pair * 128 + 128)
                parts = half_lanes(
                    grad[sub * 64 : sub * 64 + 32, tile], grad[sub * 64 + 32 : sub * 64 + 64, tile]
                )
                for odd in range(2):
                    plat = pair * 2 + odd
                    px, py = (plat // 4) * 2 + plo, plat % 4
                    r.lx[pc, pz, px, py] = parts[odd][0:16].astype(bf16)
                    r.ly[pc, pz, py, px] = parts[odd][16:32].astype(bf16)
        late_x(pz).start()
        late_y(pz).start()
        return carry

    lax.fori_loop(0, 8, chunk, 0)

    def late_arrive(pz, carry):
        late_x(pz).wait_recv()
        late_y(pz).wait_recv()
        add_pair(r.lx, r.lx0, pz)
        add_pair(r.ly, r.ly0, pz)
        return carry

    lax.fori_loop(0, 8, late_arrive, 0)
    late_one_x = stage_one(r.lx, r.lx1, x_peers, x)
    late_one_y = stage_one(r.ly, r.ly1, y_peers, y)

    def add_four(mine, theirs, here, total):
        def body(pz, carry):
            value = mine[core, pz, here].astype(f32)
            for d in range(3):
                value = value + theirs[d, pz].astype(f32)
            total[pz] = value.astype(bf16)
            return carry

        lax.fori_loop(0, 8, body, 0)

    def stage_two(arrivals, mine, slots, here, total, next_slots, targets, there):
        for made in arrivals:
            made.wait_recv()
        add_four(mine, slots, here, total)
        return [
            copy(total.at[:, (there + d) % 4], next_slots.at[d - 1], targets[d - 1])
            for d in (1, 2, 3)
        ]

    early_two_x = stage_two(early_one_x, r.ex, r.ex1, x, r.ext, r.ex2, y_peers, y)
    early_two_y = stage_two(early_one_y, r.ey, r.ey1, y, r.eyt, r.ey2, x_peers, x)

    gain_one = jnp.zeros((1, r.back_normed.shape[1]), f32)
    for i in range(2):
        part = slice(i * CELLS, i * CELLS + valid)
        state = r.state[i].astype(f32)
        inverse = inverse_rms(state)
        back = r.back_normed[part, :]
        gain_one = gain_one + jnp.sum(back * state * inverse, axis=0, keepdims=True)
        scaled = back * r.first_gain[...]
        r.grad[i] = (
            r.back_rows[i, 0:valid, :].astype(f32)
            + inverse * scaled
            - inverse * inverse * inverse * state * jnp.mean(scaled * state, axis=-1, keepdims=True)
        ).astype(bf16)
    width = r.small.shape[1]
    r.small[9:10, :] = jnp.concatenate(
        [gain_one * factor, gain_two * factor, jnp.zeros((1, width - 1024), f32)], axis=1
    )
    half = width // 2
    r.small_half[...] = r.small[:, pl.ds(pl.multiple_of(other * half, half), half)]
    small_core = copy(r.small_half, r.small_other, sibling)
    small_core.wait_recv()
    total = r.small[:, pl.ds(pl.multiple_of(core * half, half), half)] + r.small_other[...]
    for index in range(8):
        r.small_split[index] = total[:, index * 128 : index * 128 + 128]
    small_z = [
        copy(r.small_split.at[(z + d) % 8], r.small_z.at[z], z_peers[d - 1]) for d in range(1, 8)
    ]
    r.small_z[z] = r.small_split[z]

    def stage_three(arrivals, total, slots, here, first, count_rows):
        for made in arrivals:
            made.wait_recv()

        def body(pz, carry):
            value = total[pz, here].astype(f32)
            for d in range(3):
                value = value + slots[d, pz].astype(f32)
            r.final[pz, first : first + count_rows, :] = value.astype(bf16)
            return carry

        lax.fori_loop(0, 8, body, 0)

    def send_final(first, count_rows):
        rows = pl.ds(first, count_rows)
        return [
            copy(r.final.at[(z + d) % 8, rows], r.final_in.at[d - 1, rows], z_peers[d - 1])
            for d in range(1, 8)
        ]

    stage_three(early_two_x, r.ext, r.ex2, y, 0, 32)
    stage_three(early_two_y, r.eyt, r.ey2, x, 32, 32)
    final_early = send_final(0, 64)
    late_two_x = stage_two(late_one_x, r.lx, r.lx1, x, r.lxt, r.lx2, y_peers, y)
    late_two_y = stage_two(late_one_y, r.ly, r.ly1, y, r.lyt, r.ly2, x_peers, x)

    for made in small_z:
        made.wait_recv()
    total = r.small_z[0]
    for index in range(1, 8):
        total = total + r.small_z[index]
    r.small_y[y] = total
    small_y = [copy(r.small_y.at[y], r.small_y.at[y], peer) for peer in y_peers]

    stage_three(late_two_x, r.lxt, r.lx2, y, 64, 16)
    stage_three(late_two_y, r.lyt, r.ly2, x, 80, 16)
    final_late = send_final(64, 32)

    for made in small_y:
        made.wait_recv()
    r.small_x[x] = (r.small_y[0] + r.small_y[1]) + (r.small_y[2] + r.small_y[3])
    small_x = [copy(r.small_x.at[x], r.small_x.at[x], peer) for peer in x_peers]
    for made in small_x:
        made.wait_recv()
    r.sums[core, z] = (r.small_x[0] + r.small_x[1]) + (r.small_x[2] + r.small_x[3])
    small_all = [copy(r.sums.at[core, z], r.sums.at[core, z], peer) for peer in z_peers]

    for made in final_early + final_late:
        made.wait_recv()
    value = r.final[z].astype(f32)
    for d in range(7):
        value = value + r.final_in[d].astype(f32)
    r.block[...] = value
    for made in small_all:
        made.wait_recv()
    small_last = copy(r.sums.at[core], r.sums.at[core], sibling)
    small_last.wait_recv()
    for made in (
        early_one_x
        + early_one_y
        + late_one_x
        + late_one_y
        + early_two_x
        + early_two_y
        + late_two_x
        + late_two_y
        + final_early
        + final_late
        + small_z
        + small_y
        + small_x
        + small_all
        + [small_core, small_last]
    ):
        made.wait_send()

    def settle(pz, carry):
        late_x(pz).wait_send()
        late_y(pz).wait_send()
        return carry

    def settle_early(zz, carry):
        early_x(zz).wait_send()
        early_y(zz).wait_send()
        return carry

    lax.fori_loop(0, 8, settle, 0)
    lax.fori_loop(0, 4, settle_early, 0)
    halo_leave(halo)


def step_kernel(names, valid, scale, factor, *refs):
    r = Refs(names, refs)
    lat, lon = lax.axis_index("lat"), lax.axis_index("lon")
    sectors = lax.axis_size("lon")
    y, z, x_lo, core = lat % 4, lon // 4, (lon // 2) % 2, lon % 2
    x = (lat // 4) * 2 + x_lo

    def place(px, py, pz, pc):
        return ((px // 2) * 4 + py, pz * 4 + (px % 2) * 2 + pc)

    barrier = pltpu.get_barrier_semaphore()
    peers = (
        place(x, y, z, 1 - core),
        [place((x + d) % 4, y, z, core) for d in range(1, 4)],
        [place(x, (y + d) % 4, z, core) for d in range(1, 4)],
        [place(x, y, (z + d) % 8, core) for d in range(1, 8)],
    )
    greetings = halo_greet(barrier)
    for peer in peers[1] + peers[2]:
        pl.semaphore_signal(barrier, inc=1, device_id=peer, device_id_type=MESH)

    def greet(k, carry):
        pl.semaphore_signal(barrier, inc=1, device_id=(lat, partner(k, 1)), device_id_type=MESH)
        return carry

    lax.fori_loop(0, sectors - 1, greet, 0)
    greetings = greetings + len(peers[1]) + len(peers[2]) + sectors - 1
    load = {}
    for index, (name, source, target) in enumerate(
        (
            ("state", r.state_hbm, r.state),
            ("cot", r.cot_hbm, r.cot),
            ("out", r.out_hbm, r.weight_out),
            ("expand", r.expand_hbm, r.expand),
            ("shrink", r.shrink_hbm, r.shrink),
            ("in", r.in_hbm, r.weight_in),
        )
    ):
        load[name] = pltpu.make_async_copy(source, target, r.loads.at[index])
        load[name].start()
    state_halo = forward_phase(r, load, valid, greetings)
    slope_halo, near_arrive, last_arrive, settle = attention_phase(r, valid, scale)
    backward_phase(r, valid, factor, slope_halo, near_arrive, last_arrive, peers)
    settle()
    halo_leave(state_halo)
    halo_leave(slope_halo)


def whole_step(factor, scale, operands, bias, depth, first_gain, second_gain):
    f32, bf16 = jnp.float32, jnp.bfloat16
    state, cot, expand, shrink, weight_in, weight_out = operands
    valid = state.shape[1]
    channels, wide = expand.shape
    cells, half = 2 * CELLS, wide // 2
    sources = lax.axis_size("lon")
    total, block = sources * CELLS, 768
    vmem, dma = pltpu.VMEM, pltpu.SemaphoreType.DMA
    message = vmem((sources, 48, 128), bf16)

    def tree(name, rows):
        return {
            name: vmem((2, 8, 4, 4, rows, 128), bf16),
            name + "0": vmem((8, 4, 4, rows, 128), bf16),
            name + "1": vmem((3, 8, 4, rows, 128), bf16),
            name + "t": vmem((8, 4, rows, 128), bf16),
            name + "2": vmem((3, 8, rows, 128), bf16),
        }

    def halo_set(prefix, width):
        return {prefix + "sends": dma((8,)), prefix + "recvs": dma((8,))}

    scratch = {
        "state": vmem(state.shape, bf16),
        "cot": vmem(cot.shape, bf16),
        "expand": vmem(expand.shape, bf16),
        "shrink": vmem(shrink.shape, bf16),
        "weight_in": vmem(weight_in.shape, bf16),
        "weight_out": vmem(weight_out.shape, bf16),
        "rows": vmem((2, CELLS, channels), bf16),
        "edges": vmem((2, 8, channels), f32),
        "row_slots": vmem((2, CELLS, channels), bf16),
        "edge_slots": vmem((2, 3, 8, channels), f32),
        "back_rows": vmem((2, CELLS, channels), bf16),
        "back_edges": vmem((2, 8, channels), f32),
        "back_slots": vmem((2, CELLS, channels), bf16),
        "back_sides": vmem((2, 3, 8, channels), f32),
        "slope": vmem((2, CELLS, wide), bf16),
        "slope_edges": vmem((2, 8, wide), f32),
        "slope_rows": vmem((2, CELLS, wide), bf16),
        "slope_sides": vmem((2, 3, 8, wide), f32),
        "wide_normed": vmem((4 * CELLS, channels), bf16),
        "wide_back": vmem((4 * CELLS, channels), bf16),
        "total": vmem((cells, channels), f32),
        "back_normed": vmem((cells, channels), f32),
        "projected": vmem((cells, 4 * channels), bf16),
        "back_project": vmem((cells, 3 * channels), bf16),
        "heads": vmem((cells, channels), bf16),
        "cot_pad": vmem((cells, channels), bf16),
        "act": vmem((4, CELLS, wide), bf16),
        "slope_expanded": vmem((cells, wide), bf16),
        "mixed": vmem((cells, wide), bf16),
        "normed": vmem((cells, channels), bf16),
        "inner": vmem((cells, channels), bf16),
        "second": vmem((cells, channels), bf16),
        "kv_out": message,
        "kv_in": message,
        "qd_out": message,
        "qd_in": message,
        "near_out": message,
        "near_in": message,
        "last_out": message,
        "last_in": message,
        "xt": vmem((64, total), bf16),
        "kaug": vmem((total, 128), bf16),
        "vaug": vmem((total, 128), bf16),
        "scores": vmem((total, block), f32),
        "low": vmem((total, block), bf16),
        "acc": vmem((64, total), f32),
        "cell": vmem((total, 128), f32),
        "qd_cell": vmem((block, 128), f32),
        **tree("ex", 32),
        **tree("ey", 32),
        **tree("lx", 16),
        **tree("ly", 16),
        "final": vmem((8, 96, 128), bf16),
        "final_in": vmem((7, 96, 128), bf16),
        "small": vmem((16, wide), f32),
        "small_half": vmem((16, half), f32),
        "small_other": vmem((16, half), f32),
        "small_split": vmem((8, 16, 128), f32),
        "small_z": vmem((8, 16, 128), f32),
        "small_y": vmem((4, 16, 128), f32),
        "small_x": vmem((4, 16, 128), f32),
        "loads": dma((6,)),
        "core_sends": dma((24,)),
        "core_recvs": dma((24,)),
        "sends": dma((66,)),
        "recvs": dma((66,)),
    }
    for prefix in ("state_", "slope_", "back_"):
        scratch[prefix + "sends"] = dma((8,))
        scratch[prefix + "recvs"] = dma((8,))
    for prefix in ("kv_", "qd_", "near_", "last_"):
        scratch[prefix + "sends"] = dma((sources,))
        scratch[prefix + "recvs"] = dma((sources,))
    inputs = [name + "_hbm" for name in ("state", "cot", "expand", "shrink", "in", "out")]
    inputs += ["bias", "depth", "first_gain", "second_gain"]
    outputs = {
        "field": (state.shape, bf16),
        "grad": (state.shape, bf16),
        "block": ((96, 128), f32),
        "sums": ((2, 8, 16, 128), f32),
    }
    names = inputs + list(outputs) + list(scratch)
    whole, anywhere = pl.BlockSpec(memory_space=vmem), pl.BlockSpec(memory_space=pl.ANY)
    return pl.pallas_call(
        functools.partial(step_kernel, names, valid, scale, factor),
        out_shape=tuple(jax.ShapeDtypeStruct(*kind) for kind in outputs.values()),
        in_specs=[anywhere] * 6 + [whole] * 4,
        out_specs=(whole,) * 4,
        scratch_shapes=list(scratch.values()),
        compiler_params=pltpu.CompilerParams(
            vmem_limit_bytes=VMEM_MIB * 1024 * 1024, collective_id=1, has_side_effects=True
        ),
        name="step",
    )(*operands, bias, depth, first_gain, second_gain)


def owner_blocks(block):
    def unfold(part):
        return jnp.concatenate([part[:, :64], part[:, 64:]], axis=0).T

    expand = unfold(block[64:96])
    shrink = jnp.concatenate([block[0:16], block[16:32]], axis=1).T
    grad_in = unfold(block[32:56])
    grad_out = unfold(block[56:64])
    return expand, shrink, grad_in, grad_out


def per_device(
    state_field,
    cotangent,
    key_bias,
    input_gain,
    expand_weight,
    depth_weight,
    shrink_weight,
    attention_gain,
    attention_in,
    attention_out,
):
    row_count, lon_count, channels = state_field.shape
    head_count = key_bias.shape[2]
    wide_count = expand_weight.shape[1]
    norm_factor = 1.0 / math.sqrt(
        row_count * lon_count * lax.axis_size("lat") * lax.axis_size("lon")
    )
    score_scale = 1.0 / math.sqrt(channels // head_count)
    bias = key_bias.astype(jnp.float32).transpose(0, 2, 1)
    bias = bias.reshape(row_count * head_count, lon_count)
    bias = jnp.pad(bias, ((0, 0), (0, CELLS - lon_count))).reshape(-1, CELLS // 2)
    bias = jnp.pad(bias, ((0, 0), (0, 128 - CELLS // 2)))
    output_field, input_grad, block, sums = whole_step(
        norm_factor,
        score_scale,
        (state_field, cotangent, expand_weight, shrink_weight, attention_in, attention_out),
        bias,
        depth_weight.astype(jnp.float32).reshape(9, wide_count),
        input_gain.reshape(1, channels),
        attention_gain.reshape(1, channels),
    )
    sums = sums.transpose(2, 0, 1, 3).reshape(16, wide_count)
    return (
        output_field,
        input_grad,
        *owner_blocks(block),
        sums[:9].reshape(3, 3, wide_count),
        sums[9, :channels],
        sums[9, channels : 2 * channels],
    )


def solution(mesh):
    placed = (
        P("lat", "lon", None),
        P("lat", "lon", None),
        P("lat", "lon", None),
        P(),
        P(),
        P(),
        P(),
        P(),
        P(),
        P(),
    )
    return jax.shard_map(
        per_device,
        mesh=mesh,
        in_specs=placed,
        out_specs=(
            P("lat", "lon", None),
            P("lat", "lon", None),
            P("lat", "lon"),
            P("lat", "lon"),
            P("lat", "lon"),
            P("lat", "lon"),
            P(),
            P(),
            P(),
        ),
        check_vma=False,
    )
```

time: 1140 us -> 158 us (0.14); the launches traced: 1130 us -> 157 us
  waiting for transfers between devices: 609 us -> 0 us
  Pallas kernels: 0 us -> 138 us
  other arithmetic: 127 us -> 2.45 us
  matrix products: 118 us -> 0 us
  starting transfers between devices: 82 us -> 0 us
  blocking collectives: 80 us -> 0 us
  local copies, waits for them, and re-layouts: 93.8 us -> 16.2 us
  between operations: 17.2 us -> 0.67 us
    reduce_scatter x5 -> x0, waiting for transfers between devices: 406 us -> none  [the longest x1 118 us: per_device(): lax.psum_scatter(expand_local.astype(jnp.bfloat16), 'lon', scatter_dimens...]
    unnamed x12 -> x0, waiting for transfers between devices: 146 us -> none
    pallas_call x0 -> x1, Pallas kernels: none -> 138 us  [whole_step(): pl.pallas_call(functools.partial(step_kernel, names, valid, scale, factor...]
    dot_general x40 -> x0, matrix products: 118 us -> none  [the longest x8 35.1 us: score_block(): jnp.einsum('qd,kd->qk', query_block, key_row, preferred_element_type=jnp....]
    psum x1 -> x0, blocking collectives: 80 us -> none  [per_device(): lax.psum((depth_local, gain_one, gain_two), ('lat', 'lon'))]
    unnamed x6 -> x0, other arithmetic: 69 us -> none
    all_to_all x9 -> x0, starting transfers between devices: 66.3 us -> none  [the longest x1 10.6 us: per_device(): lax.all_to_all(bias_items, 'lon', split_axis=0, concat_axis=1, tiled=True)]
    convert_element_type x18 -> x0, other arithmetic: 41.3 us -> none  [the longest x4 36 us: one_block(): back_scores = (probs_float * (back_probs - centred)).astype(jnp.bfloat16)]
  transfers between devices with their start and end apart: 26 -> 0, of which waited for: 16 -> 0; matrix products, arithmetic and copies ran while one was open for 24% -> 0% of each run, Pallas kernels for 0% -> 0%
where the time goes in v4:
time: 158 us; the launch traced here: 157 us
  Pallas kernels  138 us (87%)
  local copies, waits for them, and re-layouts  16.2 us (10%)
  other arithmetic  2.45 us (2%)
    pallas_call x1, Pallas kernels, whole_step(): pl.pallas_call(functools.partial(step_kernel, names, valid, scale, factor...  138 us
    unnamed x6, local copies, waits for them, and re-layouts  7.55 us

profile of v4, /device:TPU:1, one launch (start us, length us, event | category | flops | bytes accessed | tf_op | source)
XLA Modules:
  0.0 157.0 jit_solution(11780626311469703877)
XLA Ops:
  0.6 0.7 pad.11
  1.3 0.1 reshape.46
  1.4 0.6 pad_convert_fusion.refs_6_
  2.1 1.5 reshape.54.refs_7_
  3.5 1.6 %copy.24.refs_0_ = bf16[2,90,512]{2,1,0:T(8,128)(2,1)} copy(bf16[2,90,512]{2,0,1:T(2,128)(2,1)} %param.10) | data formatting | bytes 368640 | tf_op args[0]
  5.2 1.6 %copy.25.refs_1_ = bf16[2,90,512]{2,1,0:T(8,128)(2,1)} copy(bf16[2,90,512]{2,0,1:T(2,128)(2,1)} %param.11) | data formatting | bytes 368640 | tf_op args[1]
  6.8 137.7 %step.1 = (bf16[2,90,512]{2,1,0:T(8,128)(2,1)}, bf16[2,90,512]{2,1,0:T(8,128)(2,1)}, f32[96,128]{1,0:T(8,128)}, f32[2,8,16,128]{3,2,1,0:T(8,128)}) custom-call(bf16[2,90,512]{2,1,0:T(8,128)(2,1)} %copy.24.refs_0_, bf16[2,90,512]{2,1,0:T(8,128)(2,1)} %copy.25.refs_1_, bf16[512,2048]{1,0:T(8,128)(2,1)} %refs_2_.1, bf16[2048,512]{1,0:T(8,128)(2,1)} %refs_3_.1, ...), custom_call_target="tpu_custom_call" | custom-call | tf_op jit(solution)/shard_map/step/pallas_call | solution.py:1046
  144.4 1.8 %copy.28 = bf16[2,90,512]{2,0,1:T(2,128)(2,1)} copy(bf16[2,90,512]{2,1,0:T(8,128)(2,1)} %get-tuple-element.26) | data formatting | bytes 368640
  146.2 0.8 fusion.1
  147.1 0.6 maximum_bitcast_fusion.3
  147.7 0.7 fusion.3
  148.4 0.6 maximum_bitcast_fusion.2
  149.0 0.9 fusion.2
  149.8 0.9 fusion.4
  150.7 0.7 copy.30
  151.4 0.6 maximum_bitcast_fusion.1
  152.0 0.9 copy.26
  153.0 0.7 reshape.51
  153.6 0.9 copy.27
  154.6 0.6 fusion
  155.2 1.8 %copy.29 = bf16[2,90,512]{2,0,1:T(2,128)(2,1)} copy(bf16[2,90,512]{2,1,0:T(8,128)(2,1)} %get-tuple-element.27) | data formatting | bytes 368640
  (2 shorter events, 0.1 us)

commit v5 on v4

--- a/solution.py
+++ b/solution.py
@@ -11,7 +11,7 @@
 EPSILON = 1e-06
 CELLS = 96
 MESH = pl.DeviceIdType.MESH
-VMEM_MIB = 60
+VMEM_MIB = 54
 
 
 CHUNK = 256
@@ -161,16 +161,26 @@
     )
 
 
-def partner(k, sign):
-    lon = lax.axis_index("lon")
-    z, low = lon // 4, lon % 4
-    ring, side = k // 4, 3 - k % 4
-    half = (ring + 1) // 2
-    shift = 4 + (1 - 2 * (ring % 2)) * half
-    x_lo, core = low // 2, low % 2
-    x_lo = x_lo + (side // 2) * (1 - 2 * x_lo)
-    core = core + (side % 2) * (1 - 2 * core)
-    return ((z + sign * shift + 8) % 8) * 4 + x_lo * 2 + core
+class Ring:
+    def __init__(self):
+        lon = lax.axis_index("lon")
+        z, low = lax.div(lon, 4), lax.rem(lon, 4)
+        x_lo, core = lax.div(low, 2), lax.rem(low, 2)
+        self.column, self.x_lo, self.core = lon, x_lo, core
+        self.starts = [lax.rem(z + d, 8) * 4 for d in range(8)]
+        self.sides = [self.side(low_x, low_c) for low_x in range(2) for low_c in range(2)]
+
+    def side(self, flip_x, flip_core):
+        x_lo = self.x_lo + flip_x * (1 - 2 * self.x_lo)
+        core = self.core + flip_core * (1 - 2 * self.core)
+        return x_lo * 2 + core
+
+    def start(self, ring, sign):
+        half = (ring + 1) // 2
+        return self.starts[(sign * (4 + (half if ring % 2 == 0 else -half))) % 8]
+
+    def partner(self, k, sign):
+        return self.start(k // 4, sign) + self.sides[3 - k % 4]
 
 
 def packed(cells):
@@ -191,19 +201,28 @@
     r.cot_pad[...] = jnp.zeros(r.cot_pad.shape, bf16)
     load["state"].wait()
     for i in range(2):
-        r.rows[i, 0:valid, :] = r.state[i]
+        r.rows[i, 0:valid, :] = r.state[:, i, :]
     west, east = edge_pair(r.rows[0].astype(f32), r.rows[1].astype(f32), valid - 1)
     r.edges[0] = west
     r.edges[1] = east
+    load["cot"].wait()
+    load["out"].wait()
+    for i in range(2):
+        r.cot_pad[i * CELLS : i * CELLS + valid, :] = r.cot[:, i, :]
+    r.projected[:, 1536:2048] = nt_dot(r.cot_pad[...], r.weight_out[...]).astype(bf16)
     pl.semaphore_wait(pltpu.get_barrier_semaphore(), greetings)
     copies = halo_copies(r.rows, r.edges, r.row_slots, r.edge_slots, r.state_sends, r.state_recvs)
     halo_start(copies)
-    load["cot"].wait()
-    load["out"].wait()
+    r.total[...] = jnp.zeros(r.total.shape, f32)
+    r.bias_cells[...] = jnp.zeros(r.bias_cells.shape, f32)
+    bias_lane = lax.broadcasted_iota(jnp.int32, (16, 128), 1)
     for i in range(2):
-        r.cot_pad[i * CELLS : i * CELLS + valid, :] = r.cot[i]
-    r.projected[:, 1536:2048] = nt_dot(r.cot_pad[...], r.weight_out[...]).astype(bf16)
-    r.total[...] = jnp.zeros(r.total.shape, f32)
+        r.bias_cells[i, :, 0:valid] = r.bias[i].astype(f32)
+        heads = r.bias_cells[i]
+        r.bias_low[i * 16 : i * 16 + 16, :] = jnp.where(bias_lane < 48, heads, 0.0)
+        r.bias_high[i * 16 : i * 16 + 16, :] = jnp.where(bias_lane < 48, pltpu.roll(heads, 80, 1), 0.0)
+    for a in range(3):
+        r.depth[a * 3 : a * 3 + 3, :] = r.depth_low[a].astype(f32)
     load["expand"].wait()
     load["shrink"].wait()
     halo_arrive(copies)
@@ -283,8 +302,8 @@
                 ]
                 value = jnp.where(lane < 32, moved[0], jnp.where(lane < 64, moved[1], 0.0))
                 if with_bias:
-                    value = jnp.where(row == valid, r.bias[2 * item : 2 * item + 1, :], value)
-                    value = jnp.where(row == valid + 1, r.bias[2 * item + 1 : 2 * item + 2, :], value)
+                    value = jnp.where(row == valid, r.bias_low[item : item + 1, :], value)
+                    value = jnp.where(row == valid + 1, r.bias_high[item : item + 1, :], value)
                 target[item] = packed(value)
 
 
@@ -298,6 +317,7 @@
     f32, bf16 = jnp.float32, jnp.bfloat16
     lat, lon = lax.axis_index("lat"), lax.axis_index("lon")
     groups = sources // group
+    ring, own_group = r.ring, lax.div(lon, group)
 
     def key_copy(k, to, slot):
         return exchange(
@@ -324,26 +344,25 @@
     ).astype(bf16)
     project_and_pack(r, valid, 512, 1024, r.kv_out, True)
 
-    def push_keys(k, carry):
-        key_copy(k, partner(k, 1), lon).start()
-        return carry
-
-    lax.fori_loop(0, sources - 1, push_keys, 0)
+    for k in range(sources - 1):
+        key_copy(k, ring.partner(k, 1), lon).start()
     r.projected[:, 0:512] = jnp.dot(
         r.second[...], r.weight_in[:, 0:512], preferred_element_type=f32
     ).astype(bf16)
     project_and_pack(r, valid, 0, 1536, r.qd_out, False)
 
-    def push_queries(step, carry):
-        to = ((lon // group + groups - step // group) % groups) * group + step % group
-
-        @pl.when(to != lon)
-        def _():
-            query_copy(to, lon).start()
-
-        return carry
-
-    lax.fori_loop(0, sources, push_queries, 0)
+    for step in range(groups):
+        target = lax.rem(own_group + groups - step, groups) * group
+        for part in range(group):
+            to = target + part
+            if step:
+                query_copy(to, lon).start()
+            else:
+
+                @pl.when(to != lon)
+                def _():
+                    query_copy(to, lon).start()
+
     halo = halo_copies(
         r.slope, r.slope_edges, r.slope_rows, r.slope_sides, r.slope_sends, r.slope_recvs
     )
@@ -381,13 +400,18 @@
 
     prepare(lon)
 
-    def arrive(k, carry):
-        source = partner(k, -1)
-        key_copy(k, source, source).wait_recv()
-        prepare(source)
-        return carry
-
-    lax.fori_loop(0, sources - 1, arrive, 0)
+    for part in range(8):
+        first = ring.start(part, -1)
+
+        def arrive(step, carry):
+            flip_x = (step < 2).astype(jnp.int32)
+            flip_core = 3 - step - 2 * flip_x
+            source = first + ring.side(flip_x, flip_core)
+            key_copy(part * 4 + step, source, source).wait_recv()
+            prepare(source)
+            return carry
+
+        lax.fori_loop(0, 4 if part < 7 else 3, arrive, 0)
 
     def turn(index, carry):
         start = pl.multiple_of(index * block, block)
@@ -398,7 +422,7 @@
     lax.fori_loop(0, total // block, turn, 0)
 
     def one_block(turn_index, carry):
-        index = (turn_index + lon // group) % groups
+        index = lax.rem(turn_index + own_group, groups)
         for part in range(group):
             source = index * group + part
 
@@ -475,40 +499,32 @@
         start = pl.multiple_of(source * CELLS, 32)
         r.last_out[source] = packed(r.cell[pl.ds(start, CELLS), :])
 
-    def leave(k, carry):
-        to = partner(k, 1)
+    for k in range(sources - 1):
+        to = ring.partner(k, 1)
         pack_last(to)
         last_copy(k, to, lon).start()
-        return carry
-
-    lax.fori_loop(0, sources - 1, leave, 0)
     pack_last(lon)
     r.last_in[lon] = r.last_out[lon]
 
-    def near_arrive(k, carry):
-        source = partner(k, -1)
-        near_copy(source, source).wait_recv()
-        return carry
-
-    def last_arrive(k, carry):
-        source = partner(k, -1)
-        last_copy(k, source, source).wait_recv()
-        return carry
-
-    def settle(k, carry):
-        to = partner(k, 1)
-        key_copy(k, to, lon).wait_send()
-        query_copy(to, lon).wait_send()
-        near_copy(to, lon).wait_send()
-        last_copy(k, to, lon).wait_send()
-        return carry
-
-    return (
-        halo,
-        lambda: lax.fori_loop(0, sources - 1, near_arrive, 0),
-        lambda: lax.fori_loop(0, sources - 1, last_arrive, 0),
-        lambda: lax.fori_loop(0, sources - 1, settle, 0),
-    )
+    def near_arrive():
+        for k in range(sources - 1):
+            source = ring.partner(k, -1)
+            near_copy(source, source).wait_recv()
+
+    def last_arrive():
+        for k in range(sources - 1):
+            source = ring.partner(k, -1)
+            last_copy(k, source, source).wait_recv()
+
+    def settle():
+        for k in range(sources - 1):
+            to = ring.partner(k, 1)
+            key_copy(k, to, lon).wait_send()
+            query_copy(to, lon).wait_send()
+            near_copy(to, lon).wait_send()
+            last_copy(k, to, lon).wait_send()
+
+    return halo, near_arrive, last_arrive, settle
 
 
 def gather_heads(source, first, second, i, tile):
@@ -531,10 +547,12 @@
     f32, bf16 = jnp.float32, jnp.bfloat16
     sibling, x_peers, y_peers, z_peers = peers
     lat, lon = lax.axis_index("lat"), lax.axis_index("lon")
-    y = lat % 4
-    z, x_lo, core = lon // 4, (lon // 2) % 2, lon % 2
-    x = (lat // 4) * 2 + x_lo
+    y = lax.rem(lat, 4)
+    z, x_lo, core = lax.div(lon, 4), r.ring.x_lo, r.ring.core
+    x = lax.div(lat, 4) * 2 + x_lo
     other = 1 - core
+    xs, ys = [lax.rem(x + d, 4) for d in range(4)], [lax.rem(y + d, 4) for d in range(4)]
+    zs = [lax.rem(z + d, 8) for d in range(8)]
     r.small[...] = jnp.zeros(r.small.shape, f32)
     near_arrive()
     for i in range(2):
@@ -665,14 +683,14 @@
         made.start()
         return made
 
-    def stage_one(mine, slots, targets, here):
+    def stage_one(mine, slots, targets, turns):
         return [
-            copy(mine.at[core, :, (here + d) % 4], slots.at[d - 1], targets[d - 1])
+            copy(mine.at[core, :, turns[d]], slots.at[d - 1], targets[d - 1])
             for d in (1, 2, 3)
         ]
 
-    early_one_x = stage_one(r.ex, r.ex1, x_peers, x)
-    early_one_y = stage_one(r.ey, r.ey1, y_peers, y)
+    early_one_x = stage_one(r.ex, r.ex1, x_peers, xs)
+    early_one_y = stage_one(r.ey, r.ey1, y_peers, ys)
     halo_arrive(slope_halo)
     halo_arrive(halo)
     for row in range(4):
@@ -734,44 +752,10 @@
         return carry
 
     lax.fori_loop(0, 8, chunk, 0)
-
-    def late_arrive(pz, carry):
-        late_x(pz).wait_recv()
-        late_y(pz).wait_recv()
-        add_pair(r.lx, r.lx0, pz)
-        add_pair(r.ly, r.ly0, pz)
-        return carry
-
-    lax.fori_loop(0, 8, late_arrive, 0)
-    late_one_x = stage_one(r.lx, r.lx1, x_peers, x)
-    late_one_y = stage_one(r.ly, r.ly1, y_peers, y)
-
-    def add_four(mine, theirs, here, total):
-        def body(pz, carry):
-            value = mine[core, pz, here].astype(f32)
-            for d in range(3):
-                value = value + theirs[d, pz].astype(f32)
-            total[pz] = value.astype(bf16)
-            return carry
-
-        lax.fori_loop(0, 8, body, 0)
-
-    def stage_two(arrivals, mine, slots, here, total, next_slots, targets, there):
-        for made in arrivals:
-            made.wait_recv()
-        add_four(mine, slots, here, total)
-        return [
-            copy(total.at[:, (there + d) % 4], next_slots.at[d - 1], targets[d - 1])
-            for d in (1, 2, 3)
-        ]
-
-    early_two_x = stage_two(early_one_x, r.ex, r.ex1, x, r.ext, r.ex2, y_peers, y)
-    early_two_y = stage_two(early_one_y, r.ey, r.ey1, y, r.eyt, r.ey2, x_peers, x)
-
     gain_one = jnp.zeros((1, r.back_normed.shape[1]), f32)
     for i in range(2):
         part = slice(i * CELLS, i * CELLS + valid)
-        state = r.state[i].astype(f32)
+        state = r.rows[i, 0:valid, :].astype(f32)
         inverse = inverse_rms(state)
         back = r.back_normed[part, :]
         gain_one = gain_one + jnp.sum(back * state * inverse, axis=0, keepdims=True)
@@ -785,17 +769,60 @@
     r.small[9:10, :] = jnp.concatenate(
         [gain_one * factor, gain_two * factor, jnp.zeros((1, width - 1024), f32)], axis=1
     )
-    half = width // 2
-    r.small_half[...] = r.small[:, pl.ds(pl.multiple_of(other * half, half), half)]
-    small_core = copy(r.small_half, r.small_other, sibling)
-    small_core.wait_recv()
-    total = r.small[:, pl.ds(pl.multiple_of(core * half, half), half)] + r.small_other[...]
-    for index in range(8):
-        r.small_split[index] = total[:, index * 128 : index * 128 + 128]
-    small_z = [
-        copy(r.small_split.at[(z + d) % 8], r.small_z.at[z], z_peers[d - 1]) for d in range(1, 8)
-    ]
-    r.small_z[z] = r.small_split[z]
+    for tile in range(16):
+        for part in range(2):
+            r.small_split[tile * 2 + part] = r.small[
+                part * 8 : part * 8 + 8, tile * 128 : tile * 128 + 128
+            ]
+    sectors, bands = r.small_lon.shape[0], r.small_lat.shape[0]
+    columns = [(r.ring.partner(k, 1), r.ring.partner(k, -1)) for k in range(sectors - 1)]
+
+    def scatter(k, to, slot):
+        return exchange(
+            r.small_split.at[to], r.small_lon.at[slot], r.small_sends, r.small_recvs, k, (lat, to)
+        )
+
+    def spread(k, to, slot):
+        return exchange(
+            r.sums.at[lon], r.sums.at[slot], r.spread_sends, r.spread_recvs, k, (lat, to)
+        )
+
+    for k, (to, _) in enumerate(columns):
+        scatter(k, to, lon).start()
+    r.small_lon[lon] = r.small_split[lon]
+
+    def late_arrive(pz, carry):
+        late_x(pz).wait_recv()
+        late_y(pz).wait_recv()
+        add_pair(r.lx, r.lx0, pz)
+        add_pair(r.ly, r.ly0, pz)
+        return carry
+
+    lax.fori_loop(0, 8, late_arrive, 0)
+    late_one_x = stage_one(r.lx, r.lx1, x_peers, xs)
+    late_one_y = stage_one(r.ly, r.ly1, y_peers, ys)
+
+    def add_four(mine, theirs, here, total):
+        def body(pz, carry):
+            value = mine[core, pz, here].astype(f32)
+            for d in range(3):
+                value = value + theirs[d, pz].astype(f32)
+            total[pz] = value.astype(bf16)
+            return carry
+
+        lax.fori_loop(0, 8, body, 0)
+
+    def stage_two(arrivals, mine, slots, here, total, next_slots, targets, turns):
+        for made in arrivals:
+            made.wait_recv()
+        add_four(mine, slots, here, total)
+        return [
+            copy(total.at[:, turns[d]], next_slots.at[d - 1], targets[d - 1])
+            for d in (1, 2, 3)
+        ]
+
+    early_two_x = stage_two(early_one_x, r.ex, r.ex1, x, r.ext, r.ex2, y_peers, ys)
+    early_two_y = stage_two(early_one_y, r.ey, r.ey1, y, r.eyt, r.ey2, x_peers, xs)
 
     def stage_three(arrivals, total, slots, here, first, count_rows):
         for made in arrivals:
@@ -813,36 +840,39 @@
     def send_final(first, count_rows):
         rows = pl.ds(first, count_rows)
         return [
-            copy(r.final.at[(z + d) % 8, rows], r.final_in.at[d - 1, rows], z_peers[d - 1])
+            copy(r.final.at[zs[d], rows], r.final_in.at[d - 1, rows], z_peers[d - 1])
             for d in range(1, 8)
         ]
 
     stage_three(early_two_x, r.ext, r.ex2, y, 0, 32)
     stage_three(early_two_y, r.eyt, r.ey2, x, 32, 32)
     final_early = send_final(0, 64)
-    late_two_x = stage_two(late_one_x, r.lx, r.lx1, x, r.lxt, r.lx2, y_peers, y)
-    late_two_y = stage_two(late_one_y, r.ly, r.ly1, y, r.lyt, r.ly2, x_peers, x)
-
-    for made in small_z:
-        made.wait_recv()
-    total = r.small_z[0]
-    for index in range(1, 8):
-        total = total + r.small_z[index]
-    r.small_y[y] = total
-    small_y = [copy(r.small_y.at[y], r.small_y.at[y], peer) for peer in y_peers]
+    late_two_x = stage_two(late_one_x, r.lx, r.lx1, x, r.lxt, r.lx2, y_peers, ys)
+    late_two_y = stage_two(late_one_y, r.ly, r.ly1, y, r.lyt, r.ly2, x_peers, xs)
+
+    for k, (_, source) in enumerate(columns):
+        scatter(k, source, source).wait_recv()
+    total = r.small_lon[0]
+    for index in range(1, sectors):
+        total = total + r.small_lon[index]
+    r.small_lat[lat] = total
+    small_lat = [
+        copy(r.small_lat.at[lat], r.small_lat.at[lat], (lax.rem(lat + d, bands), lon))
+        for d in range(1, bands)
+    ]
 
     stage_three(late_two_x, r.lxt, r.lx2, y, 64, 16)
     stage_three(late_two_y, r.lyt, r.ly2, x, 80, 16)
     final_late = send_final(64, 32)
 
-    for made in small_y:
+    for made in small_lat:
         made.wait_recv()
-    r.small_x[x] = (r.small_y[0] + r.small_y[1]) + (r.small_y[2] + r.small_y[3])
-    small_x = [copy(r.small_x.at[x], r.small_x.at[x], peer) for peer in x_peers]
-    for made in small_x:
-        made.wait_recv()
-    r.sums[core, z] = (r.small_x[0] + r.small_x[1]) + (r.small_x[2] + r.small_x[3])
-    small_all = [copy(r.sums.at[core, z], r.sums.at[core, z], peer) for peer in z_peers]
+    total = r.small_lat[0]
+    for index in range(1, bands):
+        total = total + r.small_lat[index]
+    r.sums[lon] = total
+    for k, (to, _) in enumerate(columns):
+        spread(k, to, lon).start()
 
     for made in final_early + final_late:
         made.wait_recv()
@@ -850,10 +880,10 @@
     for d in range(7):
         value = value + r.final_in[d].astype(f32)
     r.block[...] = value
-    for made in small_all:
-        made.wait_recv()
-    small_last = copy(r.sums.at[core], r.sums.at[core], sibling)
-    small_last.wait_recv()
+    for k, (to, source) in enumerate(columns):
+        spread(k, source, source).wait_recv()
+        spread(k, to, lon).wait_send()
+        scatter(k, to, lon).wait_send()
     for made in (
         early_one_x
         + early_one_y
@@ -865,11 +895,7 @@
         + late_two_y
         + final_early
         + final_late
-        + small_z
-        + small_y
-        + small_x
-        + small_all
-        + [small_core, small_last]
+        + small_lat
     ):
         made.wait_send()
 
@@ -892,29 +918,31 @@
     r = Refs(names, refs)
     lat, lon = lax.axis_index("lat"), lax.axis_index("lon")
     sectors = lax.axis_size("lon")
-    y, z, x_lo, core = lat % 4, lon // 4, (lon // 2) % 2, lon % 2
-    x = (lat // 4) * 2 + x_lo
+    y, z, core = lax.rem(lat, 4), lax.div(lon, 4), lax.rem(lon, 2)
+    x = lax.div(lat, 4) * 2 + lax.rem(lax.div(lon, 2), 2)
 
     def place(px, py, pz, pc):
-        return ((px // 2) * 4 + py, pz * 4 + (px % 2) * 2 + pc)
+        return (lax.div(px, 2) * 4 + py, pz * 4 + lax.rem(px, 2) * 2 + pc)
 
     barrier = pltpu.get_barrier_semaphore()
     peers = (
         place(x, y, z, 1 - core),
-        [place((x + d) % 4, y, z, core) for d in range(1, 4)],
-        [place(x, (y + d) % 4, z, core) for d in range(1, 4)],
-        [place(x, y, (z + d) % 8, core) for d in range(1, 8)],
+        [place(lax.rem(x + d, 4), y, z, core) for d in range(1, 4)],
+        [place(x, lax.rem(y + d, 4), z, core) for d in range(1, 4)],
+        [place(x, y, lax.rem(z + d, 8), core) for d in range(1, 8)],
     )
     greetings = halo_greet(barrier)
-    for peer in peers[1] + peers[2]:
+    bands = lax.axis_size("lat")
+    band_peers = [(lax.rem(lat + d, bands), lon) for d in range(1, bands)]
+    for peer in peers[1] + peers[2] + band_peers:
         pl.semaphore_signal(barrier, inc=1, device_id=peer, device_id_type=MESH)
 
-    def greet(k, carry):
-        pl.semaphore_signal(barrier, inc=1, device_id=(lat, partner(k, 1)), device_id_type=MESH)
-        return carry
-
-    lax.fori_loop(0, sectors - 1, greet, 0)
-    greetings = greetings + len(peers[1]) + len(peers[2]) + sectors - 1
+    r.ring = Ring()
+    for k in range(sectors - 1):
+        pl.semaphore_signal(
+            barrier, inc=1, device_id=(lat, r.ring.partner(k, 1)), device_id_type=MESH
+        )
+    greetings = greetings + len(peers[1]) + len(peers[2]) + bands - 1 + sectors - 1
     load = {}
     for index, (name, source, target) in enumerate(
         (
@@ -939,9 +967,9 @@
 def whole_step(factor, scale, operands, bias, depth, first_gain, second_gain):
     f32, bf16 = jnp.float32, jnp.bfloat16
     state, cot, expand, shrink, weight_in, weight_out = operands
-    valid = state.shape[1]
+    valid = state.shape[0]
     channels, wide = expand.shape
-    cells, half = 2 * CELLS, wide // 2
+    cells = 2 * CELLS
     sources = lax.axis_size("lon")
     total, block = sources * CELLS, 768
     vmem, dma = pltpu.VMEM, pltpu.SemaphoreType.DMA
@@ -966,6 +994,10 @@
         "shrink": vmem(shrink.shape, bf16),
         "weight_in": vmem(weight_in.shape, bf16),
         "weight_out": vmem(weight_out.shape, bf16),
+        "bias_cells": vmem((2, 16, 128), f32),
+        "bias_low": vmem((32, 128), f32),
+        "bias_high": vmem((32, 128), f32),
+        "depth": vmem((16, wide), f32),
         "rows": vmem((2, CELLS, channels), bf16),
         "edges": vmem((2, 8, channels), f32),
         "row_slots": vmem((2, CELLS, channels), bf16),
@@ -1015,12 +1047,9 @@
         "final": vmem((8, 96, 128), bf16),
         "final_in": vmem((7, 96, 128), bf16),
         "small": vmem((16, wide), f32),
-        "small_half": vmem((16, half), f32),
-        "small_other": vmem((16, half), f32),
-        "small_split": vmem((8, 16, 128), f32),
-        "small_z": vmem((8, 16, 128), f32),
-        "small_y": vmem((4, 16, 128), f32),
-        "small_x": vmem((4, 16, 128), f32),
+        "small_split": vmem((sources, 8, 128), f32),
+        "small_lon": vmem((sources, 8, 128), f32),
+        "small_lat": vmem((lax.axis_size("lat"), 8, 128), f32),
         "loads": dma((6,)),
         "core_sends": dma((24,)),
         "core_recvs": dma((24,)),
@@ -1030,16 +1059,16 @@
     for prefix in ("state_", "slope_", "back_"):
         scratch[prefix + "sends"] = dma((8,))
         scratch[prefix + "recvs"] = dma((8,))
-    for prefix in ("kv_", "qd_", "near_", "last_"):
+    for prefix in ("kv_", "qd_", "near_", "last_", "small_", "spread_"):
         scratch[prefix + "sends"] = dma((sources,))
         scratch[prefix + "recvs"] = dma((sources,))
     inputs = [name + "_hbm" for name in ("state", "cot", "expand", "shrink", "in", "out")]
-    inputs += ["bias", "depth", "first_gain", "second_gain"]
+    inputs += ["bias", "depth_low", "first_gain", "second_gain"]
     outputs = {
-        "field": (state.shape, bf16),
-        "grad": (state.shape, bf16),
+        "field": ((2, valid, channels), bf16),
+        "grad": ((2, valid, channels), bf16),
         "block": ((96, 128), f32),
-        "sums": ((2, 8, 16, 128), f32),
+        "sums": ((sources, 8, 128), f32),
     }
     names = inputs + list(outputs) + list(scratch)
     whole, anywhere = pl.BlockSpec(memory_space=vmem), pl.BlockSpec(memory_space=pl.ANY)
@@ -1056,15 +1085,43 @@
     )(*operands, bias, depth, first_gain, second_gain)
 
 
-def owner_blocks(block):
+def deliver_kernel(block_ref, sums_ref, expand_ref, shrink_ref, in_ref, out_ref, depth_ref, one_ref, two_ref):
     def unfold(part):
-        return jnp.concatenate([part[:, :64], part[:, 64:]], axis=0).T
-
+        return jnp.concatenate([part, pltpu.roll(part, 64, 1)], axis=0)
+
+    block = block_ref[...]
     expand = unfold(block[64:96])
-    shrink = jnp.concatenate([block[0:16], block[16:32]], axis=1).T
-    grad_in = unfold(block[32:56])
-    grad_out = unfold(block[56:64])
-    return expand, shrink, grad_in, grad_out
+    expand = jnp.concatenate([expand, jnp.zeros_like(expand)], axis=0).T
+    expand_ref[...] = expand[0:64, 0:64]
+    shrink_ref[:, 0:128] = block[0:16]
+    shrink_ref[:, 128:256] = block[16:32]
+    in_ref[...] = unfold(block[32:56])[:, 0:64]
+    out_ref[...] = unfold(block[56:64])[:, 0:64]
+    for tile in range(16):
+        lanes = slice(tile * 128, tile * 128 + 128)
+        low, high = sums_ref[tile * 2], sums_ref[tile * 2 + 1]
+        depth_ref[0, :, lanes] = low[0:3]
+        depth_ref[1, :, lanes] = low[3:6]
+        depth_ref[2, 0:2, lanes] = low[6:8]
+        depth_ref[2, 2:3, lanes] = high[0:1]
+        if tile < 4:
+            one_ref[:, lanes] = high[1:2]
+        elif tile < 8:
+            two_ref[:, tile * 128 - 512 : tile * 128 - 384] = high[1:2]
+
+
+def deliver(block, sums, channels, wide):
+    vmem = pl.BlockSpec(memory_space=pltpu.VMEM)
+    shapes = [(64, 64), (16, 256), (48, 64), (16, 64), (3, 3, wide), (1, channels), (1, channels)]
+    expand, shrink, grad_in, grad_out, depth, one, two = pl.pallas_call(
+        deliver_kernel,
+        out_shape=tuple(jax.ShapeDtypeStruct(shape, jnp.float32) for shape in shapes),
+        in_specs=[vmem] * 2,
+        out_specs=(vmem,) * 7,
+        name="deliver",
+    )(block, sums)
+    one, two = one.reshape(channels), two.reshape(channels)
+    return expand, shrink.T, grad_in.T, grad_out.T, depth, one, two
 
 
 def per_device(
@@ -1086,28 +1143,16 @@
         row_count * lon_count * lax.axis_size("lat") * lax.axis_size("lon")
     )
     score_scale = 1.0 / math.sqrt(channels // head_count)
-    bias = key_bias.astype(jnp.float32).transpose(0, 2, 1)
-    bias = bias.reshape(row_count * head_count, lon_count)
-    bias = jnp.pad(bias, ((0, 0), (0, CELLS - lon_count))).reshape(-1, CELLS // 2)
-    bias = jnp.pad(bias, ((0, 0), (0, 128 - CELLS // 2)))
     output_field, input_grad, block, sums = whole_step(
         norm_factor,
         score_scale,
-        (state_field, cotangent, expand_weight, shrink_weight, attention_in, attention_out),
-        bias,
-        depth_weight.astype(jnp.float32).reshape(9, wide_count),
+        (state_field.transpose(1, 0, 2), cotangent.transpose(1, 0, 2), expand_weight, shrink_weight, attention_in, attention_out),
+        key_bias.transpose(0, 2, 1),
+        depth_weight,
         input_gain.reshape(1, channels),
         attention_gain.reshape(1, channels),
     )
-    sums = sums.transpose(2, 0, 1, 3).reshape(16, wide_count)
-    return (
-        output_field,
-        input_grad,
-        *owner_blocks(block),
-        sums[:9].reshape(3, 3, wide_count),
-        sums[9, :channels],
-        sums[9, channels : 2 * channels],
-    )
+    return (output_field, input_grad, *deliver(block, sums, channels, wide_count))
 
 
 def solution(mesh):

time: 158 us -> 141 us (0.89)
  local copies, waits for them, and re-layouts: 16.2 us -> 3.58 us
  other arithmetic: 2.45 us -> 0 us
    slice x6 -> x0, local copies, waits for them, and re-layouts: 4.78 us -> none  [the longest x3 2.54 us: unfold(): return jnp.concatenate([part[:, :64], part[:, 64:]], axis=0).T]
    unnamed x6 -> x2, local copies, waits for them, and re-layouts: 7.55 us -> 3.58 us
    pallas_call x1, Pallas kernels: 138 us -> 135 us  [whole_step(): pl.pallas_call(functools.partial(step_kernel, names, valid, scale, factor...]
    reshape x3 -> x0, local copies, waits for them, and re-layouts: 2.23 us -> none  [the longest x1 1.48 us: per_device(): depth_weight.astype(jnp.float32).reshape(9, wide_count)]
    transpose x4 -> x0, other arithmetic: 1.83 us -> none  [the longest x3 1.22 us: unfold(): return jnp.concatenate([part[:, :64], part[:, 64:]], axis=0).T]
    pallas_call x0 -> x1, Pallas kernels: none -> 1.7 us  [deliver(): pl.pallas_call(deliver_kernel, out_shape=tuple((jax.ShapeDtypeStruct(shap...]
where the time goes in v5:
time: 141 us
  Pallas kernels  137 us (97%)
  local copies, waits for them, and re-layouts  3.58 us (3%)
    pallas_call x1, Pallas kernels, whole_step(): pl.pallas_call(functools.partial(step_kernel, names, valid, scale, factor...  135 us
    unnamed x2, local copies, waits for them, and re-layouts  3.58 us

profile of v5, /device:TPU:1, one launch (start us, length us, event | category | flops | bytes accessed | tf_op | source)
XLA Modules:
  0.0 140.7 jit_solution(4015355304325238015)
XLA Ops:
  0.6 134.8 %step.1 = (bf16[2,90,512]{2,1,0:T(8,128)(2,1)}, bf16[2,90,512]{2,1,0:T(8,128)(2,1)}, f32[96,128]{1,0:T(8,128)}, f32[32,8,128]{2,1,0:T(8,128)}) custom-call(bf16[90,2,512]{2,1,0:T(2,128)(2,1)} %bitcast.10, bf16[90,2,512]{2,1,0:T(2,128)(2,1)} %bitcast.11, bf16[512,2048]{1,0:T(8,128)(2,1)} %refs_2_.1, bf16[2048,512]{1,0:T(8,128)(2,1)} %refs_3_.1, ...), custom_call_target="tpu_custom_call" | custom-call | tf_op jit(solution)/shard_map/step/pallas_call | solution.py:1075
  135.5 1.8 %copy.19 = bf16[2,90,512]{2,0,1:T(2,128)(2,1)} copy(bf16[2,90,512]{2,1,0:T(8,128)(2,1)} %get-tuple-element.31) | data formatting | bytes 368640
  137.2 1.8 %copy.20 = bf16[2,90,512]{2,0,1:T(2,128)(2,1)} copy(bf16[2,90,512]{2,1,0:T(8,128)(2,1)} %get-tuple-element.32) | data formatting | bytes 368640
  139.0 1.7 %deliver.1 = (f32[64,64]{1,0:T(8,128)}, f32[16,256]{1,0:T(8,128)}, f32[48,64]{1,0:T(8,128)}, f32[16,64]{1,0:T(8,128)}, f32[3,3,2048]{2,1,0:T(4,128)}, /*index=5*/f32[1,512]{1,0:T(1,128)}, f32[1,512]{1,0:T(1,128)}) custom-call(f32[96,128]{1,0:T(8,128)} %get-tuple-element.22.block_ref, f32[32,8,128]{2,1,0:T(8,128)} %get-tuple-element.23.sums_ref), custom_call_target="tpu_custom_call" | custom-call | tf_op jit(solution)/shard_map/deliver/pallas_call | solution.py:1116

commit v6 on v5

--- a/solution.py
+++ b/solution.py
@@ -210,6 +210,22 @@
     for i in range(2):
         r.cot_pad[i * CELLS : i * CELLS + valid, :] = r.cot[:, i, :]
     r.projected[:, 1536:2048] = nt_dot(r.cot_pad[...], r.weight_out[...]).astype(bf16)
+    for i in range(2):
+        value = r.rows[i].astype(f32)
+        value = value * inverse_rms(value) * r.first_gain[...]
+        r.normed[i * CELLS : i * CELLS + CELLS, :] = value.astype(bf16)
+    load["expand"].wait()
+
+    def own_chunk(index, carry):
+        lanes = pl.ds(pl.multiple_of(index * CHUNK, CHUNK), CHUNK)
+        expanded = jnp.dot(r.normed[...], r.expand[:, lanes], preferred_element_type=f32)
+        activated, slope = silu_parts(expanded)
+        r.slope_expanded[:, lanes] = slope.astype(bf16)
+        for i in range(2):
+            r.act[i + 1, :, lanes] = activated[i * CELLS : i * CELLS + CELLS].astype(bf16)
+        return carry
+
+    lax.fori_loop(0, r.expand.shape[1] // CHUNK, own_chunk, 0)
     pl.semaphore_wait(pltpu.get_barrier_semaphore(), greetings)
     copies = halo_copies(r.rows, r.edges, r.row_slots, r.edge_slots, r.state_sends, r.state_recvs)
     halo_start(copies)
@@ -223,30 +239,34 @@
         r.bias_high[i * 16 : i * 16 + 16, :] = jnp.where(bias_lane < 48, pltpu.roll(heads, 80, 1), 0.0)
     for a in range(3):
         r.depth[a * 3 : a * 3 + 3, :] = r.depth_low[a].astype(f32)
-    load["expand"].wait()
     load["shrink"].wait()
     halo_arrive(copies)
-    for row in range(4):
-        base = r.rows[row - 1] if row in (1, 2) else r.row_slots[row // 3]
-        value = halo_row(row, base.astype(f32), r.edge_slots, valid)
-        value = (value * inverse_rms(value) * r.first_gain[...]).astype(bf16)
-        r.wide_normed[row * CELLS : row * CELLS + CELLS, :] = value
-        if row in (1, 2):
-            own = jnp.where(inside(value.shape, valid), value.astype(f32), 0.0).astype(bf16)
-            r.normed[(row - 1) * CELLS : row * CELLS, :] = own
+    far = [halo_row(row, r.row_slots[row // 3].astype(f32), r.edge_slots, valid) for row in (0, 3)]
+    far = jnp.concatenate(far + [r.edge_slots[0, 1], r.edge_slots[1, 1]], axis=0)
+    far = far * inverse_rms(far) * r.first_gain[...]
+    r.wide_normed[...] = far.astype(bf16)
 
     def chunk(index, carry):
         start = pl.multiple_of(index * CHUNK, CHUNK)
         lanes = pl.ds(start, CHUNK)
         expanded = jnp.dot(r.wide_normed[...], r.expand[:, lanes], preferred_element_type=f32)
-        activated, slope = silu_parts(expanded)
-        activated = activated.astype(bf16)
-        r.slope_expanded[:, lanes] = slope[CELLS : 3 * CELLS].astype(bf16)
-        planes = []
-        for row in range(4):
-            plane = activated[row * CELLS : row * CELLS + CELLS]
-            r.act[row, :, lanes] = plane
-            planes.append(plane.astype(f32))
+        activated = silu_parts(expanded)[0].astype(bf16)
+        r.act[0, :, lanes] = activated[0:CELLS]
+        r.act[3, :, lanes] = activated[CELLS : 2 * CELLS]
+        activated = activated.astype(f32)
+        planes = [activated[0:CELLS]]
+        for i in range(2):
+            base = r.act[i + 1, :, lanes].astype(f32)
+            spot = lax.broadcasted_iota(jnp.int32, base.shape, 0)
+            east, west = 2 * CELLS + i, 2 * CELLS + 8 + i
+            plane = jnp.where(
+                spot == valid,
+                activated[east : east + 1],
+                jnp.where(spot == CELLS - 1, activated[west : west + 1], base),
+            )
+            r.act[i + 1, :, lanes] = plane.astype(bf16)
+            planes.append(plane)
+        planes.append(activated[CELLS : 2 * CELLS])
         mixes, slopes = [], []
         for i in range(2):
             sums = []
@@ -1010,7 +1030,7 @@
         "slope_edges": vmem((2, 8, wide), f32),
         "slope_rows": vmem((2, CELLS, wide), bf16),
         "slope_sides": vmem((2, 3, 8, wide), f32),
-        "wide_normed": vmem((4 * CELLS, channels), bf16),
+        "wide_normed": vmem((2 * CELLS + 16, channels), bf16),
         "wide_back": vmem((4 * CELLS, channels), bf16),
         "total": vmem((cells, channels), f32),
         "back_normed": vmem((cells, channels), f32),
@@ -1085,7 +1105,25 @@
     )(*operands, bias, depth, first_gain, second_gain)
 
 
-def deliver_kernel(block_ref, sums_ref, expand_ref, shrink_ref, in_ref, out_ref, depth_ref, one_ref, two_ref):
+def deliver_kernel(
+    block_ref,
+    sums_ref,
+    field_ref,
+    grad_ref,
+    expand_ref,
+    shrink_ref,
+    in_ref,
+    out_ref,
+    depth_ref,
+    one_ref,
+    two_ref,
+    field_out,
+    grad_out,
+):
+    for source, target in ((field_ref, field_out), (grad_ref, grad_out)):
+        for i in range(2):
+            target[:, i, :] = source[i]
+
     def unfold(part):
         return jnp.concatenate([part, pltpu.roll(part, 64, 1)], axis=0)
 
@@ -1110,18 +1148,22 @@
             two_ref[:, tile * 128 - 512 : tile * 128 - 384] = high[1:2]
 
 
-def deliver(block, sums, channels, wide):
+def deliver(block, sums, field, grad, channels, wide):
     vmem = pl.BlockSpec(memory_space=pltpu.VMEM)
     shapes = [(64, 64), (16, 256), (48, 64), (16, 64), (3, 3, wide), (1, channels), (1, channels)]
-    expand, shrink, grad_in, grad_out, depth, one, two = pl.pallas_call(
+    turned = jax.ShapeDtypeStruct((field.shape[1], 2, channels), field.dtype)
+    expand, shrink, grad_in, grad_out, depth, one, two, field, grad = pl.pallas_call(
         deliver_kernel,
-        out_shape=tuple(jax.ShapeDtypeStruct(shape, jnp.float32) for shape in shapes),
-        in_specs=[vmem] * 2,
-        out_specs=(vmem,) * 7,
+        out_shape=tuple(jax.ShapeDtypeStruct(shape, jnp.float32) for shape in shapes)
+        + (turned, turned),
+        in_specs=[vmem] * 4,
+        out_specs=(vmem,) * 9,
+        compiler_params=pltpu.CompilerParams(vmem_limit_bytes=16 * 1024 * 1024),
         name="deliver",
-    )(block, sums)
+    )(block, sums, field, grad)
+    field, grad = field.transpose(1, 0, 2), grad.transpose(1, 0, 2)
     one, two = one.reshape(channels), two.reshape(channels)
-    return expand, shrink.T, grad_in.T, grad_out.T, depth, one, two
+    return field, grad, expand, shrink.T, grad_in.T, grad_out.T, depth, one, two
 
 
 def per_device(
@@ -1152,7 +1194,7 @@
         input_gain.reshape(1, channels),
         attention_gain.reshape(1, channels),
     )
-    return (output_field, input_grad, *deliver(block, sums, channels, wide_count))
+    return deliver(block, sums, output_field, input_grad, channels, wide_count)
 
 
 def solution(mesh):

time: 141 us -> 141 us (level)
    unnamed x2 -> x8, local copies, waits for them, and re-layouts: 3.58 us -> 3.55 us
where the time goes in v6:
time: 141 us
  Pallas kernels  136 us (96%)
  local copies, waits for them, and re-layouts  3.55 us (3%)
    pallas_call x1, Pallas kernels, whole_step(): pl.pallas_call(functools.partial(step_kernel, names, valid, scale, factor...  135 us
    unnamed x8, local copies, waits for them, and re-layouts  3.55 us

profile of v6, /device:TPU:1, one launch (start us, length us, event | category | flops | bytes accessed | tf_op | source)
XLA Modules:
  0.0 140.6 jit_solution(9723344438975222769)
XLA Ops:
  0.6 135.4 %step.1 = (bf16[2,90,512]{2,1,0:T(8,128)(2,1)}, bf16[2,90,512]{2,1,0:T(8,128)(2,1)}, f32[96,128]{1,0:T(8,128)}, f32[32,8,128]{2,1,0:T(8,128)}) custom-call(bf16[90,2,512]{2,1,0:T(2,128)(2,1)} %bitcast.12, bf16[90,2,512]{2,1,0:T(2,128)(2,1)} %bitcast.13, bf16[512,2048]{1,0:T(8,128)(2,1)} %refs_2_.1, bf16[2048,512]{1,0:T(8,128)(2,1)} %refs_3_.1, ...), custom_call_target="tpu_custom_call" | custom-call | tf_op jit(solution)/shard_map/step/pallas_call | solution.py:1095
  136.1 0.0 copy-start
  136.1 0.9 copy-done
  137.0 0.0 copy-start.1
  137.0 0.9 copy-done.1
  137.9 0.0 copy-start.2
  137.9 0.9 copy-done.2
  138.8 0.0 copy-start.3
  138.8 0.8 copy-done.3
  139.6 1.0 deliver.1
Async XLA Ops:
  136.1 0.9 copy-start
  137.0 0.9 copy-start.1
  137.9 0.9 copy-start.2
  138.8 0.8 copy-start.3

commit v7 on v6

--- a/solution.py
+++ b/solution.py
@@ -371,7 +371,7 @@
     ).astype(bf16)
     project_and_pack(r, valid, 0, 1536, r.qd_out, False)
 
-    for step in range(groups):
+    def push_queries(step):
         target = lax.rem(own_group + groups - step, groups) * group
         for part in range(group):
             to = target + part
@@ -383,6 +383,7 @@
                 def _():
                     query_copy(to, lon).start()
 
+    push_queries(0)
     halo = halo_copies(
         r.slope, r.slope_edges, r.slope_rows, r.slope_sides, r.slope_sends, r.slope_recvs
     )
@@ -432,6 +433,9 @@
             return carry
 
         lax.fori_loop(0, 4 if part < 7 else 3, arrive, 0)
+
+    for step in range(1, groups):
+        push_queries(step)
 
     def turn(index, carry):
         start = pl.multiple_of(index * block, block)
@@ -1106,10 +1110,10 @@
 
 
 def deliver_kernel(
-    block_ref,
-    sums_ref,
-    field_ref,
-    grad_ref,
+    block_hbm,
+    sums_hbm,
+    field_hbm,
+    grad_hbm,
     expand_ref,
     shrink_ref,
     in_ref,
@@ -1119,7 +1123,26 @@
     two_ref,
     field_out,
     grad_out,
+    block_ref,
+    sums_ref,
+    field_ref,
+    grad_ref,
+    loads,
 ):
+    pairs = (
+        (block_hbm, block_ref),
+        (sums_hbm, sums_ref),
+        (field_hbm, field_ref),
+        (grad_hbm, grad_ref),
+    )
+    copies = [
+        pltpu.make_async_copy(source, target, loads.at[index])
+        for index, (source, target) in enumerate(pairs)
+    ]
+    for made in copies:
+        made.start()
+    for made in copies:
+        made.wait()
     for source, target in ((field_ref, field_out), (grad_ref, grad_out)):
         for i in range(2):
             target[:, i, :] = source[i]
@@ -1156,9 +1179,13 @@
         deliver_kernel,
         out_shape=tuple(jax.ShapeDtypeStruct(shape, jnp.float32) for shape in shapes)
         + (turned, turned),
-        in_specs=[vmem] * 4,
+        in_specs=[pl.BlockSpec(memory_space=pl.ANY)] * 4,
         out_specs=(vmem,) * 9,
-        compiler_params=pltpu.CompilerParams(vmem_limit_bytes=16 * 1024 * 1024),
+        scratch_shapes=[
+            pltpu.VMEM(value.shape, value.dtype) for value in (block, sums, field, grad)
+        ]
+        + [pltpu.SemaphoreType.DMA((4,))],
+        compiler_params=pltpu.CompilerParams(vmem_limit_bytes=54 * 1024 * 1024),
         name="deliver",
     )(block, sums, field, grad)
     field, grad = field.transpose(1, 0, 2), grad.transpose(1, 0, 2)

time: 141 us -> 139 us (0.986)
  local copies, waits for them, and re-layouts: 3.55 us -> 0 us
  Pallas kernels: 136 us -> 138 us
    unnamed x8 -> x0, local copies, waits for them, and re-layouts: 3.55 us -> none
where the time goes in v7:
time: 139 us
  Pallas kernels  138 us (99%)
    pallas_call x1, Pallas kernels, whole_step(): pl.pallas_call(functools.partial(step_kernel, names, valid, scale, factor...  136 us

profile of v7, /device:TPU:1, one launch (start us, length us, event | category | flops | bytes accessed | tf_op | source)
XLA Modules:
  0.0 138.6 jit_solution(3958665967088610399)
XLA Ops:
  0.6 135.6 %step.1 = (bf16[2,90,512]{2,1,0:T(8,128)(2,1)}, bf16[2,90,512]{2,1,0:T(8,128)(2,1)}, f32[96,128]{1,0:T(8,128)}, f32[32,8,128]{2,1,0:T(8,128)}) custom-call(bf16[90,2,512]{2,1,0:T(2,128)(2,1)} %bitcast.12, bf16[90,2,512]{2,1,0:T(2,128)(2,1)} %bitcast.13, bf16[512,2048]{1,0:T(8,128)(2,1)} %refs_2_.1, bf16[2048,512]{1,0:T(8,128)(2,1)} %refs_3_.1, ...), custom_call_target="tpu_custom_call" | custom-call | tf_op jit(solution)/shard_map/step/pallas_call | solution.py:1099
  136.2 2.2 %deliver.1 = (f32[64,64]{1,0:T(8,128)}, f32[16,256]{1,0:T(8,128)}, f32[48,64]{1,0:T(8,128)}, f32[16,64]{1,0:T(8,128)}, f32[3,3,2048]{2,1,0:T(4,128)}, /*index=5*...) custom-call(f32[96,128]{1,0:T(8,128)} %get-tuple-element.22.block_hbm, ...), custom_call_target="tpu_custom_call" | custom-call | tf_op jit(solution)/shard_map/deliver/pallas_call | solution.py:1178
